TPU v7x, 32 devices: a whole 2x2x4 slice. The times are simulated.
32 devices in a mesh: src: 8 (over z, core), tgt: 4 (over y, x).
Axes of the slice: x: 2, y: 2, z: 4, core: 2. Of those that a mesh axis runs over, the one named last changes fastest.
Arguments:
- charges: bfloat16 [65536, 64], P(('src', 'tgt')), may hold values from -6 to 6
- near_tiles: bfloat16 [4096, 128, 128], P(('src', 'tgt')), may hold values from -0.0625 to 0.0625
- near_tgt: int32 [4096], P(('src', 'tgt')), may hold values from 0 to 127
- near_src: int32 [4096], P(('src', 'tgt')), may hold values from 0 to 15
- leaf_basis: bfloat16 [512, 64, 128], P(('src', 'tgt')), may hold values from -0.125 to 0.125
- transfer: float32 [8, 3, 64, 128], P('src'), may hold values from -0.5 to 0.5
- coupling: bfloat16 [8, 512, 64, 256], P('src', 'tgt'), may hold values from -0.375 to 0.375
- far_node: int32 [8, 512, 4], P('src', 'tgt'), may hold values from 0 to 6
- target_basis: bfloat16 [512, 64, 128], P('tgt'), may hold values from -0.25 to 0.25
Outputs:
- potential: bfloat16 [65536, 64], P('tgt')
All inputs are finite; a program needn't handle non-finite values.
Results may differ from a plain program's by a relative error of at most 0.0057.
Values may be sent and summed in bfloat16 or wider, within the bound.
No kernel may reach another device: no remote copies, remote signals or barrier semaphores. Data moves between devices by JAX's collectives and lax.ppermute only.
A program may use at most 128 MiB of HBM per device.

v0:
```python
import jax
import jax.numpy as jnp
from jax import lax
from jax.sharding import PartitionSpec as P


def climb(edges, leaves):
    levels = [leaves]
    level = leaves
    width = leaves.shape[0]
    while width > 1:
        width = width // 2
        edge_slab = edges[width - 1 : 2 * width - 1]
        pairs = level.reshape(width, 2 * level.shape[1], level.shape[2])
        level = jnp.einsum("prc,pcn->prn", edge_slab, pairs, precision=lax.Precision.HIGHEST)
        levels.insert(0, level)
    return jnp.concatenate(levels, axis=0)


def shards(
    charges, near_tiles, near_tgt, near_src, leaf_basis, transfer, coupling, far_node, target_basis
):
    groups = lax.axis_size("tgt")
    tile = near_tiles.shape[1]
    slots = near_tiles.shape[0] // groups
    nrhs = charges.shape[1]
    tdev = leaf_basis.shape[0]
    tgt_tiles = target_basis.shape[0]
    local_leaves = charges.reshape(tdev, tile, nrhs)
    block_x = lax.all_gather(charges, "tgt", axis=0, tiled=True)
    block_leaves = block_x.reshape(groups * tdev, tile, nrhs)
    got_tiles, got_tgt, got_src = (
        lax.all_to_all(
            near_tiles.reshape(groups, slots, tile, tile),
            "tgt",
            split_axis=0,
            concat_axis=0,
            tiled=True,
        ),
        lax.all_to_all(
            near_tgt.reshape(groups, slots), "tgt", split_axis=0, concat_axis=0, tiled=True
        ),
        lax.all_to_all(
            near_src.reshape(groups, slots), "tgt", split_axis=0, concat_axis=0, tiled=True
        ),
    )
    sender = jnp.arange(groups, dtype=jnp.int32)[:, None] * tdev
    picked = block_leaves[(got_src + sender).reshape(-1)]
    products = jnp.einsum(
        "kab,kbn->kan",
        got_tiles.reshape(groups * slots, tile, tile),
        picked,
        preferred_element_type=jnp.float32,
    ).astype(jnp.bfloat16)
    results = products.reshape(groups * slots, tile * nrhs)
    onehot = (
        got_tgt.reshape(-1)[None, :] == jnp.arange(tgt_tiles, dtype=jnp.int32)[:, None]
    ).astype(jnp.bfloat16)
    near_part = jnp.dot(onehot, results, preferred_element_type=jnp.float32).reshape(
        tgt_tiles, tile, nrhs
    )
    own_root = jnp.einsum(
        "irp,ipn->rn", leaf_basis, local_leaves, preferred_element_type=jnp.float32
    )
    roots = lax.all_gather(own_root[None], "tgt", axis=0, tiled=True)
    table_b = climb(transfer[0], roots).astype(jnp.bfloat16)
    chosen = table_b[far_node[0]]
    stacked = chosen.reshape(chosen.shape[0], chosen.shape[1] * chosen.shape[2], chosen.shape[3])
    zed = jnp.einsum(
        "trc,tcn->trn", coupling[0], stacked, preferred_element_type=jnp.float32
    ).astype(jnp.bfloat16)
    far_part = jnp.einsum("trp,trn->tpn", target_basis, zed, preferred_element_type=jnp.float32)
    total = lax.psum(near_part + far_part, "src")
    return total.reshape(tgt_tiles * tile, nrhs).astype(jnp.bfloat16)


def solution(mesh):
    in_specs = (
        P(("src", "tgt"), None),
        P(("src", "tgt"), None, None),
        P(("src", "tgt")),
        P(("src", "tgt")),
        P(("src", "tgt"), None, None),
        P("src", None, None, None),
        P("src", "tgt", None, None),
        P("src", "tgt", None),
        P("tgt", None, None),
    )
    out_specs = P("tgt", None)
    return jax.shard_map(shards, mesh=mesh, in_specs=in_specs, out_specs=out_specs, check_vma=False)
```

profile of v0, /device:TPU:1, one launch (start us, length us, event | category | flops | bytes accessed | tf_op | source)
XLA Modules:
  0.0 226.5 jit_solution(22342178664808645)
XLA Ops:
  6.5 1.5 all_to_all.19
  8.0 4.3 %all-to-all-start.1 = ((s32[4,1,32]{2,1,0:T(1,128)}), s32[4,1,32]{2,1,0:T(1,128)S(1)}, u32[]{:S(2)}, u32[]{:S(2)}) async-start(s32[4,1,32]{2,1,0:T(1,128)} %bitcast.2), calls=%async_computation.1 | async-start | bytes 4096 | tf_op jit(solution)/shard_map/all_to_all | solution.py:43
  12.3 0.7 all_to_all.17
  13.0 2.7 %all-to-all-done.1 = s32[4,1,32]{2,1,0:T(1,128)S(1)} async-done(((s32[4,1,32]{2,1,0:T(1,128)}), s32[4,1,32]{2,1,0:T(1,128)S(1)}, u32[]{:S(2)}, u32[]{:S(2)}) %all-to-all-start.1) | async-done | bytes 544 | tf_op jit(solution)/shard_map/all_to_all | solution.py:43
  15.7 5.8 %all_to_all.26 = s32[4,1,32]{2,1,0:T(1,128)S(1)} all-to-all(s32[4,1,32]{2,1,0:T(1,128)S(1)} %bitcast.80), channel_id=1, replica_groups=mesh['src'=8,'tgt'=4] {'tgt'}, dimensions={0} | all-to-all | bytes 1024 | tf_op jit(solution)/shard_map/all_to_all | solution.py:40
  21.5 5.1 %all-to-all-start.2 = ((bf16[4,32,128,128]{3,2,1,0:T(8,128)(2,1)}), bf16[4,32,128,128]{3,2,1,0:T(8,128)(2,1)}, u32[]{:S(2)}, u32[]{:S(2)}) async-start(bf16[4,32,128,128]{3,2,1,0:T(8,128)(2,1)} %bitcast.77), calls=%async_computation.2 | async-start | bytes 8388608 | tf_op jit(solution)/shard_map/all_to_all | solution.py:33
  26.6 0.7 all-gather.3.cloned.1.call-update
  27.3 0.2 convolution_bitcast_fusion.1
  27.6 56.0 %all-gather = f32[256,64]{1,0:T(8,128)S(1)} all-gather(f32[64,64]{1,0:T(8,128)S(1)} %convolution_bitcast_fusion.1), channel_id=2, replica_groups=mesh['src'=8,'tgt'=4] {'tgt'}, dimensions={0}, use_global_device_ids=true | all-gather | bytes 81920 | tf_op jit(solution)/shard_map/all_gather | solution.py:65
  83.6 0.4 fusion.20
  84.0 0.1 copy.64
  84.0 0.1 reshape.116
  84.2 0.2 fusion.9
  84.3 0.1 copy.65
  84.4 0.1 copy.66
  84.5 0.1 copy.67
  84.7 0.1 reshape.129
  84.8 0.1 add.49
  84.9 0.1 add.50
  85.0 13.4 %gather_fusion.1 = bf16[512,64,64]{2,1,0:T(8,128)(2,1)} fusion(bf16[7,64,64]{2,1,0:T(8,128)(2,1)S(1)} %pad_maximum_fusion, s32[1024]{0:T(1024)S(1)} %pad_clamp_fusion), kind=kCustom, calls=%fused_computation.1 | custom fusion | bytes 8390656 | tf_op jit(solution)/shard_map/gather | solution.py:67
  98.4 10.1 %fusion.3 = f32[128,64,128]{2,1,0:T(8,128)} fusion(bf16[128,64,128]{2,1,0:T(8,128)(2,1)S(1)} %copy-done, bf16[128,256,64]{2,1,0:T(8,128)(2,1)} %bitcast.75, bf16[1,128,64,256]{3,2,1,0:T(8,128)(2,1)} %param.15), kind=kOutput, calls=%fused_computation.7 | convolution fusion | flops 403177472 | bytes 14680064 | tf_op jit(solution)/shard_map/trp,trn->tpn/dot_general | solution.py:72
  108.5 0.5 broadcast.53
  109.0 0.7 reduce.6
  109.7 0.1 all_to_all.21
  109.8 0.7 reduce.7
  110.4 0.1 eq.15
  110.6 1.5 copy_bitcast_fusion.1
  112.1 2.1 gather_fusion
  114.2 5.9 %convert_bitcast_fusion = bf16[128,64,128]{0,1,2:T(8,128)(2,1)S(1)} fusion(bf16[128,128,64]{1,2,0:T(8,128)(2,1)} %gather_fusion, bf16[128,128,128]{2,1,0:T(8,128)(2,1)} %bitcast.5), kind=kOutput, calls=%fused_computation.9 | convolution fusion | flops 269484032 | bytes 8388608 | tf_op jit(solution)/shard_map/kab,kbn->kan/dot_general | solution.py:49
  120.2 5.8 %bitcast_add_fusion = f32[128,128,64]{1,0,2:T(8,128)} fusion(f32[128,64,128]{2,1,0:T(8,128)S(1)} %copy-done.1, bf16[128,64,128]{0,1,2:T(8,128)(2,1)S(1)} %convert_bitcast_fusion, s32[128]{0:T(128)S(1)} %eq.15), kind=kOutput, calls=%fused_computation.2 | convolution fusion | flops 269500416 | bytes 10486272 | tf_op jit(solution)/shard_map/dot_general | solution.py:59
  125.9 89.5 %all-reduce.1 = bf16[128,128,64]{1,0,2:T(8,128)(2,1)} all-reduce(f32[128,128,64]{1,0,2:T(8,128)} %bitcast_add_fusion), channel_id=1, replica_groups=mesh['src'=8,'tgt'=4] {'src'}, use_global_device_ids=true, to_apply=%region_0.0 | all-reduce | flops 1048576 | bytes 6291456 | tf_op jit(solution)/shard_map/psum | solution.py:73
  215.4 4.3 %copy.87 = bf16[8,8,128,128]{3,1,2,0:T(8,128)(2,1)} copy(bf16[8,8,128,128]{3,2,1,0:T(8,128)(2,1)} %bitcast.76) | data formatting | bytes 4194304
  (22 shorter events, 0.2 us)
Async XLA Ops:
  6.5 91.9 %copy-start = (bf16[128,64,128]{2,1,0:T(8,128)(2,1)S(1)}, bf16[128,64,128]{2,1,0:T(8,128)(2,1)}, u32[]{:S(2)}) copy-start(bf16[128,64,128]{2,1,0:T(8,128)(2,1)} %param.17) | copy-start | bytes 6291460
  8.0 7.7 %all-to-all-start.1 = ((s32[4,1,32]{2,1,0:T(1,128)}), s32[4,1,32]{2,1,0:T(1,128)S(1)}, u32[]{:S(2)}, u32[]{:S(2)}) async-start(s32[4,1,32]{2,1,0:T(1,128)} %bitcast.2), calls=%async_computation.1 | async-start | bytes 4096 | tf_op jit(solution)/shard_map/all_to_all | solution.py:43
  21.5 5.8 %copy-start.2 = (bf16[2048,64]{0,1:T(8,128)(2,1)S(1)}, bf16[2048,64]{0,1:T(8,128)(2,1)}, u32[]{:S(2)}) copy-start(bf16[2048,64]{0,1:T(8,128)(2,1)} %param.9) | copy-start | bytes 786436
  21.5 5.8 %copy-start.3 = (bf16[16,64,128]{2,1,0:T(8,128)(2,1)S(1)}, bf16[16,64,128]{2,1,0:T(8,128)(2,1)}, u32[]{:S(2)}) copy-start(bf16[16,64,128]{2,1,0:T(8,128)(2,1)} %param.13) | copy-start | bytes 786436
  21.5 62.1 %copy-start.4 = (f32[1,3,64,128]{3,2,1,0:T(8,128)S(1)}, f32[1,3,64,128]{3,2,1,0:T(8,128)}, u32[]{:S(2)}) copy-start(f32[1,3,64,128]{3,2,1,0:T(8,128)} %param.14) | copy-start | bytes 294916
  21.5 62.6 %copy-start.5 = (s32[1,128,4]{1,2,0:T(4,128)S(1)}, s32[1,128,4]{1,2,0:T(4,128)}, u32[]{:S(2)}) copy-start(s32[1,128,4]{1,2,0:T(4,128)} %param.16) | copy-start | bytes 6148
  21.5 92.7 %all-to-all-start.2 = ((bf16[4,32,128,128]{3,2,1,0:T(8,128)(2,1)}), bf16[4,32,128,128]{3,2,1,0:T(8,128)(2,1)}, u32[]{:S(2)}, u32[]{:S(2)}) async-start(bf16[4,32,128,128]{3,2,1,0:T(8,128)(2,1)} %bitcast.77), calls=%async_computation.2 | async-start | bytes 8388608 | tf_op jit(solution)/shard_map/all_to_all | solution.py:33
  26.6 84.0 %all-gather.3.cloned.1.call-start = ((), (), s32[]{:S(2)}) async-start(), calls=%async_computation.3 | async-start | bytes 1310720 | tf_op jit(solution)/shard_map/all_gather | solution.py:30
  114.2 5.9 %copy-start.1 = (f32[128,64,128]{2,1,0:T(8,128)S(1)}, f32[128,64,128]{2,1,0:T(8,128)}, u32[]{:S(2)}) copy-start(f32[128,64,128]{2,1,0:T(8,128)} %fusion.3) | copy-start | bytes 12582916
Sparse Core Ops, SparseCore 0:
  29.3 47.1 all-gather.2
where the time goes:
time: 230 us; the launch traced here: 227 us
  blocking collectives  151 us (66%)
  local copies, waits for them, and re-layouts  25 us (11%)
  matrix products  22.5 us (10%)
  between operations  13.6 us (6%)
  starting transfers between devices  9.36 us (4%)
  waiting for transfers between devices  3.39 us (1%)
    psum x1, blocking collectives, shards(): total = lax.psum(near_part + far_part, 'src')  89.5 us
    all_gather x1, blocking collectives, shards(): roots = lax.all_gather(own_root[None], 'tgt', axis=0, tiled=True)  56 us
    gather x1, local copies, waits for them, and re-layouts, shards(): chosen = table_b[far_node[0]]  13.4 us
    dot_general x1, matrix products, shards(): jnp.einsum('trp,trn->tpn', target_basis, zed, preferred_element_type=jnp....  10.1 us
    dot_general x1, matrix products, shards(): jnp.einsum('kab,kbn->kan', got_tiles.reshape(groups * slots, tile, tile),...  5.94 us
    all_to_all x1, blocking collectives, shards(): lax.all_to_all(near_tgt.reshape(groups, slots), 'tgt', split_axis=0, conc...  5.82 us
    dot_general x1, matrix products, shards(): jnp.dot(onehot, results, preferred_element_type=jnp.float32)  5.76 us
    all_to_all x1, starting transfers between devices, shards(): lax.all_to_all(near_tiles.reshape(groups, slots, tile, tile), 'tgt', spli...  5.05 us
  transfers between devices with their start and end apart: 3, of which 1 were waited for; matrix products, arithmetic and copies ran while one was open for 14% of the time, Pallas kernels for 0%

commit v1 on v0

v1 whole, which is shorter than its diff:
```python
import functools

import jax
import jax.numpy as jnp
from jax import lax
from jax.experimental import pallas as pl
from jax.experimental.pallas import tpu as pltpu
from jax.sharding import PartitionSpec as P

CHUNKS = 1
F32, BF16 = jnp.float32, jnp.bfloat16
NT = (((1,), (1,)), ((), ()))
SMEM = pl.BlockSpec(memory_space=pltpu.SMEM)
VMEM = pl.BlockSpec(memory_space=pltpu.VMEM)
PARAMS = pltpu.CompilerParams(vmem_limit_bytes=48 * 2**20)


def tree_width(rank):
    return 2 * rank


def root_kernel(x_ref, basis_ref, tgt_ref, out_ref):
    leaves, rank, tile = basis_ref.shape
    nrhs = x_ref.shape[0]
    acc = jnp.zeros((nrhs, rank), F32)
    for i in range(leaves):
        acc += lax.dot_general(
            x_ref[:, i * tile : (i + 1) * tile], basis_ref[i], NT, preferred_element_type=F32
        )
    out_ref[:nrhs, :rank] = acc
    out_ref[nrhs:, :] = jnp.broadcast_to(tgt_ref[...].astype(F32), (8, out_ref.shape[1]))


def near_kernel(block_ref, src_ref, x_ref, tiles_ref, *out_refs):
    slots, tile, _ = tiles_ref.shape
    rows = out_refs[0].shape[0]
    first = block_ref[0] * slots
    for k in range(slots):
        leaf = src_ref[first + k]
        x = x_ref[:, pl.ds(pl.multiple_of(leaf * tile, tile), tile)]
        y = lax.dot_general(x, tiles_ref[k], NT, preferred_element_type=F32).astype(BF16)
        for c, out_ref in enumerate(out_refs):
            out_ref[:, k * tile : (k + 1) * tile] = y[c * rows : (c + 1) * rows]


def near_products(block, near_src, x, tiles, groups):
    slots = tiles.shape[0] // groups
    tile = tiles.shape[1]
    nrhs, width = x.shape
    rows = nrhs // CHUNKS
    return pl.pallas_call(
        near_kernel,
        out_shape=[jax.ShapeDtypeStruct((rows, slots * tile), BF16)] * CHUNKS,
        grid_spec=pltpu.PrefetchScalarGridSpec(
            num_scalar_prefetch=2,
            grid=(1,),
            in_specs=[
                pl.BlockSpec((nrhs, width), lambda i, b, s: (0, 0)),
                pl.BlockSpec((slots, tile, tile), lambda i, b, s: (b[0], 0, 0)),
            ],
            out_specs=[pl.BlockSpec((rows, slots * tile), lambda i, b, s: (0, 0))] * CHUNKS,
        ),
        compiler_params=PARAMS,
    )(block, near_src, x, tiles)


def far_kernel(groups, me_ref, node_ref, *refs):
    root_refs = refs[:groups]
    edge_ref, coupling_ref, basis_ref, out_ref, exact, low, high = refs[groups:]
    step = pl.program_id(0)
    leaves, rank, tile = basis_ref.shape
    per = coupling_ref.shape[2] // rank
    chunks, rows = out_ref.shape[0], out_ref.shape[2]
    nrhs = chunks * rows

    @pl.when(step == 0)
    def _():
        for m in range(groups):
            exact[groups - 1 + (me_ref[0] ^ m)] = root_refs[m][:nrhs, :rank]
        for n in range(groups - 2, -1, -1):
            pair = jnp.concatenate([exact[2 * n + 1], exact[2 * n + 2]], axis=1)
            exact[n] = lax.dot_general(
                pair, edge_ref[n], NT, precision=lax.Precision.HIGHEST, preferred_element_type=F32
            )
        zero = jnp.zeros((nrhs, rank), BF16)
        for n in range(2 * groups - 1):
            node = exact[n].astype(BF16)
            low[n] = jnp.concatenate([node, zero], axis=1)
            high[n] = jnp.concatenate([zero, node], axis=1)

    for i in range(leaves):
        tau = step * leaves + i
        nodes = [node_ref[tau * per + k] for k in range(per)]
        stacked = jnp.concatenate(
            [low[nodes[k]] + high[nodes[k + 1]] for k in range(0, per, 2)], axis=1
        )
        z = lax.dot_general(stacked, coupling_ref[i], NT, preferred_element_type=F32).astype(BF16)
        far = jnp.dot(z, basis_ref[i], preferred_element_type=F32)
        for c in range(chunks):
            out_ref[c, 0, :, i * tile : (i + 1) * tile] = far[c * rows : (c + 1) * rows]


def far_field(me, far_node, roots, transfer, coupling, target_basis, pieces):
    groups = len(roots)
    tgt_tiles, rank, tile = target_basis.shape
    leaves = tgt_tiles // pieces
    nrhs = roots[0].shape[0] - 8
    rows = nrhs // CHUNKS
    nodes = 2 * groups - 1
    return pl.pallas_call(
        functools.partial(far_kernel, groups),
        out_shape=jax.ShapeDtypeStruct((CHUNKS, pieces, rows, leaves * tile), F32),
        grid_spec=pltpu.PrefetchScalarGridSpec(
            num_scalar_prefetch=2,
            grid=(pieces,),
            in_specs=[pl.BlockSpec(r.shape, lambda i, a, b: (0, 0)) for r in roots]
            + [
                pl.BlockSpec(transfer.shape, lambda i, a, b: (0, 0, 0)),
                pl.BlockSpec((leaves,) + coupling.shape[1:], lambda i, a, b: (i, 0, 0)),
                pl.BlockSpec((leaves, rank, tile), lambda i, a, b: (i, 0, 0)),
            ],
            out_specs=pl.BlockSpec((CHUNKS, 1, rows, leaves * tile), lambda i, a, b: (0, i, 0, 0)),
            scratch_shapes=[
                pltpu.VMEM((nodes, nrhs, rank), F32),
                pltpu.VMEM((nodes, nrhs, 2 * rank), BF16),
                pltpu.VMEM((nodes, nrhs, 2 * rank), BF16),
            ],
        ),
        compiler_params=PARAMS,
    )(me, far_node, *roots, transfer, coupling, target_basis)


def gather_kernel(chunk, groups, core_ref, tgt_ref, far_ref, *refs):
    got_refs = refs[:groups]
    keep_ref, send_ref, acc = refs[groups:]
    pieces, rows, width = acc.shape
    slots = tgt_ref.shape[0] // groups
    tile = got_refs[0].shape[1] // slots
    leaves = width // tile
    acc[...] = far_ref[0]
    for m in range(groups):
        for k in range(slots):
            leaf = tgt_ref[m * slots + k]
            piece = leaf // leaves
            spot = pl.ds(pl.multiple_of((leaf - piece * leaves) * tile, tile), tile)
            acc[piece, :, spot] = acc[piece, :, spot] + got_refs[m][
                :, k * tile : (k + 1) * tile
            ].astype(F32)
    core = core_ref[0]
    for z in range(pieces // 2):
        keep_ref[z] = acc[2 * z + core]
        send_ref[z] = acc[2 * z + 1 - core].astype(BF16)


def gather_near(chunk, core, tgt, far, got):
    _, pieces, rows, width = far.shape
    groups = len(got)
    half = (pieces // 2, rows, width)
    return pl.pallas_call(
        functools.partial(gather_kernel, chunk, groups),
        out_shape=[jax.ShapeDtypeStruct(half, F32), jax.ShapeDtypeStruct(half, BF16)],
        grid_spec=pltpu.PrefetchScalarGridSpec(
            num_scalar_prefetch=2,
            grid=(1,),
            in_specs=[pl.BlockSpec((1, pieces, rows, width), lambda i, a, b: (chunk, 0, 0, 0))]
            + [pl.BlockSpec(g.shape, lambda i, a, b: (0, 0)) for g in got],
            out_specs=[pl.BlockSpec(half, lambda i, a, b: (0, 0, 0))] * 2,
            scratch_shapes=[pltpu.VMEM((pieces, rows, width), F32)],
        ),
        compiler_params=PARAMS,
    )(core, tgt, far, *got)


def place_kernel(count, me_ref, *refs):
    piece_refs, out_ref, sems = refs[:count], refs[count], refs[count + 1]
    pieces = count // CHUNKS
    rows, width = piece_refs[0].shape
    copies = []
    for c in range(CHUNKS):
        for m in range(pieces):
            owner = me_ref[0] ^ m
            spot = pl.ds(pl.multiple_of(owner * width, width), width)
            n = c * pieces + m
            copies.append(
                pltpu.make_async_copy(
                    piece_refs[n], out_ref.at[pl.ds(c * rows, rows), spot], sems.at[n]
                )
            )
    for copy in copies:
        copy.start()
    for copy in copies:
        copy.wait()


def place(me, parts):
    rows, width = parts[0].shape
    pieces = len(parts) // CHUNKS
    return pl.pallas_call(
        functools.partial(place_kernel, len(parts)),
        out_shape=jax.ShapeDtypeStruct((rows * CHUNKS, width * pieces), BF16),
        in_specs=[SMEM] + [pl.BlockSpec(memory_space=pl.ANY)] * len(parts),
        out_specs=pl.BlockSpec(memory_space=pl.ANY),
        scratch_shapes=[pltpu.SemaphoreType.DMA((len(parts),))],
    )(me, *parts)


def swap(value, axis, mask):
    size = lax.axis_size(axis)
    return lax.ppermute(value, axis, [(i, i ^ mask) for i in range(size)])


def shards(
    charges, near_tiles, near_tgt, near_src, leaf_basis, transfer, coupling, far_node, target_basis
):
    groups = lax.axis_size("tgt")
    sources = lax.axis_size("src")
    me_t = lax.axis_index("tgt").astype(jnp.int32)
    me_s = lax.axis_index("src").astype(jnp.int32)
    core, me_z = me_s % 2, me_s // 2
    tiles, tile, _ = near_tiles.shape
    slots = tiles // groups
    nrhs = charges.shape[1]
    x = charges.T

    message = pl.pallas_call(
        root_kernel,
        out_shape=jax.ShapeDtypeStruct((nrhs + 8, tiles), F32),
        in_specs=[VMEM] * 3,
        out_specs=VMEM,
        compiler_params=PARAMS,
    )(x, leaf_basis, near_tgt.reshape(1, tiles))
    messages = [message] + [swap(message, "tgt", m) for m in range(1, groups)]

    products = [
        near_products((me_t ^ m).reshape(1), near_src, x, near_tiles, groups)
        for m in range(groups)
    ]
    targets = jnp.concatenate(
        [
            lax.dynamic_slice(msg, (nrhs, me_t * slots), (1, slots))[0].astype(jnp.int32)
            for msg in messages
        ]
    )
    far = far_field(
        me_t.reshape(1),
        far_node[0].reshape(-1),
        messages,
        transfer[0],
        coupling[0],
        target_basis,
        sources,
    )
    parts = []
    for c in range(CHUNKS):
        got = [products[0][c]] + [swap(products[m][c], "tgt", m) for m in range(1, groups)]
        keep, send = gather_near(c, core.reshape(1), targets, far, got)
        total = keep + swap(send, "src", 1).astype(F32)
        final = total[me_z]
        for m in range(1, sources // 2):
            final = final + swap(total[me_z ^ m].astype(BF16), "src", 2 * m).astype(F32)
        final = final.astype(BF16)
        mine = [final] + [swap(final, "src", 2 * m) for m in range(1, sources // 2)]
        other = [swap(p, "src", 1) for p in mine]
        for a, b in zip(mine, other):
            parts += [a, b]
    return place(me_s.reshape(1), parts).T


def solution(mesh):
    in_specs = (
        P(("src", "tgt"), None),
        P(("src", "tgt"), None, None),
        P(("src", "tgt")),
        P(("src", "tgt")),
        P(("src", "tgt"), None, None),
        P("src", None, None, None),
        P("src", "tgt", None, None),
        P("src", "tgt", None),
        P("tgt", None, None),
    )
    out_specs = P("tgt", None)
    return jax.shard_map(shards, mesh=mesh, in_specs=in_specs, out_specs=out_specs, check_vma=False)
```

time: 230 us -> 178 us (0.77)
  blocking collectives: 151 us -> 0 us
  Pallas kernels: 0 us -> 93.2 us
  starting transfers between devices: 9.36 us -> 36.2 us
  waiting for transfers between devices: 3.39 us -> 26 us
  matrix products: 22.5 us -> 0 us
  between operations: 13.6 us -> 0.13 us
  local copies, waits for them, and re-layouts: 25 us -> 16.5 us
  other arithmetic: 1.39 us -> 4.46 us
    pallas_call x0 -> x8, Pallas kernels: none -> 93.2 us  [the longest x1 64.7 us: place(): pl.pallas_call(functools.partial(place_kernel, len(parts)), out_shape=jax...]
    psum x1 -> x0, blocking collectives: 89.5 us -> none  [shards(): total = lax.psum(near_part + far_part, 'src')]
    all_gather x1 -> x0, blocking collectives: 56 us -> none  [shards(): roots = lax.all_gather(own_root[None], 'tgt', axis=0, tiled=True)]
    ppermute x0 -> x17, starting transfers between devices: none -> 36.2 us  [swap(): return lax.ppermute(value, axis, [(i, i ^ mask) for i in range(size)])]
    ppermute x0 -> x17, waiting for transfers between devices: none -> 26 us  [swap(): return lax.ppermute(value, axis, [(i, i ^ mask) for i in range(size)])]
    dot_general x6 -> x0, matrix products: 22.5 us -> none  [the longest x1 10.1 us: shards(): jnp.einsum('trp,trn->tpn', target_basis, zed, preferred_element_type=jnp....]
    gather x2 -> x0, local copies, waits for them, and re-layouts: 15.6 us -> none  [the longest x1 13.4 us: shards(): chosen = table_b[far_node[0]]]
    unnamed x13 -> x49, local copies, waits for them, and re-layouts: 4.3 us -> 15 us
  transfers between devices with their start and end apart: 3 -> 17, of which waited for: 1 -> 6; matrix products, arithmetic and copies ran while one was open for 14% -> 1% of each run, Pallas kernels for 0% -> 13%
where the time goes in v1:
time: 178 us; the launch traced here: 177 us
  Pallas kernels  93.2 us (52%)
  starting transfers between devices  36.2 us (20%)
  waiting for transfers between devices  26 us (15%)
  local copies, waits for them, and re-layouts  16.5 us (9%)
  other arithmetic  4.46 us (3%)
    pallas_call x1, Pallas kernels, place(): pl.pallas_call(functools.partial(place_kernel, len(parts)), out_shape=jax...  64.7 us
    ppermute x17, starting transfers between devices, swap(): return lax.ppermute(value, axis, [(i, i ^ mask) for i in range(size)])  36.2 us
    ppermute x17, waiting for transfers between devices, swap(): return lax.ppermute(value, axis, [(i, i ^ mask) for i in range(size)])  26 us
    unnamed x49, local copies, waits for them, and re-layouts  15 us
    pallas_call x1, Pallas kernels, far_field(): pl.pallas_call(functools.partial(far_kernel, groups), out_shape=jax.Shape...  14.9 us
    pallas_call x4, Pallas kernels, near_products(): pl.pallas_call(near_kernel, out_shape=[jax.ShapeDtypeStruct((rows, slots...  7.84 us
    pallas_call x1, Pallas kernels, gather_near(): pl.pallas_call(functools.partial(gather_kernel, chunk, groups), out_shape...  5.6 us
  transfers between devices with their start and end apart: 17, of which 6 were waited for; matrix products, arithmetic and copies ran while one was open for 1% of the time, Pallas kernels for 13%

profile of v1, /device:TPU:1, one launch (start us, length us, event | category | flops | bytes accessed | tf_op | source)
XLA Modules:
  0.0 176.5 jit_solution(2776598123502158194)
XLA Ops:
  2.8 2.1 %collective-permute-start.1 = (f32[72,128]{1,0:T(8,128)S(1)}, f32[72,128]{1,0:T(8,128)S(1)}, u32[]{:S(2)}, u32[]{:S(2)}) collective-permute-start(f32[72,128]{1,0:T(8,128)S(1)} %shard_map.91.refs_0_), channel_id=1, source_target_pairs={{0,2},{1,3},{2,0},{3,1},{4,6},{5,7},{6,4},{7,5},{8,10},{9,11},{10,... | collective-permute-start | bytes 110600 | tf_op jit(solution)/shard_map/ppermute | solution.py:209
  4.9 1.2 collective-permute-start.2
  6.2 2.2 %copy-done = bf16[128,128,128]{2,1,0:T(8,128)(2,1)S(1)} copy-done((bf16[128,128,128]{2,1,0:T(8,128)(2,1)S(1)}, bf16[128,128,128]{2,1,0:T(8,128)(2,1)}, u32[]{:S(2)}) %copy-start) | copy-done | bytes 4194328
  10.0 2.2 %shard_map.94 = bf16[64,4096]{1,0:T(8,128)(2,1)} custom-call(s32[1]{0:T(128)} %bitcast.11.block_ref, s32[128]{0:T(128)S(1)} %copy-done.12, bf16[64,2048]{1,0:T(8,128)(2,1)S(1)} %bitcast.34, bf16[128,128,128]{2,1,0:T(8,128)(2,1)S(1)} %copy-done), custom_call_target="tpu_custom_call" | custom-call | tf_op jit(solution)/shard_map/pallas_call | solution.py:51
  12.1 1.4 collective-permute-start.3
  13.5 2.2 %copy-done.1 = bf16[128,128,128]{2,1,0:T(8,128)(2,1)S(1)} copy-done((bf16[128,128,128]{2,1,0:T(8,128)(2,1)S(1)}, bf16[128,128,128]{2,1,0:T(8,128)(2,1)}, u32[]{:S(2)}) %copy-start.1) | copy-done | bytes 4194328
  15.7 2.2 %shard_map.95 = bf16[64,4096]{1,0:T(8,128)(2,1)} custom-call(s32[1]{0:T(128)} %bitcast.12.block_ref, s32[128]{0:T(128)S(1)} %copy-done.13, bf16[64,2048]{1,0:T(8,128)(2,1)S(1)} %bitcast.35, bf16[128,128,128]{2,1,0:T(8,128)(2,1)S(1)} %copy-done.1), custom_call_target="tpu_custom_call" | custom-call | tf_op jit(solution)/shard_map/pallas_call | solution.py:51
  17.8 1.2 collective-permute-start.4
  19.1 2.2 %copy-done.2 = bf16[128,128,128]{2,1,0:T(8,128)(2,1)S(1)} copy-done((bf16[128,128,128]{2,1,0:T(8,128)(2,1)S(1)}, bf16[128,128,128]{2,1,0:T(8,128)(2,1)}, u32[]{:S(2)}) %copy-start.2) | copy-done | bytes 4194328
  21.3 2.2 %shard_map.96 = bf16[64,4096]{1,0:T(8,128)(2,1)} custom-call(s32[1]{0:T(128)} %bitcast.13.block_ref, s32[128]{0:T(128)S(1)} %copy-done.13, bf16[64,2048]{1,0:T(8,128)(2,1)S(1)} %bitcast.36, bf16[128,128,128]{2,1,0:T(8,128)(2,1)S(1)} %copy-done.2), custom_call_target="tpu_custom_call" | custom-call | tf_op jit(solution)/shard_map/pallas_call | solution.py:51
  24.1 2.2 %copy-done.3 = bf16[128,128,128]{2,1,0:T(8,128)(2,1)S(1)} copy-done((bf16[128,128,128]{2,1,0:T(8,128)(2,1)S(1)}, bf16[128,128,128]{2,1,0:T(8,128)(2,1)}, u32[]{:S(2)}) %copy-start.3) | copy-done | bytes 4194328
  26.2 1.4 shard_map.93.refs_0_
  28.6 14.9 %shard_map.92.far_ref = f32[1,8,64,2048]{3,2,1,0:T(8,128)} custom-call(s32[1]{0:T(128)} %bitcast.8.me_ref.block_ref, s32[512]{0:T(512)S(1)} %reshape_squeeze.3.node_ref, f32[72,128]{1,0:T(8,128)S(1)} %shard_map.91.refs_0_, f32[72,128]{1,0:T(8,128)} %collective-permute-done.refs_1_, f32[72,128]{1,0:T(8,128)S(1)} %copy-done.11, ...), custom_call_target="tpu_custom_call" | custom-call | tf_op jit(solution)/shard_map/pallas_call | solution.py:110
  45.1 5.6 %shard_map.97 = (f32[4,64,2048]{2,1,0:T(8,128)S(1)}, bf16[4,64,2048]{2,1,0:T(8,128)(2,1)}) custom-call(s32[1]{0:T(128)} %bitcast.1.core_ref, s32[128]{0:T(128)S(1)} %pad_add_fusion.tgt_ref, f32[1,8,64,2048]{3,2,1,0:T(8,128)} %shard_map.92.far_ref, bf16[64,4096]{1,0:T(8,128)(2,1)S(1)} %shard_map.93.refs_0_, ...), custom_call_target="tpu_custom_call" | custom-call | tf_op jit(solution)/shard_map/pallas_call | solution.py:159
  50.7 2.1 %collective-permute-start.6 = (bf16[4,64,2048]{2,1,0:T(8,128)(2,1)}, bf16[4,64,2048]{2,1,0:T(8,128)(2,1)S(1)}, u32[]{:S(2)}, u32[]{:S(2)}) collective-permute-start(bf16[4,64,2048]{2,1,0:T(8,128)(2,1)} %get-tuple-element.8), channel_id=1, source_target_pairs={{0,4},{4,0},{8,12},{12,8},{16,20},{20,16},{24,28},{28,24},{1,5},{5... | collective-permute-start | bytes 3145736 | tf_op jit(solution)/shard_map/ppermute | solution.py:209
  52.8 2.5 %collective-permute-done.6 = bf16[4,64,2048]{2,1,0:T(8,128)(2,1)S(1)} collective-permute-done((bf16[4,64,2048]{2,1,0:T(8,128)(2,1)}, bf16[4,64,2048]{2,1,0:T(8,128)(2,1)S(1)}, u32[]{:S(2)}, u32[]{:S(2)}) %collective-permute-start.6) | collective-permute-done | bytes 1048608 | tf_op jit(solution)/shard_map/ppermute | solution.py:209
  55.3 1.6 convert_add_fusion
  56.9 1.5 fusion.3
  58.4 1.5 collective-permute-start.7
  59.9 2.3 %collective-permute-start.8 = (bf16[64,2048]{1,0:T(8,128)(2,1)S(1)}, bf16[64,2048]{1,0:T(8,128)(2,1)S(1)}, u32[]{:S(2)}, u32[]{:S(2)}) collective-permute-start(bf16[64,2048]{1,0:T(8,128)(2,1)S(1)} %get-tuple-element.11), channel_id=1, source_target_pairs={{0,16},{4,20},{8,24},{12,28},{16,0},{20,4},{24,8},{28,12},{1,17},{... | collective-permute-start | bytes 786440 | tf_op jit(solution)/shard_map/ppermute | solution.py:209
  62.2 8.8 %collective-permute-done.7 = bf16[64,2048]{1,0:T(8,128)(2,1)S(1)} collective-permute-done((bf16[64,2048]{1,0:T(8,128)(2,1)S(1)}, bf16[64,2048]{1,0:T(8,128)(2,1)S(1)}, u32[]{:S(2)}, u32[]{:S(2)}) %collective-permute-start.7) | collective-permute-done | bytes 262176 | tf_op jit(solution)/shard_map/ppermute | solution.py:209
  71.0 8.4 %collective-permute-done.9 = bf16[64,2048]{1,0:T(8,128)(2,1)S(1)} collective-permute-done((bf16[64,2048]{1,0:T(8,128)(2,1)S(1)}, bf16[64,2048]{1,0:T(8,128)(2,1)S(1)}, u32[]{:S(2)}, u32[]{:S(2)}) %collective-permute-start.9) | collective-permute-done | bytes 262176 | tf_op jit(solution)/shard_map/ppermute | solution.py:209
  79.4 1.2 fusion.2.refs_0_
  80.6 5.9 %collective-permute-start.11 = (bf16[64,2048]{1,0:T(8,128)(2,1)S(1)}, bf16[64,2048]{1,0:T(8,128)(2,1)S(1)}, u32[]{:S(2)}, u32[]{:S(2)}) collective-permute-start(bf16[64,2048]{1,0:T(8,128)(2,1)S(1)} %fusion.2.refs_0_), channel_id=1, source_target_pairs={{0,8},{4,12},{8,0},{12,4},{16,24},{20,28},{24,16},{28,20},{1,9},{5... | collective-permute-start | bytes 786440 | tf_op jit(solution)/shard_map/ppermute | solution.py:209
  86.5 1.1 collective-permute-start.13
  87.5 1.1 collective-permute-start.15
  88.7 2.0 %collective-permute-start.10 = (bf16[64,2048]{1,0:T(8,128)(2,1)S(1)}, bf16[64,2048]{1,0:T(8,128)(2,1)S(1)}, u32[]{:S(2)}, u32[]{:S(2)}) collective-permute-start(bf16[64,2048]{1,0:T(8,128)(2,1)S(1)} %fusion.2.refs_0_), channel_id=1, source_target_pairs={{0,4},{4,0},{8,12},{12,8},{16,20},{20,16},{24,28},{28,24},{1,5},{5... | collective-permute-start | bytes 786440 | tf_op jit(solution)/shard_map/ppermute | solution.py:209
  90.7 4.8 %collective-permute-done.11.refs_2_ = bf16[64,2048]{1,0:T(8,128)(2,1)S(1)} collective-permute-done((bf16[64,2048]{1,0:T(8,128)(2,1)S(1)}, bf16[64,2048]{1,0:T(8,128)(2,1)S(1)}, u32[]{:S(2)}, u32[]{:S(2)}) %collective-permute-start.11) | collective-permute-done | bytes 262176 | tf_op jit(solution)/shard_map/ppermute | solution.py:209
  95.5 2.7 %collective-permute-start.12 = (bf16[64,2048]{1,0:T(8,128)(2,1)S(1)}, bf16[64,2048]{1,0:T(8,128)(2,1)S(1)}, u32[]{:S(2)}, u32[]{:S(2)}) collective-permute-start(bf16[64,2048]{1,0:T(8,128)(2,1)S(1)} %collective-permute-done.11.refs_2_), channel_id=1, source_target_pairs={{0,4},{4,0},{8,12},{12,8},{16,20},{20,16},{24,28},{28,24},{1,5},{5... | collective-permute-start | bytes 786440 | tf_op jit(solution)/shard_map/ppermute | solution.py:209
  98.2 11.4 %collective-permute-start.14 = (bf16[64,2048]{1,0:T(8,128)(2,1)S(1)}, bf16[64,2048]{1,0:T(8,128)(2,1)S(1)}, u32[]{:S(2)}, u32[]{:S(2)}) collective-permute-start(bf16[64,2048]{1,0:T(8,128)(2,1)S(1)} %collective-permute-done.13.refs_4_), channel_id=1, source_target_pairs={{0,4},{4,0},{8,12},{12,8},{16,20},{20,16},{24,28},{28,24},{1,5},{5... | collective-permute-start | bytes 786440 | tf_op jit(solution)/shard_map/ppermute | solution.py:209
  109.7 1.1 collective-permute-done.14.refs_5_
  111.8 64.7 %shard_map.98 = bf16[64,16384]{1,0:T(8,128)(2,1)} custom-call(s32[1]{0:T(128)} %bitcast.me_ref, bf16[64,2048]{1,0:T(8,128)(2,1)} %copy-done.15, bf16[64,2048]{1,0:T(8,128)(2,1)} %copy-done.19, bf16[64,2048]{1,0:T(8,128)(2,1)} %copy-done.16, bf16[64,2048]{1,0:T(8,128)(2,1)} %copy-done.20, bf16[64,2048]{1,0:T(8,128)(2,1)} %copy-done.17, ...), custom_call_target="tpu_custom_call" | custom-call | tf_op jit(solution)/shard_map/pallas_call | solution.py:198
  (68 shorter events, 9.0 us)
Async XLA Ops:
  2.8 20.6 %collective-permute-start.1 = (f32[72,128]{1,0:T(8,128)S(1)}, f32[72,128]{1,0:T(8,128)S(1)}, u32[]{:S(2)}, u32[]{:S(2)}) collective-permute-start(f32[72,128]{1,0:T(8,128)S(1)} %shard_map.91.refs_0_), channel_id=1, source_target_pairs={{0,2},{1,3},{2,0},{3,1},{4,6},{5,7},{6,4},{7,5},{8,10},{9,11},{10,... | collective-permute-start | bytes 110600 | tf_op jit(solution)/shard_map/ppermute | solution.py:209
  4.9 22.7 %collective-permute-start.2 = (f32[72,128]{1,0:T(8,128)S(1)}, f32[72,128]{1,0:T(8,128)}, u32[]{:S(2)}, u32[]{:S(2)}) collective-permute-start(f32[72,128]{1,0:T(8,128)S(1)} %shard_map.91.refs_0_), channel_id=1, source_target_pairs={{0,3},{1,2},{2,1},{3,0},{4,7},{5,6},{6,5},{7,4},{8,11},{9,10},{10,... | collective-permute-start | bytes 110600 | tf_op jit(solution)/shard_map/ppermute | solution.py:209
  6.1 21.6 %collective-permute-start = (f32[72,128]{1,0:T(8,128)S(1)}, f32[72,128]{1,0:T(8,128)}, u32[]{:S(2)}, u32[]{:S(2)}) collective-permute-start(f32[72,128]{1,0:T(8,128)S(1)} %shard_map.91.refs_0_), channel_id=1, source_target_pairs={{0,1},{1,0},{2,3},{3,2},{4,5},{5,4},{6,7},{7,6},{8,9},{9,8},{10,11... | collective-permute-start | bytes 110600 | tf_op jit(solution)/shard_map/ppermute | solution.py:209
  6.2 2.2 %copy-start = (bf16[128,128,128]{2,1,0:T(8,128)(2,1)S(1)}, bf16[128,128,128]{2,1,0:T(8,128)(2,1)}, u32[]{:S(2)}) copy-start(bf16[128,128,128]{2,1,0:T(8,128)(2,1)} %tiles_ref.7) | copy-start | bytes 12582916
  10.0 3.5 %copy-start.6 = (bf16[2048,64]{0,1:T(8,128)(2,1)S(1)}, bf16[2048,64]{0,1:T(8,128)(2,1)}, u32[]{:S(2)}) copy-start(bf16[2048,64]{0,1:T(8,128)(2,1)} %param.9) | copy-start | bytes 786436
  10.0 3.5 %copy-start.13 = (s32[128]{0:T(128)S(1)}, s32[128]{0:T(128)}, u32[]{:S(2)}) copy-start(s32[128]{0:T(128)} %src_ref.7) | copy-start | bytes 1540
  12.1 33.0 %collective-permute-start.3 = (bf16[64,4096]{1,0:T(8,128)(2,1)}, bf16[64,4096]{1,0:T(8,128)(2,1)S(1)}, u32[]{:S(2)}, u32[]{:S(2)}) collective-permute-start(bf16[64,4096]{1,0:T(8,128)(2,1)} %shard_map.94), channel_id=1, source_target_pairs={{0,1},{1,0},{2,3},{3,2},{4,5},{5,4},{6,7},{7,6},{8,9},{9,8},{10,11... | collective-permute-start | bytes 1572872 | tf_op jit(solution)/shard_map/ppermute | solution.py:209
  13.5 2.2 %copy-start.1 = (bf16[128,128,128]{2,1,0:T(8,128)(2,1)S(1)}, bf16[128,128,128]{2,1,0:T(8,128)(2,1)}, u32[]{:S(2)}) copy-start(bf16[128,128,128]{2,1,0:T(8,128)(2,1)} %tiles_ref.7) | copy-start | bytes 12582916
  17.8 27.3 %collective-permute-start.4 = (bf16[64,4096]{1,0:T(8,128)(2,1)}, bf16[64,4096]{1,0:T(8,128)(2,1)}, u32[]{:S(2)}, u32[]{:S(2)}) collective-permute-start(bf16[64,4096]{1,0:T(8,128)(2,1)} %shard_map.95), channel_id=1, source_target_pairs={{0,2},{1,3},{2,0},{3,1},{4,6},{5,7},{6,4},{7,5},{8,10},{9,11},{10,... | collective-permute-start | bytes 1572872 | tf_op jit(solution)/shard_map/ppermute | solution.py:209
  19.1 2.2 %copy-start.2 = (bf16[128,128,128]{2,1,0:T(8,128)(2,1)S(1)}, bf16[128,128,128]{2,1,0:T(8,128)(2,1)}, u32[]{:S(2)}) copy-start(bf16[128,128,128]{2,1,0:T(8,128)(2,1)} %tiles_ref.7) | copy-start | bytes 12582916
  21.3 2.3 %copy-start.23 = (s32[1,128,4]{1,2,0:T(4,128)S(1)}, s32[1,128,4]{1,2,0:T(4,128)}, u32[]{:S(2)}) copy-start(s32[1,128,4]{1,2,0:T(4,128)} %param.16) | copy-start | bytes 6148
  23.4 21.7 %collective-permute-start.5 = (bf16[64,4096]{1,0:T(8,128)(2,1)}, bf16[64,4096]{1,0:T(8,128)(2,1)}, u32[]{:S(2)}, u32[]{:S(2)}) collective-permute-start(bf16[64,4096]{1,0:T(8,128)(2,1)} %shard_map.96), channel_id=1, source_target_pairs={{0,3},{1,2},{2,1},{3,0},{4,7},{5,6},{6,5},{7,4},{8,11},{9,10},{10,... | collective-permute-start | bytes 1572872 | tf_op jit(solution)/shard_map/ppermute | solution.py:209
  24.1 2.2 %copy-start.3 = (bf16[128,128,128]{2,1,0:T(8,128)(2,1)S(1)}, bf16[128,128,128]{2,1,0:T(8,128)(2,1)}, u32[]{:S(2)}) copy-start(bf16[128,128,128]{2,1,0:T(8,128)(2,1)} %tiles_ref.7) | copy-start | bytes 12582916
  26.2 1.6 copy-start.7
  26.2 1.6 copy-start.9
  50.7 4.6 %collective-permute-start.6 = (bf16[4,64,2048]{2,1,0:T(8,128)(2,1)}, bf16[4,64,2048]{2,1,0:T(8,128)(2,1)S(1)}, u32[]{:S(2)}, u32[]{:S(2)}) collective-permute-start(bf16[4,64,2048]{2,1,0:T(8,128)(2,1)} %get-tuple-element.8), channel_id=1, source_target_pairs={{0,4},{4,0},{8,12},{12,8},{16,20},{20,16},{24,28},{28,24},{1,5},{5... | collective-permute-start | bytes 3145736 | tf_op jit(solution)/shard_map/ppermute | solution.py:209
  58.4 12.6 %collective-permute-start.7 = (bf16[64,2048]{1,0:T(8,128)(2,1)S(1)}, bf16[64,2048]{1,0:T(8,128)(2,1)S(1)}, u32[]{:S(2)}, u32[]{:S(2)}) collective-permute-start(bf16[64,2048]{1,0:T(8,128)(2,1)S(1)} %get-tuple-element.9), channel_id=1, source_target_pairs={{0,8},{4,12},{8,0},{12,4},{16,24},{20,28},{24,16},{28,20},{1,9},{5... | collective-permute-start | bytes 786440 | tf_op jit(solution)/shard_map/ppermute | solution.py:209
  59.9 11.1 %collective-permute-start.8 = (bf16[64,2048]{1,0:T(8,128)(2,1)S(1)}, bf16[64,2048]{1,0:T(8,128)(2,1)S(1)}, u32[]{:S(2)}, u32[]{:S(2)}) collective-permute-start(bf16[64,2048]{1,0:T(8,128)(2,1)S(1)} %get-tuple-element.11), channel_id=1, source_target_pairs={{0,16},{4,20},{8,24},{12,28},{16,0},{20,4},{24,8},{28,12},{1,17},{... | collective-permute-start | bytes 786440 | tf_op jit(solution)/shard_map/ppermute | solution.py:209
  62.2 17.2 %collective-permute-start.9 = (bf16[64,2048]{1,0:T(8,128)(2,1)S(1)}, bf16[64,2048]{1,0:T(8,128)(2,1)S(1)}, u32[]{:S(2)}, u32[]{:S(2)}) collective-permute-start(bf16[64,2048]{1,0:T(8,128)(2,1)S(1)} %get-tuple-element.10), channel_id=1, source_target_pairs={{0,24},{4,28},{8,16},{12,20},{16,8},{20,12},{24,0},{28,4},{1,25},{... | collective-permute-start | bytes 786440 | tf_op jit(solution)/shard_map/ppermute | solution.py:209
  80.6 30.6 %copy-start.15 = (bf16[64,2048]{1,0:T(8,128)(2,1)}, bf16[64,2048]{1,0:T(8,128)(2,1)S(1)}, u32[]{:S(2)}) copy-start(bf16[64,2048]{1,0:T(8,128)(2,1)S(1)} %fusion.2.refs_0_) | copy-start | bytes 786436
  80.6 14.9 %collective-permute-start.11 = (bf16[64,2048]{1,0:T(8,128)(2,1)S(1)}, bf16[64,2048]{1,0:T(8,128)(2,1)S(1)}, u32[]{:S(2)}, u32[]{:S(2)}) collective-permute-start(bf16[64,2048]{1,0:T(8,128)(2,1)S(1)} %fusion.2.refs_0_), channel_id=1, source_target_pairs={{0,8},{4,12},{8,0},{12,4},{16,24},{20,28},{24,16},{28,20},{1,9},{5... | collective-permute-start | bytes 786440 | tf_op jit(solution)/shard_map/ppermute | solution.py:209
  86.5 11.7 %collective-permute-start.13 = (bf16[64,2048]{1,0:T(8,128)(2,1)S(1)}, bf16[64,2048]{1,0:T(8,128)(2,1)S(1)}, u32[]{:S(2)}, u32[]{:S(2)}) collective-permute-start(bf16[64,2048]{1,0:T(8,128)(2,1)S(1)} %fusion.2.refs_0_), channel_id=1, source_target_pairs={{0,16},{4,20},{8,24},{12,28},{16,0},{20,4},{24,8},{28,12},{1,17},{... | collective-permute-start | bytes 786440 | tf_op jit(solution)/shard_map/ppermute | solution.py:209
  87.5 22.0 %collective-permute-start.15 = (bf16[64,2048]{1,0:T(8,128)(2,1)S(1)}, bf16[64,2048]{1,0:T(8,128)(2,1)S(1)}, u32[]{:S(2)}, u32[]{:S(2)}) collective-permute-start(bf16[64,2048]{1,0:T(8,128)(2,1)S(1)} %fusion.2.refs_0_), channel_id=1, source_target_pairs={{0,24},{4,28},{8,16},{12,20},{16,8},{20,12},{24,0},{28,4},{1,25},{... | collective-permute-start | bytes 786440 | tf_op jit(solution)/shard_map/ppermute | solution.py:209
  88.7 21.0 %collective-permute-start.10 = (bf16[64,2048]{1,0:T(8,128)(2,1)S(1)}, bf16[64,2048]{1,0:T(8,128)(2,1)S(1)}, u32[]{:S(2)}, u32[]{:S(2)}) collective-permute-start(bf16[64,2048]{1,0:T(8,128)(2,1)S(1)} %fusion.2.refs_0_), channel_id=1, source_target_pairs={{0,4},{4,0},{8,12},{12,8},{16,20},{20,16},{24,28},{28,24},{1,5},{5... | collective-permute-start | bytes 786440 | tf_op jit(solution)/shard_map/ppermute | solution.py:209
  95.5 15.7 %copy-start.16 = (bf16[64,2048]{1,0:T(8,128)(2,1)}, bf16[64,2048]{1,0:T(8,128)(2,1)S(1)}, u32[]{:S(2)}) copy-start(bf16[64,2048]{1,0:T(8,128)(2,1)S(1)} %collective-permute-done.11.refs_2_) | copy-start | bytes 786436
  95.5 14.2 %collective-permute-start.12 = (bf16[64,2048]{1,0:T(8,128)(2,1)S(1)}, bf16[64,2048]{1,0:T(8,128)(2,1)S(1)}, u32[]{:S(2)}, u32[]{:S(2)}) collective-permute-start(bf16[64,2048]{1,0:T(8,128)(2,1)S(1)} %collective-permute-done.11.refs_2_), channel_id=1, source_target_pairs={{0,4},{4,0},{8,12},{12,8},{16,20},{20,16},{24,28},{28,24},{1,5},{5... | collective-permute-start | bytes 786440 | tf_op jit(solution)/shard_map/ppermute | solution.py:209
  98.2 13.0 %copy-start.17 = (bf16[64,2048]{1,0:T(8,128)(2,1)}, bf16[64,2048]{1,0:T(8,128)(2,1)S(1)}, u32[]{:S(2)}) copy-start(bf16[64,2048]{1,0:T(8,128)(2,1)S(1)} %collective-permute-done.13.refs_4_) | copy-start | bytes 786436
  98.2 12.6 %collective-permute-start.14 = (bf16[64,2048]{1,0:T(8,128)(2,1)S(1)}, bf16[64,2048]{1,0:T(8,128)(2,1)S(1)}, u32[]{:S(2)}, u32[]{:S(2)}) collective-permute-start(bf16[64,2048]{1,0:T(8,128)(2,1)S(1)} %collective-permute-done.13.refs_4_), channel_id=1, source_target_pairs={{0,4},{4,0},{8,12},{12,8},{16,20},{20,16},{24,28},{28,24},{1,5},{5... | collective-permute-start | bytes 786440 | tf_op jit(solution)/shard_map/ppermute | solution.py:209
  109.6 1.6 copy-start.18
  109.6 1.5 collective-permute-start.16
  109.7 1.5 copy-start.19
  109.7 1.5 copy-start.20
  (9 other events, 7.0 us)

commit v2 on v1

v2 whole, which is shorter than its diff:
```python
import functools

import jax
import jax.numpy as jnp
from jax import lax
from jax.experimental import pallas as pl
from jax.experimental.pallas import tpu as pltpu
from jax.sharding import PartitionSpec as P

NEAR_SPLIT = 4
FAR_STEPS = 4
F32, BF16 = jnp.float32, jnp.bfloat16
NT = (((1,), (1,)), ((), ()))
SMEM = pl.BlockSpec(memory_space=pltpu.SMEM)
VMEM = pl.BlockSpec(memory_space=pltpu.VMEM)
ANY = pl.BlockSpec(memory_space=pl.ANY)


def root_kernel(x_ref, basis_ref, tgt_ref, out_ref):
    leaves, rank, tile = basis_ref.shape
    nrhs = x_ref.shape[0]
    acc = jnp.zeros((nrhs, rank), F32)
    for i in range(leaves):
        acc += lax.dot_general(
            x_ref[:, i * tile : (i + 1) * tile], basis_ref[i], NT, preferred_element_type=F32
        )
    out_ref[:nrhs, :rank] = acc
    out_ref[nrhs:, :] = jnp.broadcast_to(tgt_ref[...].astype(F32), (8, out_ref.shape[1]))


def near_kernel(masks, groups, me_ref, src_ref, x_ref, tiles_ref, *refs):
    out_refs, held, sems = refs[:-2], refs[-2], refs[-1]
    tile = held.shape[1]
    slots = held.shape[0] // len(masks)
    step = slots // NEAR_SPLIT
    firsts = [(me_ref[0] ^ m) * slots for m in masks]
    copies = [
        pltpu.make_async_copy(
            tiles_ref.at[pl.ds(first + j * step, step)],
            held.at[pl.ds(n * slots + j * step, step)],
            sems.at[n * NEAR_SPLIT + j],
        )
        for n, first in enumerate(firsts)
        for j in range(NEAR_SPLIT)
    ]
    for copy in copies:
        copy.start()
    for n, first in enumerate(firsts):
        for k in range(slots):
            if k % step == 0:
                copies[n * NEAR_SPLIT + k // step].wait()
            leaf = src_ref[first + k]
            x = x_ref[:, pl.ds(pl.multiple_of(leaf * tile, tile), tile)]
            y = lax.dot_general(x, held[n * slots + k], NT, preferred_element_type=F32)
            out_refs[n][:, k * tile : (k + 1) * tile] = y.astype(BF16)


def near_products(masks, me, near_src, x, tiles, groups):
    count, tile, _ = tiles.shape
    slots = count // groups
    nrhs = x.shape[0]
    return pl.pallas_call(
        functools.partial(near_kernel, masks, groups),
        out_shape=[jax.ShapeDtypeStruct((nrhs, slots * tile), BF16)] * len(masks),
        in_specs=[SMEM, SMEM, VMEM, ANY],
        out_specs=[VMEM] * len(masks),
        scratch_shapes=[
            pltpu.VMEM((slots * len(masks), tile, tile), BF16),
            pltpu.SemaphoreType.DMA((NEAR_SPLIT * len(masks),)),
        ],
        compiler_params=pltpu.CompilerParams(vmem_limit_bytes=58 * 2**20),
        cost_estimate=pl.CostEstimate(
            flops=2 * slots * len(masks) * tile * tile * nrhs,
            bytes_accessed=slots * len(masks) * tile * (tile + nrhs) * 2,
            transcendentals=0,
        ),
    )(me, near_src, x, tiles)


def far_kernel(groups, me_ref, node_ref, *refs):
    root_refs = refs[:groups]
    edge_ref, coupling_ref, basis_ref, out_ref, exact, low, high = refs[groups:]
    step = pl.program_id(0)
    leaves, rank, tile = basis_ref.shape
    per = coupling_ref.shape[2] // rank
    nrhs = out_ref.shape[1]

    @pl.when(step == 0)
    def _():
        for m in range(groups):
            exact[groups - 1 + (me_ref[0] ^ m)] = root_refs[m][:nrhs, :rank]
        for n in range(groups - 2, -1, -1):
            pair = jnp.concatenate([exact[2 * n + 1], exact[2 * n + 2]], axis=1)
            exact[n] = lax.dot_general(
                pair, edge_ref[n], NT, precision=lax.Precision.HIGHEST, preferred_element_type=F32
            )
        zero = jnp.zeros((nrhs, rank), BF16)
        for n in range(2 * groups - 1):
            node = exact[n].astype(BF16)
            low[n] = jnp.concatenate([node, zero], axis=1)
            high[n] = jnp.concatenate([zero, node], axis=1)

    zs = []
    for i in range(leaves):
        tau = step * leaves + i
        nodes = [node_ref[tau * per + k] for k in range(per)]
        stacked = jnp.concatenate(
            [low[nodes[k]] + high[nodes[k + 1]] for k in range(0, per, 2)], axis=1
        )
        zs.append(
            lax.dot_general(stacked, coupling_ref[i], NT, preferred_element_type=F32).astype(BF16)
        )
    wide = out_ref.shape[2] // tile
    for i in range(leaves):
        at = (i % wide) * tile
        out_ref[i // wide, :, at : at + tile] = jnp.dot(
            zs[i], basis_ref[i], preferred_element_type=F32
        )


def far_field(me, far_node, roots, transfer, coupling, target_basis, pieces):
    groups = len(roots)
    tgt_tiles, rank, tile = target_basis.shape
    leaves = tgt_tiles // FAR_STEPS
    nrhs = roots[0].shape[0] - 8
    nodes = 2 * groups - 1
    many = pieces // FAR_STEPS
    width = tgt_tiles // pieces * tile
    return pl.pallas_call(
        functools.partial(far_kernel, groups),
        out_shape=jax.ShapeDtypeStruct((pieces, nrhs, width), F32),
        grid_spec=pltpu.PrefetchScalarGridSpec(
            num_scalar_prefetch=2,
            grid=(FAR_STEPS,),
            in_specs=[pl.BlockSpec(r.shape, lambda i, a, b: (0, 0)) for r in roots]
            + [
                pl.BlockSpec(transfer.shape, lambda i, a, b: (0, 0, 0)),
                pl.BlockSpec((leaves,) + coupling.shape[1:], lambda i, a, b: (i, 0, 0)),
                pl.BlockSpec((leaves, rank, tile), lambda i, a, b: (i, 0, 0)),
            ],
            out_specs=pl.BlockSpec((many, nrhs, width), lambda i, a, b: (i, 0, 0)),
            scratch_shapes=[
                pltpu.VMEM((nodes, nrhs, rank), F32),
                pltpu.VMEM((nodes, nrhs, 2 * rank), BF16),
                pltpu.VMEM((nodes, nrhs, 2 * rank), BF16),
            ],
        ),
        compiler_params=pltpu.CompilerParams(vmem_limit_bytes=24 * 2**20),
        cost_estimate=pl.CostEstimate(
            flops=2 * tgt_tiles * nrhs * (coupling.shape[1] * coupling.shape[2] + rank * tile),
            bytes_accessed=(coupling.size + target_basis.size) * 2 + tgt_tiles * tile * nrhs * 4,
            transcendentals=0,
        ),
    )(me, far_node, *roots, transfer, coupling, target_basis)


def gather_kernel(groups, core_ref, tgt_ref, far_ref, *refs):
    got_refs, (acc, send_ref) = refs[:groups], refs[groups:]
    pieces, rows, width = acc.shape
    slots = tgt_ref.shape[0] // groups
    tile = got_refs[0].shape[1] // slots
    leaves = width // tile
    for m in range(groups):
        for k in range(slots):
            leaf = tgt_ref[m * slots + k]
            piece = leaf // leaves
            spot = pl.ds(pl.multiple_of((leaf - piece * leaves) * tile, tile), tile)
            acc[piece, :, spot] = acc[piece, :, spot] + got_refs[m][
                :, k * tile : (k + 1) * tile
            ].astype(F32)
    core = core_ref[0]
    for z in range(pieces // 2):
        send_ref[z] = acc[2 * z + 1 - core].astype(BF16)


def gather_near(core, tgt, far, got):
    pieces, rows, width = far.shape
    groups = len(got)
    return pl.pallas_call(
        functools.partial(gather_kernel, groups),
        out_shape=[
            jax.ShapeDtypeStruct(far.shape, F32),
            jax.ShapeDtypeStruct((pieces // 2, rows, width), BF16),
        ],
        in_specs=[SMEM, SMEM, VMEM] + [VMEM] * groups,
        out_specs=[VMEM, VMEM],
        input_output_aliases={2: 0},
        compiler_params=pltpu.CompilerParams(vmem_limit_bytes=16 * 2**20),
    )(core, tgt, far, *got)


def split_kernel(masks, me_ref, acc_ref, got_ref, *out_refs):
    z, core = me_ref[0] // 2, me_ref[0] % 2
    for m, out_ref in zip(masks, out_refs):
        piece = z ^ m
        out_ref[...] = (acc_ref[2 * piece + core] + got_ref[piece].astype(F32)).astype(
            out_ref.dtype
        )


def split(masks, dtypes, me, acc, got):
    return pl.pallas_call(
        functools.partial(split_kernel, masks),
        out_shape=[jax.ShapeDtypeStruct(got.shape[1:], d) for d in dtypes],
        in_specs=[SMEM, VMEM, VMEM],
        out_specs=[VMEM] * len(masks),
        compiler_params=pltpu.CompilerParams(vmem_limit_bytes=16 * 2**20),
    )(me, acc, got)


def place_kernel(masks, me_ref, *refs):
    out_ref = refs[-1]
    for m, piece_ref in zip(masks, refs):
        width = piece_ref.shape[1]
        spot = pl.ds(pl.multiple_of((me_ref[0] ^ m) * width, width), width)
        out_ref[:, spot] = piece_ref[...]


def place(masks, me, parts):
    rows, width = parts[0].shape
    return pl.pallas_call(
        functools.partial(place_kernel, masks),
        out_shape=jax.ShapeDtypeStruct((rows, width * len(parts)), BF16),
        in_specs=[SMEM] + [VMEM] * len(parts),
        out_specs=VMEM,
        compiler_params=pltpu.CompilerParams(vmem_limit_bytes=16 * 2**20),
    )(me, *parts)


def swap(value, axis, mask):
    size = lax.axis_size(axis)
    return lax.ppermute(value, axis, [(i, i ^ mask) for i in range(size)])


def tied(value, *others):
    return lax.optimization_barrier((value,) + others)[0]


def sum_and_share(me, acc, got):
    chips = acc.shape[0] // 2
    if chips == 4:
        masks = (3, 2, 1, 0)
        first, cross, near, own = split(masks, (BF16, F32, BF16, F32), me, acc, got)
        a = swap(first, "src", 2)
        cross = (cross + a.astype(F32)).astype(BF16)
        b = swap(cross, "src", 4)
        c = swap(tied(near, cross), "src", 2)
        own = (own + b.astype(F32) + c.astype(F32)).astype(BF16)
        d = swap(own, "src", 4)
        e = swap(own, "src", 2)
        return (0, 1, 2, 3), [own, e, d, swap(d, "src", 2)]
    masks = tuple(range(chips))
    dtypes = (F32,) + (BF16,) * (chips - 1)
    own, *rest = split(masks, dtypes, me, acc, got)
    for m, part in zip(masks[1:], rest):
        own = own + swap(part, "src", 2 * m).astype(F32)
    own = own.astype(BF16)
    return masks, [own] + [swap(own, "src", 2 * m) for m in masks[1:]]


def shards(
    charges, near_tiles, near_tgt, near_src, leaf_basis, transfer, coupling, far_node, target_basis
):
    groups = lax.axis_size("tgt")
    sources = lax.axis_size("src")
    me_t = lax.axis_index("tgt").astype(jnp.int32)
    me_s = lax.axis_index("src").astype(jnp.int32)
    tiles, tile, _ = near_tiles.shape
    slots = tiles // groups
    nrhs = charges.shape[1]
    x = charges.T
    me = me_t.reshape(1)

    masks = sorted(range(groups), key=lambda m: -bin(m).count("1"))
    (first,) = near_products(masks[:1], me, near_src, x, near_tiles, groups)
    x_late = tied(x, first)
    message = pl.pallas_call(
        root_kernel,
        out_shape=jax.ShapeDtypeStruct((nrhs + 8, tiles), F32),
        in_specs=[VMEM] * 3,
        out_specs=VMEM,
        compiler_params=pltpu.CompilerParams(vmem_limit_bytes=16 * 2**20),
    )(x_late, leaf_basis, near_tgt.reshape(1, tiles))
    messages = [message] + [swap(message, "tgt", m) for m in range(1, groups)]
    rest = near_products(masks[1:], me, near_src, x_late, near_tiles, groups)
    got = [swap(y, "tgt", m) if m else y for m, y in zip(masks, [first, *rest])]
    far = far_field(
        me,
        far_node[0].reshape(-1),
        messages,
        transfer[0],
        coupling[0],
        target_basis,
        sources,
    )
    targets = jnp.concatenate(
        [
            lax.dynamic_slice(messages[m], (nrhs, me_t * slots), (1, slots))[0].astype(jnp.int32)
            for m in masks
        ]
    )
    acc, send = gather_near((me_s % 2).reshape(1), targets, far, got)
    owners, mine = sum_and_share(me_s.reshape(1), acc, swap(send, "src", 1))
    other = [swap(p, "src", 1) for p in mine]
    spots = [2 * m for m in owners] + [2 * m + 1 for m in owners]
    return place(spots, me_s.reshape(1), mine + other).T


def solution(mesh):
    in_specs = (
        P(("src", "tgt"), None),
        P(("src", "tgt"), None, None),
        P(("src", "tgt")),
        P(("src", "tgt")),
        P(("src", "tgt"), None, None),
        P("src", None, None, None),
        P("src", "tgt", None, None),
        P("src", "tgt", None),
        P("tgt", None, None),
    )
    out_specs = P("tgt", None)
    return jax.shard_map(shards, mesh=mesh, in_specs=in_specs, out_specs=out_specs, check_vma=False)
```

time: 178 us -> 85 us (0.48)
  Pallas kernels: 93.2 us -> 18.2 us
  local copies, waits for them, and re-layouts: 16.5 us -> 2.43 us
  waiting for transfers between devices: 26 us -> 39.7 us
  starting transfers between devices: 36.2 us -> 23.4 us
  other arithmetic: 4.46 us -> 0.53 us
    pallas_call x6 -> x5, Pallas kernels: 78.1 us -> 14.3 us  [the longest x2 10.4 us: near_products(): pl.pallas_call(functools.partial(near_kernel, masks, groups), out_shape=[...]
    ppermute x17, waiting for transfers between devices: 26 us -> 39.7 us  [swap(): return lax.ppermute(value, axis, [(i, i ^ mask) for i in range(size)])]
    ppermute x17, starting transfers between devices: 36.2 us -> 23.4 us  [swap(): return lax.ppermute(value, axis, [(i, i ^ mask) for i in range(size)])]
    unnamed x49 -> x17, local copies, waits for them, and re-layouts: 15 us -> 2.32 us
    pallas_call x1, Pallas kernels: 14.9 us -> 3.66 us  [far_field(): pl.pallas_call(functools.partial(far_kernel, groups), out_shape=jax.Shape...]
    convert_element_type x5 -> x6, other arithmetic: 2.82 us -> 0.46 us  [the longest x4 0.3 us: shards(): lax.dynamic_slice(messages[m], (nrhs, me_t * slots), (1, slots))[0]]
  transfers between devices with their start and end apart: 17 -> 17, of which waited for: 6 -> 8; matrix products, arithmetic and copies ran while one was open for 1% -> 1% of each run, Pallas kernels for 13% -> 12%
where the time goes in v2:
time: 85 us; the launch traced here: 84.4 us
  waiting for transfers between devices  39.7 us (47%)
  starting transfers between devices  23.4 us (28%)
  Pallas kernels  18.2 us (21%)
  local copies, waits for them, and re-layouts  2.43 us (3%)
    ppermute x17, waiting for transfers between devices, swap(): return lax.ppermute(value, axis, [(i, i ^ mask) for i in range(size)])  39.7 us
    ppermute x17, starting transfers between devices, swap(): return lax.ppermute(value, axis, [(i, i ^ mask) for i in range(size)])  23.4 us
    pallas_call x2, Pallas kernels, near_products(): pl.pallas_call(functools.partial(near_kernel, masks, groups), out_shape=[...  10.4 us
    pallas_call x1, Pallas kernels, far_field(): pl.pallas_call(functools.partial(far_kernel, groups), out_shape=jax.Shape...  3.66 us
    unnamed x17, local copies, waits for them, and re-layouts  2.32 us
    pallas_call x1, Pallas kernels, gather_near(): pl.pallas_call(functools.partial(gather_kernel, groups), out_shape=[jax.S...  2.28 us
  transfers between devices with their start and end apart: 17, of which 8 were waited for; matrix products, arithmetic and copies ran while one was open for 1% of the time, Pallas kernels for 12%

profile of v2, /device:TPU:1, one launch (start us, length us, event | category | flops | bytes accessed | tf_op | source)
XLA Modules:
  0.0 84.4 jit_solution(9504309083676058971)
XLA Ops:
  0.0 4.0 %shard_map.91 = bf16[64,4096]{1,0:T(8,128)(2,1)} custom-call(s32[1]{0:T(128)} %bitcast.3.me_ref, s32[128]{0:T(128)} %src_ref.3, bf16[64,2048]{1,0:T(8,128)(2,1)} %bitcast.17, bf16[128,128,128]{2,1,0:T(8,128)(2,1)} %tiles_ref.3), custom_call_target="tpu_custom_call" | custom-call | flops 67108864 | bytes 1572864 | tf_op jit(solution)/shard_map/pallas_call | solution.py:62
  4.1 0.3 shard_map.92.refs_0_
  4.4 2.1 %collective-permute-start.2 = (f32[72,128]{1,0:T(8,128)S(1)}, f32[72,128]{1,0:T(8,128)S(1)}, u32[]{:S(2)}, u32[]{:S(2)}) collective-permute-start(f32[72,128]{1,0:T(8,128)S(1)} %shard_map.92.refs_0_), channel_id=1, source_target_pairs={{0,2},{1,3},{2,0},{3,1},{4,6},{5,7},{6,4},{7,5},{8,10},{9,11},{10,... | collective-permute-start | bytes 110600 | tf_op jit(solution)/shard_map/ppermute | solution.py:232
  6.5 1.2 %collective-permute-start.1 = (f32[72,128]{1,0:T(8,128)S(1)}, f32[72,128]{1,0:T(8,128)S(1)}, u32[]{:S(2)}, u32[]{:S(2)}) collective-permute-start(f32[72,128]{1,0:T(8,128)S(1)} %shard_map.92.refs_0_), channel_id=1, source_target_pairs={{0,1},{1,0},{2,3},{3,2},{4,5},{5,4},{6,7},{7,6},{8,9},{9,8},{10,11... | collective-permute-start | bytes 110600 | tf_op jit(solution)/shard_map/ppermute | solution.py:232
  7.7 2.3 %collective-permute-start.3 = (bf16[64,4096]{1,0:T(8,128)(2,1)}, bf16[64,4096]{1,0:T(8,128)(2,1)S(1)}, u32[]{:S(2)}, u32[]{:S(2)}) collective-permute-start(bf16[64,4096]{1,0:T(8,128)(2,1)} %shard_map.91), channel_id=1, source_target_pairs={{0,3},{1,2},{2,1},{3,0},{4,7},{5,6},{6,5},{7,4},{8,11},{9,10},{10,... | collective-permute-start | bytes 1572872 | tf_op jit(solution)/shard_map/ppermute | solution.py:232
  10.0 6.3 %shard_map.94 = (bf16[64,4096]{1,0:T(8,128)(2,1)}, bf16[64,4096]{1,0:T(8,128)(2,1)}, bf16[64,4096]{1,0:T(8,128)(2,1)}) custom-call(s32[1]{0:T(128)} %bitcast.3.me_ref, s32[128]{0:T(128)} %src_ref.3, bf16[64,2048]{1,0:T(8,128)(2,1)} %bitcast.18, bf16[128,128,128]{2,1,0:T(8,128)(2,1)} %tiles_ref.3), custom_call_target="tpu_custom_call" | custom-call | flops 201326592 | bytes 4718592 | tf_op jit(solution)/shard_map/pallas_call | solution.py:62
  16.4 0.3 collective-permute-start.4
  16.9 0.1 copy.11
  17.0 0.1 reshape_squeeze.3.node_ref
  17.1 2.2 %copy-done = bf16[1,128,64,256]{3,2,1,0:T(8,128)(2,1)S(1)} copy-done((bf16[1,128,64,256]{3,2,1,0:T(8,128)(2,1)S(1)}, bf16[1,128,64,256]{3,2,1,0:T(8,128)(2,1)}, u32[]{:S(2)}) %copy-start) | copy-done | bytes 4194328
  19.3 3.7 %shard_map.93.far_ref = f32[8,64,2048]{2,1,0:T(8,128)S(1)} custom-call(s32[1]{0:T(128)} %bitcast.3.me_ref, s32[512]{0:T(512)S(1)} %reshape_squeeze.3.node_ref, f32[72,128]{1,0:T(8,128)S(1)} %shard_map.92.refs_0_, f32[72,128]{1,0:T(8,128)S(1)} %collective-permute-done.1.refs_1_, f32[72,128]{1,0:T(8,128)S(1)} %collective-permute-done.2.refs_2_, ...), custom_call_target="tpu_custom_call" | custom-call | flops 402653184 | bytes 10485760 | tf_op jit(solution)/shard_map/pallas_call | solution.py:129
  23.3 9.8 %collective-permute-done.4.refs_1_ = bf16[64,4096]{1,0:T(8,128)(2,1)S(1)} collective-permute-done((bf16[64,4096]{1,0:T(8,128)(2,1)}, bf16[64,4096]{1,0:T(8,128)(2,1)S(1)}, u32[]{:S(2)}, u32[]{:S(2)}) %collective-permute-start.4) | collective-permute-done | bytes 524320 | tf_op jit(solution)/shard_map/ppermute | solution.py:232
  33.1 1.2 %collective-permute-done.5.refs_2_ = bf16[64,4096]{1,0:T(8,128)(2,1)} collective-permute-done((bf16[64,4096]{1,0:T(8,128)(2,1)}, bf16[64,4096]{1,0:T(8,128)(2,1)}, u32[]{:S(2)}, u32[]{:S(2)}) %collective-permute-start.5) | collective-permute-done | bytes 524320 | tf_op jit(solution)/shard_map/ppermute | solution.py:232
  34.3 2.3 %shard_map.95 = (f32[8,64,2048]{2,1,0:T(8,128)S(1)}, bf16[4,64,2048]{2,1,0:T(8,128)(2,1)S(1)}) custom-call(s32[1]{0:T(128)} %bitcast.1.core_ref, s32[128]{0:T(128)S(1)} %pad_add_fusion.tgt_ref, f32[8,64,2048]{2,1,0:T(8,128)S(1)} %shard_map.93.far_ref, bf16[64,4096]{1,0:T(8,128)(2,1)S(1)} %collective-permute-done.3.refs_0_, ...), custom_call_target="tpu_custom_call", output_to_operand_aliasing={{0}: (2, {})} | custom-call | tf_op jit(solution)/shard_map/pallas_call | solution.py:179
  36.6 0.8 collective-permute-start.6
  37.4 2.3 %collective-permute-done.6.got_ref = bf16[4,64,2048]{2,1,0:T(8,128)(2,1)S(1)} collective-permute-done((bf16[4,64,2048]{2,1,0:T(8,128)(2,1)S(1)}, bf16[4,64,2048]{2,1,0:T(8,128)(2,1)S(1)}, u32[]{:S(2)}, u32[]{:S(2)}) %collective-permute-start.6) | collective-permute-done | bytes 1048608 | tf_op jit(solution)/shard_map/ppermute | solution.py:232
  39.7 0.2 shard_map.96
  39.9 1.4 %collective-permute-start.7 = (bf16[64,2048]{1,0:T(8,128)(2,1)S(1)}, bf16[64,2048]{1,0:T(8,128)(2,1)S(1)}, u32[]{:S(2)}, u32[]{:S(2)}) collective-permute-start(bf16[64,2048]{1,0:T(8,128)(2,1)S(1)} %get-tuple-element.24), channel_id=1, source_target_pairs={{0,8},{4,12},{8,0},{12,4},{16,24},{20,28},{24,16},{28,20},{1,9},{5... | collective-permute-start | bytes 786440 | tf_op jit(solution)/shard_map/ppermute | solution.py:232
  41.2 6.2 %collective-permute-done.7 = bf16[64,2048]{1,0:T(8,128)(2,1)S(1)} collective-permute-done((bf16[64,2048]{1,0:T(8,128)(2,1)S(1)}, bf16[64,2048]{1,0:T(8,128)(2,1)S(1)}, u32[]{:S(2)}, u32[]{:S(2)}) %collective-permute-start.7) | collective-permute-done | bytes 262176 | tf_op jit(solution)/shard_map/ppermute | solution.py:232
  47.5 1.4 %collective-permute-start.9 = (bf16[64,2048]{1,0:T(8,128)(2,1)S(1)}, bf16[64,2048]{1,0:T(8,128)(2,1)S(1)}, u32[]{:S(2)}, u32[]{:S(2)}) collective-permute-start(bf16[64,2048]{1,0:T(8,128)(2,1)S(1)} %get-tuple-element.26), channel_id=1, source_target_pairs={{0,8},{4,12},{8,0},{12,4},{16,24},{20,28},{24,16},{28,20},{1,9},{5... | collective-permute-start | bytes 786440 | tf_op jit(solution)/shard_map/ppermute | solution.py:232
  48.9 2.3 %collective-permute-start.8 = (bf16[64,2048]{1,0:T(8,128)(2,1)S(1)}, bf16[64,2048]{1,0:T(8,128)(2,1)S(1)}, u32[]{:S(2)}, u32[]{:S(2)}) collective-permute-start(bf16[64,2048]{1,0:T(8,128)(2,1)S(1)} %add_convert_fusion.1), channel_id=1, source_target_pairs={{0,16},{4,20},{8,24},{12,28},{16,0},{20,4},{24,8},{28,12},{1,17},{... | collective-permute-start | bytes 786440 | tf_op jit(solution)/shard_map/ppermute | solution.py:232
  51.2 8.3 %collective-permute-done.9 = bf16[64,2048]{1,0:T(8,128)(2,1)S(1)} collective-permute-done((bf16[64,2048]{1,0:T(8,128)(2,1)S(1)}, bf16[64,2048]{1,0:T(8,128)(2,1)S(1)}, u32[]{:S(2)}, u32[]{:S(2)}) %collective-permute-start.9) | collective-permute-done | bytes 262176 | tf_op jit(solution)/shard_map/ppermute | solution.py:232
  59.6 2.6 %collective-permute-start.11 = (bf16[64,2048]{1,0:T(8,128)(2,1)S(1)}, bf16[64,2048]{1,0:T(8,128)(2,1)S(1)}, u32[]{:S(2)}, u32[]{:S(2)}) collective-permute-start(bf16[64,2048]{1,0:T(8,128)(2,1)S(1)} %add_convert_fusion.refs_0_), channel_id=1, source_target_pairs={{0,16},{4,20},{8,24},{12,28},{16,0},{20,4},{24,8},{28,12},{1,17},{... | collective-permute-start | bytes 786440 | tf_op jit(solution)/shard_map/ppermute | solution.py:232
  62.2 0.6 collective-permute-start.10
  62.8 9.1 %collective-permute-done.11.refs_2_ = bf16[64,2048]{1,0:T(8,128)(2,1)S(1)} collective-permute-done((bf16[64,2048]{1,0:T(8,128)(2,1)S(1)}, bf16[64,2048]{1,0:T(8,128)(2,1)S(1)}, u32[]{:S(2)}, u32[]{:S(2)}) %collective-permute-start.11) | collective-permute-done | bytes 262176 | tf_op jit(solution)/shard_map/ppermute | solution.py:232
  72.0 1.6 %collective-permute-start.12 = (bf16[64,2048]{1,0:T(8,128)(2,1)S(1)}, bf16[64,2048]{1,0:T(8,128)(2,1)S(1)}, u32[]{:S(2)}, u32[]{:S(2)}) collective-permute-start(bf16[64,2048]{1,0:T(8,128)(2,1)S(1)} %collective-permute-done.11.refs_2_), channel_id=1, source_target_pairs={{0,8},{4,12},{8,0},{12,4},{16,24},{20,28},{24,16},{28,20},{1,9},{5... | collective-permute-start | bytes 786440 | tf_op jit(solution)/shard_map/ppermute | solution.py:232
  73.5 1.9 %collective-permute-start.13 = (bf16[64,2048]{1,0:T(8,128)(2,1)S(1)}, bf16[64,2048]{1,0:T(8,128)(2,1)S(1)}, u32[]{:S(2)}, u32[]{:S(2)}) collective-permute-start(bf16[64,2048]{1,0:T(8,128)(2,1)S(1)} %add_convert_fusion.refs_0_), channel_id=1, source_target_pairs={{0,4},{4,0},{8,12},{12,8},{16,20},{20,16},{24,28},{28,24},{1,5},{5... | collective-permute-start | bytes 786440 | tf_op jit(solution)/shard_map/ppermute | solution.py:232
  75.4 0.5 collective-permute-start.14
  75.9 1.6 %collective-permute-done.12.refs_3_ = bf16[64,2048]{1,0:T(8,128)(2,1)S(1)} collective-permute-done((bf16[64,2048]{1,0:T(8,128)(2,1)S(1)}, bf16[64,2048]{1,0:T(8,128)(2,1)S(1)}, u32[]{:S(2)}, u32[]{:S(2)}) %collective-permute-start.12) | collective-permute-done | bytes 262176 | tf_op jit(solution)/shard_map/ppermute | solution.py:232
  77.5 4.3 %collective-permute-start.16 = (bf16[64,2048]{1,0:T(8,128)(2,1)S(1)}, bf16[64,2048]{1,0:T(8,128)(2,1)S(1)}, u32[]{:S(2)}, u32[]{:S(2)}) collective-permute-start(bf16[64,2048]{1,0:T(8,128)(2,1)S(1)} %collective-permute-done.12.refs_3_), channel_id=1, source_target_pairs={{0,4},{4,0},{8,12},{12,8},{16,20},{20,16},{24,28},{28,24},{1,5},{5... | collective-permute-start | bytes 786440 | tf_op jit(solution)/shard_map/ppermute | solution.py:232
  81.8 1.1 %collective-permute-done.16.refs_7_ = bf16[64,2048]{1,0:T(8,128)(2,1)S(1)} collective-permute-done((bf16[64,2048]{1,0:T(8,128)(2,1)S(1)}, bf16[64,2048]{1,0:T(8,128)(2,1)S(1)}, u32[]{:S(2)}, u32[]{:S(2)}) %collective-permute-start.16) | collective-permute-done | bytes 262176 | tf_op jit(solution)/shard_map/ppermute | solution.py:232
  83.0 1.5 %shard_map.97 = bf16[64,16384]{1,0:T(8,128)(2,1)} custom-call(s32[1]{0:T(128)} %bitcast.me_ref, bf16[64,2048]{1,0:T(8,128)(2,1)S(1)} %add_convert_fusion.refs_0_, bf16[64,2048]{1,0:T(8,128)(2,1)S(1)} %collective-permute-done.10.refs_1_, bf16[64,2048]{1,0:T(8,128)(2,1)S(1)} %collective-permute-done.11.refs_2_, ...), custom_call_target="tpu_custom_call" | custom-call | tf_op jit(solution)/shard_map/pallas_call | solution.py:221
  (34 shorter events, 0.7 us)
Async XLA Ops:
  0.0 4.1 %copy-start.1 = (bf16[2048,64]{0,1:T(8,128)(2,1)S(1)}, bf16[2048,64]{0,1:T(8,128)(2,1)}, u32[]{:S(2)}) copy-start(bf16[2048,64]{0,1:T(8,128)(2,1)} %param.9) | copy-start | bytes 786436
  0.0 4.1 %copy-start.4 = (bf16[16,64,128]{2,1,0:T(8,128)(2,1)S(1)}, bf16[16,64,128]{2,1,0:T(8,128)(2,1)}, u32[]{:S(2)}) copy-start(bf16[16,64,128]{2,1,0:T(8,128)(2,1)} %basis_ref.1) | copy-start | bytes 786436
  0.0 4.1 %copy-start.6 = (s32[128]{0:T(128)S(1)}, s32[128]{0:T(128)}, u32[]{:S(2)}) copy-start(s32[128]{0:T(128)} %param.11) | copy-start | bytes 1540
  0.0 16.9 %copy-start.7 = (s32[1,128,4]{1,2,0:T(4,128)S(1)}, s32[1,128,4]{1,2,0:T(4,128)}, u32[]{:S(2)}) copy-start(s32[1,128,4]{1,2,0:T(4,128)} %param.16) | copy-start | bytes 6148
  0.0 17.1 %copy-start.2 = (bf16[128,64,128]{2,1,0:T(8,128)(2,1)S(1)}, bf16[128,64,128]{2,1,0:T(8,128)(2,1)}, u32[]{:S(2)}) copy-start(bf16[128,64,128]{2,1,0:T(8,128)(2,1)} %refs_6_.1) | copy-start | bytes 6291460
  0.0 17.1 %copy-start.5 = (f32[1,3,64,128]{3,2,1,0:T(8,128)S(1)}, f32[1,3,64,128]{3,2,1,0:T(8,128)}, u32[]{:S(2)}) copy-start(f32[1,3,64,128]{3,2,1,0:T(8,128)} %param.14) | copy-start | bytes 294916
  4.4 12.4 %collective-permute-start.2 = (f32[72,128]{1,0:T(8,128)S(1)}, f32[72,128]{1,0:T(8,128)S(1)}, u32[]{:S(2)}, u32[]{:S(2)}) collective-permute-start(f32[72,128]{1,0:T(8,128)S(1)} %shard_map.92.refs_0_), channel_id=1, source_target_pairs={{0,2},{1,3},{2,0},{3,1},{4,6},{5,7},{6,4},{7,5},{8,10},{9,11},{10,... | collective-permute-start | bytes 110600 | tf_op jit(solution)/shard_map/ppermute | solution.py:232
  6.5 10.6 %collective-permute-start.1 = (f32[72,128]{1,0:T(8,128)S(1)}, f32[72,128]{1,0:T(8,128)S(1)}, u32[]{:S(2)}, u32[]{:S(2)}) collective-permute-start(f32[72,128]{1,0:T(8,128)S(1)} %shard_map.92.refs_0_), channel_id=1, source_target_pairs={{0,1},{1,0},{2,3},{3,2},{4,5},{5,4},{6,7},{7,6},{8,9},{9,8},{10,11... | collective-permute-start | bytes 110600 | tf_op jit(solution)/shard_map/ppermute | solution.py:232
  7.7 9.4 %collective-permute-start = (f32[72,128]{1,0:T(8,128)S(1)}, f32[72,128]{1,0:T(8,128)S(1)}, u32[]{:S(2)}, u32[]{:S(2)}) collective-permute-start(f32[72,128]{1,0:T(8,128)S(1)} %shard_map.92.refs_0_), channel_id=1, source_target_pairs={{0,3},{1,2},{2,1},{3,0},{4,7},{5,6},{6,5},{7,4},{8,11},{9,10},{10,... | collective-permute-start | bytes 110600 | tf_op jit(solution)/shard_map/ppermute | solution.py:232
  7.7 15.6 %collective-permute-start.3 = (bf16[64,4096]{1,0:T(8,128)(2,1)}, bf16[64,4096]{1,0:T(8,128)(2,1)S(1)}, u32[]{:S(2)}, u32[]{:S(2)}) collective-permute-start(bf16[64,4096]{1,0:T(8,128)(2,1)} %shard_map.91), channel_id=1, source_target_pairs={{0,3},{1,2},{2,1},{3,0},{4,7},{5,6},{6,5},{7,4},{8,11},{9,10},{10,... | collective-permute-start | bytes 1572872 | tf_op jit(solution)/shard_map/ppermute | solution.py:232
  16.4 16.7 %collective-permute-start.4 = (bf16[64,4096]{1,0:T(8,128)(2,1)}, bf16[64,4096]{1,0:T(8,128)(2,1)S(1)}, u32[]{:S(2)}, u32[]{:S(2)}) collective-permute-start(bf16[64,4096]{1,0:T(8,128)(2,1)} %get-tuple-element.17), channel_id=1, source_target_pairs={{0,1},{1,0},{2,3},{3,2},{4,5},{5,4},{6,7},{7,6},{8,9},{9,8},{10,11... | collective-permute-start | bytes 1572872 | tf_op jit(solution)/shard_map/ppermute | solution.py:232
  16.7 17.6 %collective-permute-start.5 = (bf16[64,4096]{1,0:T(8,128)(2,1)}, bf16[64,4096]{1,0:T(8,128)(2,1)}, u32[]{:S(2)}, u32[]{:S(2)}) collective-permute-start(bf16[64,4096]{1,0:T(8,128)(2,1)} %get-tuple-element.18), channel_id=1, source_target_pairs={{0,2},{1,3},{2,0},{3,1},{4,6},{5,7},{6,4},{7,5},{8,10},{9,11},{10,... | collective-permute-start | bytes 1572872 | tf_op jit(solution)/shard_map/ppermute | solution.py:232
  17.1 2.2 %copy-start = (bf16[1,128,64,256]{3,2,1,0:T(8,128)(2,1)S(1)}, bf16[1,128,64,256]{3,2,1,0:T(8,128)(2,1)}, u32[]{:S(2)}) copy-start(bf16[1,128,64,256]{3,2,1,0:T(8,128)(2,1)} %param.15) | copy-start | bytes 12582916
  19.3 15.0 %copy-start.3 = (bf16[64,4096]{1,0:T(8,128)(2,1)S(1)}, bf16[64,4096]{1,0:T(8,128)(2,1)}, u32[]{:S(2)}) copy-start(bf16[64,4096]{1,0:T(8,128)(2,1)} %get-tuple-element.19.refs_3_) | copy-start | bytes 1572868
  36.6 3.1 %collective-permute-start.6 = (bf16[4,64,2048]{2,1,0:T(8,128)(2,1)S(1)}, bf16[4,64,2048]{2,1,0:T(8,128)(2,1)S(1)}, u32[]{:S(2)}, u32[]{:S(2)}) collective-permute-start(bf16[4,64,2048]{2,1,0:T(8,128)(2,1)S(1)} %get-tuple-element.21), channel_id=1, source_target_pairs={{0,4},{4,0},{8,12},{12,8},{16,20},{20,16},{24,28},{28,24},{1,5},{5... | collective-permute-start | bytes 3145736 | tf_op jit(solution)/shard_map/ppermute | solution.py:232
  39.9 7.6 %collective-permute-start.7 = (bf16[64,2048]{1,0:T(8,128)(2,1)S(1)}, bf16[64,2048]{1,0:T(8,128)(2,1)S(1)}, u32[]{:S(2)}, u32[]{:S(2)}) collective-permute-start(bf16[64,2048]{1,0:T(8,128)(2,1)S(1)} %get-tuple-element.24), channel_id=1, source_target_pairs={{0,8},{4,12},{8,0},{12,4},{16,24},{20,28},{24,16},{28,20},{1,9},{5... | collective-permute-start | bytes 786440 | tf_op jit(solution)/shard_map/ppermute | solution.py:232
  47.5 12.0 %collective-permute-start.9 = (bf16[64,2048]{1,0:T(8,128)(2,1)S(1)}, bf16[64,2048]{1,0:T(8,128)(2,1)S(1)}, u32[]{:S(2)}, u32[]{:S(2)}) collective-permute-start(bf16[64,2048]{1,0:T(8,128)(2,1)S(1)} %get-tuple-element.26), channel_id=1, source_target_pairs={{0,8},{4,12},{8,0},{12,4},{16,24},{20,28},{24,16},{28,20},{1,9},{5... | collective-permute-start | bytes 786440 | tf_op jit(solution)/shard_map/ppermute | solution.py:232
  48.9 10.6 %collective-permute-start.8 = (bf16[64,2048]{1,0:T(8,128)(2,1)S(1)}, bf16[64,2048]{1,0:T(8,128)(2,1)S(1)}, u32[]{:S(2)}, u32[]{:S(2)}) collective-permute-start(bf16[64,2048]{1,0:T(8,128)(2,1)S(1)} %add_convert_fusion.1), channel_id=1, source_target_pairs={{0,16},{4,20},{8,24},{12,28},{16,0},{20,4},{24,8},{28,12},{1,17},{... | collective-permute-start | bytes 786440 | tf_op jit(solution)/shard_map/ppermute | solution.py:232
  59.6 12.4 %collective-permute-start.11 = (bf16[64,2048]{1,0:T(8,128)(2,1)S(1)}, bf16[64,2048]{1,0:T(8,128)(2,1)S(1)}, u32[]{:S(2)}, u32[]{:S(2)}) collective-permute-start(bf16[64,2048]{1,0:T(8,128)(2,1)S(1)} %add_convert_fusion.refs_0_), channel_id=1, source_target_pairs={{0,16},{4,20},{8,24},{12,28},{16,0},{20,4},{24,8},{28,12},{1,17},{... | collective-permute-start | bytes 786440 | tf_op jit(solution)/shard_map/ppermute | solution.py:232
  62.2 13.2 %collective-permute-start.10 = (bf16[64,2048]{1,0:T(8,128)(2,1)S(1)}, bf16[64,2048]{1,0:T(8,128)(2,1)S(1)}, u32[]{:S(2)}, u32[]{:S(2)}) collective-permute-start(bf16[64,2048]{1,0:T(8,128)(2,1)S(1)} %add_convert_fusion.refs_0_), channel_id=1, source_target_pairs={{0,8},{4,12},{8,0},{12,4},{16,24},{20,28},{24,16},{28,20},{1,9},{5... | collective-permute-start | bytes 786440 | tf_op jit(solution)/shard_map/ppermute | solution.py:232
  72.0 5.6 %collective-permute-start.12 = (bf16[64,2048]{1,0:T(8,128)(2,1)S(1)}, bf16[64,2048]{1,0:T(8,128)(2,1)S(1)}, u32[]{:S(2)}, u32[]{:S(2)}) collective-permute-start(bf16[64,2048]{1,0:T(8,128)(2,1)S(1)} %collective-permute-done.11.refs_2_), channel_id=1, source_target_pairs={{0,8},{4,12},{8,0},{12,4},{16,24},{20,28},{24,16},{28,20},{1,9},{5... | collective-permute-start | bytes 786440 | tf_op jit(solution)/shard_map/ppermute | solution.py:232
  73.5 8.3 %collective-permute-start.13 = (bf16[64,2048]{1,0:T(8,128)(2,1)S(1)}, bf16[64,2048]{1,0:T(8,128)(2,1)S(1)}, u32[]{:S(2)}, u32[]{:S(2)}) collective-permute-start(bf16[64,2048]{1,0:T(8,128)(2,1)S(1)} %add_convert_fusion.refs_0_), channel_id=1, source_target_pairs={{0,4},{4,0},{8,12},{12,8},{16,20},{20,16},{24,28},{28,24},{1,5},{5... | collective-permute-start | bytes 786440 | tf_op jit(solution)/shard_map/ppermute | solution.py:232
  75.4 6.4 %collective-permute-start.15 = (bf16[64,2048]{1,0:T(8,128)(2,1)S(1)}, bf16[64,2048]{1,0:T(8,128)(2,1)S(1)}, u32[]{:S(2)}, u32[]{:S(2)}) collective-permute-start(bf16[64,2048]{1,0:T(8,128)(2,1)S(1)} %collective-permute-done.11.refs_2_), channel_id=1, source_target_pairs={{0,4},{4,0},{8,12},{12,8},{16,20},{20,16},{24,28},{28,24},{1,5},{5... | collective-permute-start | bytes 786440 | tf_op jit(solution)/shard_map/ppermute | solution.py:232
  75.4 6.4 %collective-permute-start.14 = (bf16[64,2048]{1,0:T(8,128)(2,1)S(1)}, bf16[64,2048]{1,0:T(8,128)(2,1)S(1)}, u32[]{:S(2)}, u32[]{:S(2)}) collective-permute-start(bf16[64,2048]{1,0:T(8,128)(2,1)S(1)} %collective-permute-done.10.refs_1_), channel_id=1, source_target_pairs={{0,4},{4,0},{8,12},{12,8},{16,20},{20,16},{24,28},{28,24},{1,5},{5... | collective-permute-start | bytes 786440 | tf_op jit(solution)/shard_map/ppermute | solution.py:232
  77.5 5.4 %collective-permute-start.16 = (bf16[64,2048]{1,0:T(8,128)(2,1)S(1)}, bf16[64,2048]{1,0:T(8,128)(2,1)S(1)}, u32[]{:S(2)}, u32[]{:S(2)}) collective-permute-start(bf16[64,2048]{1,0:T(8,128)(2,1)S(1)} %collective-permute-done.12.refs_3_), channel_id=1, source_target_pairs={{0,4},{4,0},{8,12},{12,8},{16,20},{20,16},{24,28},{28,24},{1,5},{5... | collective-permute-start | bytes 786440 | tf_op jit(solution)/shard_map/ppermute | solution.py:232

commit v3 on v0

v3 whole, which is shorter than its diff:
```python
import functools
import typing

import jax
import jax.numpy as jnp
from jax import lax
from jax.experimental import pallas as pl
from jax.experimental.pallas import tpu as pltpu
from jax.sharding import PartitionSpec as P

STEP = 8
HEAD = 8
FIRST_HEAD = 32
FAR_PIECES = 2
NEAR_VMEM = 60
F32, BF16 = jnp.float32, jnp.bfloat16
NT = (((1,), (1,)), ((), ()))
SMEM = pl.BlockSpec(memory_space=pltpu.SMEM)
LONG = pl.CostEstimate(flops=2**36, bytes_accessed=2**24, transcendentals=0)
VMEM = pl.BlockSpec(memory_space=pltpu.VMEM)
ANY = pl.BlockSpec(memory_space=pl.ANY)


class Part(typing.NamedTuple):
    mask: int
    slots: int
    begin: int
    end: int
    head: bool


def near_kernel(parts, me_ref, src_ref, tgt_ref, x_hbm, basis_ref, tiles_ref, *refs):
    outs, (x_ref, basis, held, sems) = refs[: len(parts)], refs[len(parts) :]
    tile = held.shape[1]
    leaves, rank, _ = basis.shape
    nrhs = x_ref.shape[0]
    count = tiles_ref.shape[0]
    slots = parts[0].slots
    extra = [
        pltpu.make_async_copy(x_hbm, x_ref, sems.at[0]),
        pltpu.make_async_copy(basis_ref, basis, sems.at[1]),
    ]
    copies, spans, at = [], [], 0
    for part in parts:
        first = (me_ref[0] ^ part.mask) * slots
        for k in range(part.begin, part.end, STEP):
            size = min(STEP, part.end - k)
            spans.append((part, k, size, at))
            copies.append(
                pltpu.make_async_copy(
                    tiles_ref.at[pl.ds(first + k, size)],
                    held.at[pl.ds(at, size)],
                    sems.at[2 + len(copies)],
                )
            )
            at += size
    for copy in extra + copies:
        copy.start()
    for copy in extra:
        copy.wait()
    if any(part.head for part in parts):
        root = jnp.zeros((nrhs, rank), F32)
        for i in range(leaves):
            root += lax.dot_general(
                x_ref[:, i * tile : (i + 1) * tile], basis[i], NT, preferred_element_type=F32
            )
        high = root.astype(BF16)
        low = (root - high.astype(F32)).astype(BF16)
        roots = jnp.concatenate([high, low], axis=1)
        tgt = jnp.broadcast_to(tgt_ref[...].astype(F32).astype(BF16), (nrhs, count))
        for part, out in zip(parts, outs):
            if part.head:
                end = out.shape[1] - count
                out[:, end - 2 * rank : end] = roots
                out[:, end:] = tgt
    for (part, begin, size, at), copy in zip(spans, copies):
        copy.wait()
        first = (me_ref[0] ^ part.mask) * slots
        out = outs[parts.index(part)]
        for k in range(size):
            leaf = src_ref[first + begin + k]
            x = x_ref[:, pl.ds(pl.multiple_of(leaf * tile, tile), tile)]
            y = lax.dot_general(x, held[at + k], NT, preferred_element_type=F32)
            spot = (begin - part.begin + k) * tile
            out[:, spot : spot + tile] = y.astype(BF16)


def near_products(parts, me, near_src, near_tgt, x, basis, tiles):
    count, tile, _ = tiles.shape
    nrhs, rank = x.shape[0], basis.shape[1]
    widths = [(p.end - p.begin) * tile + (2 * rank + count if p.head else 0) for p in parts]
    blocks = sum(-(-(p.end - p.begin) // STEP) for p in parts)
    return pl.pallas_call(
        functools.partial(near_kernel, parts),
        out_shape=[jax.ShapeDtypeStruct((nrhs, w), BF16) for w in widths],
        in_specs=[SMEM, SMEM, VMEM, ANY, ANY, ANY],
        out_specs=[VMEM] * len(widths),
        scratch_shapes=[
            pltpu.VMEM(x.shape, BF16),
            pltpu.VMEM(basis.shape, BF16),
            pltpu.VMEM((sum(p.end - p.begin for p in parts), tile, tile), BF16),
            pltpu.SemaphoreType.DMA((blocks + 2,)),
        ],
        compiler_params=pltpu.CompilerParams(vmem_limit_bytes=NEAR_VMEM * 2**20),
    )(me, near_src, near_tgt.reshape(1, count), x, basis, tiles)


def add_products(acc, tgt_ref, me, parts, got_refs, tile):
    leaves = acc.shape[2] // tile
    for n, (part, got_ref) in enumerate(zip(parts, got_refs)):
        for k in range(part.begin, part.end):
            leaf = tgt_ref[n, me * part.slots + k]
            piece = leaf // leaves
            spot = pl.ds(pl.multiple_of((leaf - piece * leaves) * tile, tile), tile)
            at = (k - part.begin) * tile
            got = got_ref[:, at : at + tile].astype(F32)
            acc[piece, :, spot] = acc[piece, :, spot] + got


def start_kernel(parts, tile, me_ref, tgt_ref, *refs):
    acc = refs[-1]
    acc[...] = jnp.zeros_like(acc)
    add_products(acc, tgt_ref, me_ref[0], parts, refs[:-1], tile)


def start_near(parts, me, tgt, got, pieces, width, tile):
    return pl.pallas_call(
        functools.partial(start_kernel, parts, tile),
        out_shape=jax.ShapeDtypeStruct((pieces, got[0].shape[0], width), F32),
        in_specs=[SMEM, SMEM] + [VMEM] * len(got),
        out_specs=VMEM,
        cost_estimate=LONG,
        compiler_params=pltpu.CompilerParams(vmem_limit_bytes=16 * 2**20),
    )(me, tgt, *got)


def far_kernel(groups, count, me_ref, node_ref, *refs):
    head_refs = refs[:groups]
    edge_ref, coupling_ref, basis_ref, near_ref, out_ref, exact, low, high = refs[groups:]
    tgt_tiles, rank, tile = basis_ref.shape
    per = coupling_ref.shape[2] // rank
    pieces, nrhs, width = out_ref.shape
    leaves = width // tile
    for m in range(groups):
        end = head_refs[m].shape[1] - count
        pair = head_refs[m][:, end - 2 * rank : end].astype(F32)
        exact[groups - 1 + (me_ref[0] ^ m)] = pair[:, :rank] + pair[:, rank:]
    for n in range(groups - 2, -1, -1):
        pair = jnp.concatenate([exact[2 * n + 1], exact[2 * n + 2]], axis=1)
        exact[n] = lax.dot_general(
            pair, edge_ref[n], NT, precision=lax.Precision.HIGHEST, preferred_element_type=F32
        )
    zero = jnp.zeros((nrhs, rank), BF16)
    for n in range(2 * groups - 1):
        node = exact[n].astype(BF16)
        low[n] = jnp.concatenate([node, zero], axis=1)
        high[n] = jnp.concatenate([zero, node], axis=1)

    @pl.loop(0, pieces // FAR_PIECES)
    def _(block):
        first = block * FAR_PIECES
        zs = []
        for i in range(FAR_PIECES * leaves):
            tau = first * leaves + i
            nodes = [node_ref[tau * per + k] for k in range(per)]
            stacked = jnp.concatenate(
                [low[nodes[k]] + high[nodes[k + 1]] for k in range(0, per, 2)], axis=1
            )
            z = lax.dot_general(stacked, coupling_ref[tau], NT, preferred_element_type=F32)
            zs.append(z.astype(BF16))
        for i in range(FAR_PIECES * leaves):
            far = jnp.dot(zs[i], basis_ref[first * leaves + i], preferred_element_type=F32)
            p, at = first + i // leaves, slice(i % leaves * tile, (i % leaves + 1) * tile)
            out_ref[p, :, at] = near_ref[p, :, at] + far


def far_field(me, far_node, heads, transfer, coupling, target_basis, near, count):
    groups = len(heads)
    rank = target_basis.shape[1]
    nrhs = near.shape[1]
    nodes = 2 * groups - 1
    return pl.pallas_call(
        functools.partial(far_kernel, groups, count),
        out_shape=jax.ShapeDtypeStruct(near.shape, F32),
        in_specs=[SMEM, SMEM] + [VMEM] * (groups + 4),
        out_specs=VMEM,
        scratch_shapes=[
            pltpu.VMEM((nodes, nrhs, rank), F32),
            pltpu.VMEM((nodes, nrhs, 2 * rank), BF16),
            pltpu.VMEM((nodes, nrhs, 2 * rank), BF16),
        ],
        input_output_aliases={groups + 5: 0},
        compiler_params=pltpu.CompilerParams(vmem_limit_bytes=16 * 2**20),
    )(me, far_node, *heads, transfer, coupling, target_basis, near)


def gather_kernel(parts, tile, me_ref, core_ref, tgt_ref, far_ref, *refs):
    got_refs, (acc, send_ref) = refs[:-2], refs[-2:]
    add_products(acc, tgt_ref, me_ref[0], parts, got_refs, tile)
    for z in range(send_ref.shape[0]):
        send_ref[z] = acc[2 * z + 1 - core_ref[0]].astype(BF16)


def gather_near(parts, me, core, tgt, far, got, tile):
    pieces, rows, width = far.shape
    return pl.pallas_call(
        functools.partial(gather_kernel, parts, tile),
        out_shape=[
            jax.ShapeDtypeStruct(far.shape, F32),
            jax.ShapeDtypeStruct((pieces // 2, rows, width), BF16),
        ],
        in_specs=[SMEM] * 3 + [VMEM] * (1 + len(got)),
        out_specs=[VMEM, VMEM],
        input_output_aliases={3: 0},
        compiler_params=pltpu.CompilerParams(vmem_limit_bytes=16 * 2**20),
    )(me, core, tgt, far, *got)


def split_kernel(masks, me_ref, acc_ref, got_ref, *out_refs):
    z, core = me_ref[0] // 2, me_ref[0] % 2
    for m, out_ref in zip(masks, out_refs):
        piece = z ^ m
        out_ref[...] = (acc_ref[2 * piece + core] + got_ref[piece].astype(F32)).astype(
            out_ref.dtype
        )


def split(masks, dtypes, me, acc, got):
    return pl.pallas_call(
        functools.partial(split_kernel, masks),
        out_shape=[jax.ShapeDtypeStruct(got.shape[1:], d) for d in dtypes],
        in_specs=[SMEM, VMEM, VMEM],
        out_specs=[VMEM] * len(masks),
        compiler_params=pltpu.CompilerParams(vmem_limit_bytes=16 * 2**20),
    )(me, acc, got)


def place_kernel(masks, me_ref, *refs):
    out_ref = refs[-1]
    for m, piece_ref in zip(masks, refs):
        width = piece_ref.shape[1]
        spot = pl.ds(pl.multiple_of((me_ref[0] ^ m) * width, width), width)
        out_ref[:, spot] = piece_ref[...]


def place(masks, me, parts):
    rows, width = parts[0].shape
    return pl.pallas_call(
        functools.partial(place_kernel, masks),
        out_shape=jax.ShapeDtypeStruct((rows, width * len(parts)), BF16),
        in_specs=[SMEM] + [VMEM] * len(parts),
        out_specs=VMEM,
        compiler_params=pltpu.CompilerParams(vmem_limit_bytes=16 * 2**20),
    )(me, *parts)


def swap(value, axis, mask):
    size = lax.axis_size(axis)
    return lax.ppermute(value, axis, [(i, i ^ mask) for i in range(size)])


def tied(value, *others):
    return lax.optimization_barrier((value,) + others)[0]


def sum_and_share(me, acc, got):
    chips = acc.shape[0] // 2
    if chips == 4:
        masks = (3, 2, 1, 0)
        first, cross, near, own = split(masks, (BF16, F32, BF16, F32), me, acc, got)
        a = swap(first, "src", 2)
        cross = (cross + a.astype(F32)).astype(BF16)
        b = swap(cross, "src", 4)
        c = swap(tied(near, cross), "src", 2)
        own = (own + b.astype(F32) + c.astype(F32)).astype(BF16)
        d = swap(own, "src", 4)
        e = swap(own, "src", 2)
        return (0, 1, 2, 3), [own, e, d, swap(d, "src", 2)]
    masks = tuple(range(chips))
    dtypes = (F32,) + (BF16,) * (chips - 1)
    own, *rest = split(masks, dtypes, me, acc, got)
    for m, part in zip(masks[1:], rest):
        own = own + swap(part, "src", 2 * m).astype(F32)
    own = own.astype(BF16)
    return masks, [own] + [swap(own, "src", 2 * m) for m in masks[1:]]


def shards(
    charges, near_tiles, near_tgt, near_src, leaf_basis, transfer, coupling, far_node, target_basis
):
    groups = lax.axis_size("tgt")
    sources = lax.axis_size("src")
    me_t = lax.axis_index("tgt").astype(jnp.int32)
    me_s = lax.axis_index("src").astype(jnp.int32)
    count, tile, _ = near_tiles.shape
    slots = count // groups
    x = charges.T
    me, core = me_t.reshape(1), (me_s % 2).reshape(1)

    masks = sorted(range(groups), key=lambda m: -bin(m).count("1"))
    ends = [min(FIRST_HEAD, slots)] + [min(HEAD, slots)] * (groups - 2) + [slots]
    heads = [Part(m, slots, 0, e, True) for m, e in zip(masks, ends)]
    tails = [Part(m, slots, e, slots, False) for m, e in zip(masks, ends) if e < slots]
    first = near_products(heads[:1], me, near_src, near_tgt, x, leaf_basis, near_tiles)
    rest = near_products(
        heads[1:] + tails, me, near_src, near_tgt, tied(x, *first), leaf_basis, near_tiles
    )
    parts = heads + tails
    got = {
        part: swap(y, "tgt", part.mask) if part.mask else y
        for part, y in zip(parts, [*first, *rest])
    }
    by_mask = {part.mask: got[part] for part in heads}

    def targets(some):
        rows = [by_mask[part.mask][:1, -count:] for part in some]
        return jnp.concatenate(rows).astype(F32).astype(jnp.int32)

    early = [part for part in heads if part.mask in (masks[0], masks[-1])]
    late = [part for part in parts if part not in early]
    acc = start_near(
        early,
        me,
        targets(early),
        [got[part] for part in early],
        sources,
        target_basis.shape[0] // sources * tile,
        tile,
    )
    acc = far_field(
        me,
        far_node[0].reshape(-1),
        [by_mask[m] for m in range(groups)],
        transfer[0],
        coupling[0],
        target_basis,
        acc,
        count,
    )
    acc, send = gather_near(
        late, me, core, targets(late), acc, [got[part] for part in late], tile
    )
    owners, mine = sum_and_share(me_s.reshape(1), acc, swap(send, "src", 1))
    other = [swap(p, "src", 1) for p in mine]
    spots = [2 * m for m in owners] + [2 * m + 1 for m in owners]
    return place(spots, me_s.reshape(1), mine + other).T


def solution(mesh):
    in_specs = (
        P(("src", "tgt"), None),
        P(("src", "tgt"), None, None),
        P(("src", "tgt")),
        P(("src", "tgt")),
        P(("src", "tgt"), None, None),
        P("src", None, None, None),
        P("src", "tgt", None, None),
        P("src", "tgt", None),
        P("tgt", None, None),
    )
    out_specs = P("tgt", None)
    return jax.shard_map(shards, mesh=mesh, in_specs=in_specs, out_specs=out_specs, check_vma=False)
```

time: 230 us -> 83.2 us (0.36); the launches traced: 227 us -> 82.6 us
  blocking collectives: 151 us -> 0 us
  waiting for transfers between devices: 3.39 us -> 35.2 us
  matrix products: 22.5 us -> 0 us
  local copies, waits for them, and re-layouts: 25 us -> 3.44 us
  Pallas kernels: 0 us -> 19.5 us
  starting transfers between devices: 9.36 us -> 24.2 us
  between operations: 13.6 us -> 0.13 us
    psum x1 -> x0, blocking collectives: 89.5 us -> none  [shards(): total = lax.psum(near_part + far_part, 'src')]
    all_gather x1 -> x0, blocking collectives: 56 us -> none  [shards(): roots = lax.all_gather(own_root[None], 'tgt', axis=0, tiled=True)]
    ppermute x0 -> x16, waiting for transfers between devices: none -> 35.2 us  [swap(): return lax.ppermute(value, axis, [(i, i ^ mask) for i in range(size)])]
    ppermute x0 -> x16, starting transfers between devices: none -> 24.2 us  [swap(): return lax.ppermute(value, axis, [(i, i ^ mask) for i in range(size)])]
    dot_general x6 -> x0, matrix products: 22.5 us -> none  [the longest x1 10.1 us: shards(): jnp.einsum('trp,trn->tpn', target_basis, zed, preferred_element_type=jnp....]
    pallas_call x0 -> x7, Pallas kernels: none -> 19.5 us  [the longest x2 11.1 us: near_products(): pl.pallas_call(functools.partial(near_kernel, parts), out_shape=[jax.Shap...]
    gather x2 -> x0, local copies, waits for them, and re-layouts: 15.6 us -> none  [the longest x1 13.4 us: shards(): chosen = table_b[far_node[0]]]
    all_to_all x2 -> x0, starting transfers between devices: 9.32 us -> none  [the longest x1 5.05 us: shards(): lax.all_to_all(near_tiles.reshape(groups, slots, tile, tile), 'tgt', spli...]
  transfers between devices with their start and end apart: 3 -> 16, of which waited for: 1 -> 9; matrix products, arithmetic and copies ran while one was open for 14% -> 1% of each run, Pallas kernels for 0% -> 15%
where the time goes in v3:
time: 83.2 us; the launch traced here: 82.6 us
  waiting for transfers between devices  35.2 us (42%)
  starting transfers between devices  24.2 us (29%)
  Pallas kernels  19.5 us (23%)
  local copies, waits for them, and re-layouts  3.44 us (4%)
    ppermute x16, waiting for transfers between devices, swap(): return lax.ppermute(value, axis, [(i, i ^ mask) for i in range(size)])  35.2 us
    ppermute x16, starting transfers between devices, swap(): return lax.ppermute(value, axis, [(i, i ^ mask) for i in range(size)])  24.2 us
    pallas_call x2, Pallas kernels, near_products(): pl.pallas_call(functools.partial(near_kernel, parts), out_shape=[jax.Shap...  11.1 us
    pallas_call x1, Pallas kernels, far_field(): pl.pallas_call(functools.partial(far_kernel, groups, count), out_shape=ja...  4.08 us
    unnamed x11, local copies, waits for them, and re-layouts  2.64 us
  transfers between devices with their start and end apart: 16, of which 9 were waited for; matrix products, arithmetic and copies ran while one was open for 1% of the time, Pallas kernels for 15%

profile of v3, /device:TPU:1, one launch (start us, length us, event | category | flops | bytes accessed | tf_op | source)
XLA Modules:
  0.0 82.6 jit_solution(4284270862520350346)
XLA Ops:
  0.0 4.4 %shard_map.91 = bf16[64,4352]{1,0:T(8,128)(2,1)} custom-call(s32[1]{0:T(128)} %bitcast.1.me_ref, s32[128]{0:T(128)} %src_ref.3, s32[1,128]{1,0:T(1,128)} %bitcast.12, bf16[64,2048]{1,0:T(8,128)(2,1)} %bitcast.10, bf16[16,64,128]{2,1,0:T(8,128)(2,1)} %basis_ref.3, bf16[128,128,128]{2,1,0:T(8,128)(2,1)} %tiles_ref.3), custom_call_target="tpu_custom_call" | custom-call | tf_op jit(solution)/shard_map/pallas_call | solution.py:93
  4.4 3.1 %collective-permute-start.2 = (bf16[64,4352]{1,0:T(8,128)(2,1)}, bf16[64,4352]{1,0:T(8,128)(2,1)S(1)}, u32[]{:S(2)}, u32[]{:S(2)}) collective-permute-start(bf16[64,4352]{1,0:T(8,128)(2,1)} %shard_map.91), channel_id=1, source_target_pairs={{0,3},{1,2},{2,1},{3,0},{4,7},{5,6},{6,5},{7,4},{8,11},{9,10},{10,... | collective-permute-start | bytes 1671176 | tf_op jit(solution)/shard_map/ppermute | solution.py:259
  7.5 6.7 %shard_map.92 = (bf16[64,1280]{1,0:T(8,128)(2,1)}, bf16[64,1280]{1,0:T(8,128)(2,1)}, bf16[64,4352]{1,0:T(8,128)(2,1)}, bf16[64,3072]{1,0:T(8,128)(2,1)}, bf16[64,3072]{1,0:T(8,128)(2,1)}) custom-call(s32[1]{0:T(128)} %bitcast.1.me_ref, s32[128]{0:T(128)} %src_ref.3, s32[1,128]{1,0:T(1,128)} %bitcast.13, bf16[64,2048]{1,0:T(8,128)(2,1)} %bitcast.11, ...), custom_call_target="tpu_custom_call" | custom-call | tf_op jit(solution)/shard_map/pallas_call | solution.py:93
  14.6 1.4 %collective-permute-start.3 = (bf16[64,3072]{1,0:T(8,128)(2,1)}, bf16[64,3072]{1,0:T(8,128)(2,1)S(1)}, u32[]{:S(2)}, u32[]{:S(2)}) collective-permute-start(bf16[64,3072]{1,0:T(8,128)(2,1)} %get-tuple-element.22), channel_id=1, source_target_pairs={{0,1},{1,0},{2,3},{3,2},{4,5},{5,4},{6,7},{7,6},{8,9},{9,8},{10,11... | collective-permute-start | bytes 1179656 | tf_op jit(solution)/shard_map/ppermute | solution.py:259
  16.0 1.2 %collective-permute-start.4 = (bf16[64,3072]{1,0:T(8,128)(2,1)}, bf16[64,3072]{1,0:T(8,128)(2,1)S(1)}, u32[]{:S(2)}, u32[]{:S(2)}) collective-permute-start(bf16[64,3072]{1,0:T(8,128)(2,1)} %get-tuple-element.23), channel_id=1, source_target_pairs={{0,2},{1,3},{2,0},{3,1},{4,6},{5,7},{6,4},{7,5},{8,10},{9,11},{10,... | collective-permute-start | bytes 1179656 | tf_op jit(solution)/shard_map/ppermute | solution.py:259
  17.2 0.7 slice.17
  18.1 5.4 %collective-permute-done.refs_1_.refs_0_ = bf16[64,1280]{1,0:T(8,128)(2,1)S(1)} collective-permute-done((bf16[64,1280]{1,0:T(8,128)(2,1)}, bf16[64,1280]{1,0:T(8,128)(2,1)S(1)}, u32[]{:S(2)}, u32[]{:S(2)}) %collective-permute-start) | collective-permute-done | bytes 163872 | tf_op jit(solution)/shard_map/ppermute | solution.py:259
  23.5 0.8 collective-permute-done.1.refs_2_.refs_1_
  24.3 1.0 %copy-done.2 = bf16[64,4352]{1,0:T(8,128)(2,1)S(1)} copy-done((bf16[64,4352]{1,0:T(8,128)(2,1)S(1)}, bf16[64,4352]{1,0:T(8,128)(2,1)}, u32[]{:S(2)}) %copy-start.2) | copy-done | bytes 557080
  25.4 1.4 %shard_map.93.refs_7_ = f32[8,64,2048]{2,1,0:T(8,128)S(1)} custom-call(s32[1]{0:T(128)} %bitcast.1.me_ref, s32[2,128]{1,0:T(2,128)S(1)} %convert_convert_fusion.1.tgt_ref, bf16[64,4352]{1,0:T(8,128)(2,1)S(1)} %collective-permute-done.2.refs_0_.refs_3_, bf16[64,4352]{1,0:T(8,128)(2,1)S(1)} %copy-done.2), custom_call_target="tpu_custom_call" | custom-call | flops 68719476736 | bytes 16777216 | tf_op jit(solution)/shard_map/pallas_call | solution.py:127
  26.8 0.8 copy-done
  27.6 0.7 copy-done.1
  28.3 4.1 %shard_map.94.far_ref = f32[8,64,2048]{2,1,0:T(8,128)S(1)} custom-call(s32[1]{0:T(128)} %bitcast.1.me_ref, s32[512]{0:T(512)S(1)} %reshape_squeeze.3.node_ref, bf16[64,4352]{1,0:T(8,128)(2,1)S(1)} %copy-done.2, bf16[64,1280]{1,0:T(8,128)(2,1)S(1)} %collective-permute-done.refs_1_.refs_0_, ...), custom_call_target="tpu_custom_call", output_to_operand_aliasing={{}: (9, {})} | custom-call | tf_op jit(solution)/shard_map/pallas_call | solution.py:182
  32.4 0.4 collective-permute-done.4.refs_3_
  32.7 1.2 %shard_map.95 = (f32[8,64,2048]{2,1,0:T(8,128)S(1)}, bf16[4,64,2048]{2,1,0:T(8,128)(2,1)S(1)}) custom-call(s32[1]{0:T(128)} %bitcast.1.me_ref, s32[1]{0:T(128)} %bitcast.2.core_ref, s32[4,128]{1,0:T(4,128)S(1)} %convert_convert_fusion.tgt_ref, f32[8,64,2048]{2,1,0:T(8,128)S(1)} %shard_map.94.far_ref, ...), custom_call_target="tpu_custom_call", output_to_operand_aliasing={{0}: (3, {})} | custom-call | tf_op jit(solution)/shard_map/pallas_call | solution.py:206
  34.0 1.7 %collective-permute-start.5 = (bf16[4,64,2048]{2,1,0:T(8,128)(2,1)S(1)}, bf16[4,64,2048]{2,1,0:T(8,128)(2,1)S(1)}, u32[]{:S(2)}, u32[]{:S(2)}) collective-permute-start(bf16[4,64,2048]{2,1,0:T(8,128)(2,1)S(1)} %get-tuple-element.25), channel_id=1, source_target_pairs={{0,4},{4,0},{8,12},{12,8},{16,20},{20,16},{24,28},{28,24},{1,5},{5... | collective-permute-start | bytes 3145736 | tf_op jit(solution)/shard_map/ppermute | solution.py:259
  35.6 2.3 %collective-permute-done.5.got_ref = bf16[4,64,2048]{2,1,0:T(8,128)(2,1)S(1)} collective-permute-done((bf16[4,64,2048]{2,1,0:T(8,128)(2,1)S(1)}, bf16[4,64,2048]{2,1,0:T(8,128)(2,1)S(1)}, u32[]{:S(2)}, u32[]{:S(2)}) %collective-permute-start.5) | collective-permute-done | bytes 1048608 | tf_op jit(solution)/shard_map/ppermute | solution.py:259
  38.1 1.4 %collective-permute-start.6 = (bf16[64,2048]{1,0:T(8,128)(2,1)S(1)}, bf16[64,2048]{1,0:T(8,128)(2,1)S(1)}, u32[]{:S(2)}, u32[]{:S(2)}) collective-permute-start(bf16[64,2048]{1,0:T(8,128)(2,1)S(1)} %get-tuple-element.28), channel_id=1, source_target_pairs={{0,8},{4,12},{8,0},{12,4},{16,24},{20,28},{24,16},{28,20},{1,9},{5... | collective-permute-start | bytes 786440 | tf_op jit(solution)/shard_map/ppermute | solution.py:259
  39.5 6.2 %collective-permute-done.6 = bf16[64,2048]{1,0:T(8,128)(2,1)S(1)} collective-permute-done((bf16[64,2048]{1,0:T(8,128)(2,1)S(1)}, bf16[64,2048]{1,0:T(8,128)(2,1)S(1)}, u32[]{:S(2)}, u32[]{:S(2)}) %collective-permute-start.6) | collective-permute-done | bytes 262176 | tf_op jit(solution)/shard_map/ppermute | solution.py:259
  45.7 1.4 %collective-permute-start.8 = (bf16[64,2048]{1,0:T(8,128)(2,1)S(1)}, bf16[64,2048]{1,0:T(8,128)(2,1)S(1)}, u32[]{:S(2)}, u32[]{:S(2)}) collective-permute-start(bf16[64,2048]{1,0:T(8,128)(2,1)S(1)} %get-tuple-element.30), channel_id=1, source_target_pairs={{0,8},{4,12},{8,0},{12,4},{16,24},{20,28},{24,16},{28,20},{1,9},{5... | collective-permute-start | bytes 786440 | tf_op jit(solution)/shard_map/ppermute | solution.py:259
  47.1 2.3 %collective-permute-start.7 = (bf16[64,2048]{1,0:T(8,128)(2,1)S(1)}, bf16[64,2048]{1,0:T(8,128)(2,1)S(1)}, u32[]{:S(2)}, u32[]{:S(2)}) collective-permute-start(bf16[64,2048]{1,0:T(8,128)(2,1)S(1)} %add_convert_fusion.1), channel_id=1, source_target_pairs={{0,16},{4,20},{8,24},{12,28},{16,0},{20,4},{24,8},{28,12},{1,17},{... | collective-permute-start | bytes 786440 | tf_op jit(solution)/shard_map/ppermute | solution.py:259
  49.4 8.3 %collective-permute-done.8 = bf16[64,2048]{1,0:T(8,128)(2,1)S(1)} collective-permute-done((bf16[64,2048]{1,0:T(8,128)(2,1)S(1)}, bf16[64,2048]{1,0:T(8,128)(2,1)S(1)}, u32[]{:S(2)}, u32[]{:S(2)}) %collective-permute-start.8) | collective-permute-done | bytes 262176 | tf_op jit(solution)/shard_map/ppermute | solution.py:259
  57.8 2.6 %collective-permute-start.10 = (bf16[64,2048]{1,0:T(8,128)(2,1)S(1)}, bf16[64,2048]{1,0:T(8,128)(2,1)S(1)}, u32[]{:S(2)}, u32[]{:S(2)}) collective-permute-start(bf16[64,2048]{1,0:T(8,128)(2,1)S(1)} %add_convert_fusion.refs_0_), channel_id=1, source_target_pairs={{0,16},{4,20},{8,24},{12,28},{16,0},{20,4},{24,8},{28,12},{1,17},{... | collective-permute-start | bytes 786440 | tf_op jit(solution)/shard_map/ppermute | solution.py:259
  60.4 0.6 collective-permute-start.9
  61.0 9.2 %collective-permute-done.10.refs_2_ = bf16[64,2048]{1,0:T(8,128)(2,1)S(1)} collective-permute-done((bf16[64,2048]{1,0:T(8,128)(2,1)S(1)}, bf16[64,2048]{1,0:T(8,128)(2,1)S(1)}, u32[]{:S(2)}, u32[]{:S(2)}) %collective-permute-start.10) | collective-permute-done | bytes 262176 | tf_op jit(solution)/shard_map/ppermute | solution.py:259
  70.2 1.5 %collective-permute-start.11 = (bf16[64,2048]{1,0:T(8,128)(2,1)S(1)}, bf16[64,2048]{1,0:T(8,128)(2,1)S(1)}, u32[]{:S(2)}, u32[]{:S(2)}) collective-permute-start(bf16[64,2048]{1,0:T(8,128)(2,1)S(1)} %collective-permute-done.10.refs_2_), channel_id=1, source_target_pairs={{0,8},{4,12},{8,0},{12,4},{16,24},{20,28},{24,16},{28,20},{1,9},{5... | collective-permute-start | bytes 786440 | tf_op jit(solution)/shard_map/ppermute | solution.py:259
  71.7 1.9 %collective-permute-start.12 = (bf16[64,2048]{1,0:T(8,128)(2,1)S(1)}, bf16[64,2048]{1,0:T(8,128)(2,1)S(1)}, u32[]{:S(2)}, u32[]{:S(2)}) collective-permute-start(bf16[64,2048]{1,0:T(8,128)(2,1)S(1)} %add_convert_fusion.refs_0_), channel_id=1, source_target_pairs={{0,4},{4,0},{8,12},{12,8},{16,20},{20,16},{24,28},{28,24},{1,5},{5... | collective-permute-start | bytes 786440 | tf_op jit(solution)/shard_map/ppermute | solution.py:259
  73.7 0.5 collective-permute-start.13
  74.2 1.6 %collective-permute-done.11.refs_3_ = bf16[64,2048]{1,0:T(8,128)(2,1)S(1)} collective-permute-done((bf16[64,2048]{1,0:T(8,128)(2,1)S(1)}, bf16[64,2048]{1,0:T(8,128)(2,1)S(1)}, u32[]{:S(2)}, u32[]{:S(2)}) %collective-permute-start.11) | collective-permute-done | bytes 262176 | tf_op jit(solution)/shard_map/ppermute | solution.py:259
  75.7 4.3 %collective-permute-start.15 = (bf16[64,2048]{1,0:T(8,128)(2,1)S(1)}, bf16[64,2048]{1,0:T(8,128)(2,1)S(1)}, u32[]{:S(2)}, u32[]{:S(2)}) collective-permute-start(bf16[64,2048]{1,0:T(8,128)(2,1)S(1)} %collective-permute-done.11.refs_3_), channel_id=1, source_target_pairs={{0,4},{4,0},{8,12},{12,8},{16,20},{20,16},{24,28},{28,24},{1,5},{5... | collective-permute-start | bytes 786440 | tf_op jit(solution)/shard_map/ppermute | solution.py:259
  80.0 1.1 %collective-permute-done.15.refs_7_ = bf16[64,2048]{1,0:T(8,128)(2,1)S(1)} collective-permute-done((bf16[64,2048]{1,0:T(8,128)(2,1)S(1)}, bf16[64,2048]{1,0:T(8,128)(2,1)S(1)}, u32[]{:S(2)}, u32[]{:S(2)}) %collective-permute-start.15) | collective-permute-done | bytes 262176 | tf_op jit(solution)/shard_map/ppermute | solution.py:259
  81.2 1.5 %shard_map.97 = bf16[64,16384]{1,0:T(8,128)(2,1)} custom-call(s32[1]{0:T(128)} %bitcast.me_ref, bf16[64,2048]{1,0:T(8,128)(2,1)S(1)} %add_convert_fusion.refs_0_, bf16[64,2048]{1,0:T(8,128)(2,1)S(1)} %collective-permute-done.9.refs_1_, bf16[64,2048]{1,0:T(8,128)(2,1)S(1)} %collective-permute-done.10.refs_2_, ...), custom_call_target="tpu_custom_call" | custom-call | tf_op jit(solution)/shard_map/pallas_call | solution.py:248
  (27 shorter events, 0.9 us)
Async XLA Ops:
  0.0 17.9 %copy-start.4 = (s32[1,128,4]{1,2,0:T(4,128)S(1)}, s32[1,128,4]{1,2,0:T(4,128)}, u32[]{:S(2)}) copy-start(s32[1,128,4]{1,2,0:T(4,128)} %param.16) | copy-start | bytes 6148
  4.4 19.9 %collective-permute-start.2 = (bf16[64,4352]{1,0:T(8,128)(2,1)}, bf16[64,4352]{1,0:T(8,128)(2,1)S(1)}, u32[]{:S(2)}, u32[]{:S(2)}) collective-permute-start(bf16[64,4352]{1,0:T(8,128)(2,1)} %shard_map.91), channel_id=1, source_target_pairs={{0,3},{1,2},{2,1},{3,0},{4,7},{5,6},{6,5},{7,4},{8,11},{9,10},{10,... | collective-permute-start | bytes 1671176 | tf_op jit(solution)/shard_map/ppermute | solution.py:259
  14.2 9.3 %collective-permute-start = (bf16[64,1280]{1,0:T(8,128)(2,1)}, bf16[64,1280]{1,0:T(8,128)(2,1)S(1)}, u32[]{:S(2)}, u32[]{:S(2)}) collective-permute-start(bf16[64,1280]{1,0:T(8,128)(2,1)} %get-tuple-element.19), channel_id=1, source_target_pairs={{0,1},{1,0},{2,3},{3,2},{4,5},{5,4},{6,7},{7,6},{8,9},{9,8},{10,11... | collective-permute-start | bytes 491528 | tf_op jit(solution)/shard_map/ppermute | solution.py:259
  14.5 9.8 %collective-permute-start.1 = (bf16[64,1280]{1,0:T(8,128)(2,1)}, bf16[64,1280]{1,0:T(8,128)(2,1)S(1)}, u32[]{:S(2)}, u32[]{:S(2)}) collective-permute-start(bf16[64,1280]{1,0:T(8,128)(2,1)} %get-tuple-element.20), channel_id=1, source_target_pairs={{0,2},{1,3},{2,0},{3,1},{4,6},{5,7},{6,4},{7,5},{8,10},{9,11},{10,... | collective-permute-start | bytes 491528 | tf_op jit(solution)/shard_map/ppermute | solution.py:259
  14.6 17.8 %collective-permute-start.3 = (bf16[64,3072]{1,0:T(8,128)(2,1)}, bf16[64,3072]{1,0:T(8,128)(2,1)S(1)}, u32[]{:S(2)}, u32[]{:S(2)}) collective-permute-start(bf16[64,3072]{1,0:T(8,128)(2,1)} %get-tuple-element.22), channel_id=1, source_target_pairs={{0,1},{1,0},{2,3},{3,2},{4,5},{5,4},{6,7},{7,6},{8,9},{9,8},{10,11... | collective-permute-start | bytes 1179656 | tf_op jit(solution)/shard_map/ppermute | solution.py:259
  16.0 16.7 %collective-permute-start.4 = (bf16[64,3072]{1,0:T(8,128)(2,1)}, bf16[64,3072]{1,0:T(8,128)(2,1)S(1)}, u32[]{:S(2)}, u32[]{:S(2)}) collective-permute-start(bf16[64,3072]{1,0:T(8,128)(2,1)} %get-tuple-element.23), channel_id=1, source_target_pairs={{0,2},{1,3},{2,0},{3,1},{4,6},{5,7},{6,4},{7,5},{8,10},{9,11},{10,... | collective-permute-start | bytes 1179656 | tf_op jit(solution)/shard_map/ppermute | solution.py:259
  24.3 1.1 %copy-start.2 = (bf16[64,4352]{1,0:T(8,128)(2,1)S(1)}, bf16[64,4352]{1,0:T(8,128)(2,1)}, u32[]{:S(2)}) copy-start(bf16[64,4352]{1,0:T(8,128)(2,1)} %get-tuple-element.21.refs_1_.refs_0_) | copy-start | bytes 1671172
  25.4 2.2 %copy-start = (bf16[1,128,64,256]{3,2,1,0:T(8,128)(2,1)S(1)}, bf16[1,128,64,256]{3,2,1,0:T(8,128)(2,1)}, u32[]{:S(2)}) copy-start(bf16[1,128,64,256]{3,2,1,0:T(8,128)(2,1)} %param.15) | copy-start | bytes 12582916
  25.4 2.9 %copy-start.1 = (bf16[128,64,128]{2,1,0:T(8,128)(2,1)S(1)}, bf16[128,64,128]{2,1,0:T(8,128)(2,1)}, u32[]{:S(2)}) copy-start(bf16[128,64,128]{2,1,0:T(8,128)(2,1)} %refs_6_.1) | copy-start | bytes 6291460
  25.4 2.9 %copy-start.3 = (f32[1,3,64,128]{3,2,1,0:T(8,128)S(1)}, f32[1,3,64,128]{3,2,1,0:T(8,128)}, u32[]{:S(2)}) copy-start(f32[1,3,64,128]{3,2,1,0:T(8,128)} %param.14) | copy-start | bytes 294916
  34.0 4.0 %collective-permute-start.5 = (bf16[4,64,2048]{2,1,0:T(8,128)(2,1)S(1)}, bf16[4,64,2048]{2,1,0:T(8,128)(2,1)S(1)}, u32[]{:S(2)}, u32[]{:S(2)}) collective-permute-start(bf16[4,64,2048]{2,1,0:T(8,128)(2,1)S(1)} %get-tuple-element.25), channel_id=1, source_target_pairs={{0,4},{4,0},{8,12},{12,8},{16,20},{20,16},{24,28},{28,24},{1,5},{5... | collective-permute-start | bytes 3145736 | tf_op jit(solution)/shard_map/ppermute | solution.py:259
  38.1 7.6 %collective-permute-start.6 = (bf16[64,2048]{1,0:T(8,128)(2,1)S(1)}, bf16[64,2048]{1,0:T(8,128)(2,1)S(1)}, u32[]{:S(2)}, u32[]{:S(2)}) collective-permute-start(bf16[64,2048]{1,0:T(8,128)(2,1)S(1)} %get-tuple-element.28), channel_id=1, source_target_pairs={{0,8},{4,12},{8,0},{12,4},{16,24},{20,28},{24,16},{28,20},{1,9},{5... | collective-permute-start | bytes 786440 | tf_op jit(solution)/shard_map/ppermute | solution.py:259
  45.7 12.0 %collective-permute-start.8 = (bf16[64,2048]{1,0:T(8,128)(2,1)S(1)}, bf16[64,2048]{1,0:T(8,128)(2,1)S(1)}, u32[]{:S(2)}, u32[]{:S(2)}) collective-permute-start(bf16[64,2048]{1,0:T(8,128)(2,1)S(1)} %get-tuple-element.30), channel_id=1, source_target_pairs={{0,8},{4,12},{8,0},{12,4},{16,24},{20,28},{24,16},{28,20},{1,9},{5... | collective-permute-start | bytes 786440 | tf_op jit(solution)/shard_map/ppermute | solution.py:259
  47.1 10.6 %collective-permute-start.7 = (bf16[64,2048]{1,0:T(8,128)(2,1)S(1)}, bf16[64,2048]{1,0:T(8,128)(2,1)S(1)}, u32[]{:S(2)}, u32[]{:S(2)}) collective-permute-start(bf16[64,2048]{1,0:T(8,128)(2,1)S(1)} %add_convert_fusion.1), channel_id=1, source_target_pairs={{0,16},{4,20},{8,24},{12,28},{16,0},{20,4},{24,8},{28,12},{1,17},{... | collective-permute-start | bytes 786440 | tf_op jit(solution)/shard_map/ppermute | solution.py:259
  57.8 12.4 %collective-permute-start.10 = (bf16[64,2048]{1,0:T(8,128)(2,1)S(1)}, bf16[64,2048]{1,0:T(8,128)(2,1)S(1)}, u32[]{:S(2)}, u32[]{:S(2)}) collective-permute-start(bf16[64,2048]{1,0:T(8,128)(2,1)S(1)} %add_convert_fusion.refs_0_), channel_id=1, source_target_pairs={{0,16},{4,20},{8,24},{12,28},{16,0},{20,4},{24,8},{28,12},{1,17},{... | collective-permute-start | bytes 786440 | tf_op jit(solution)/shard_map/ppermute | solution.py:259
  60.4 13.2 %collective-permute-start.9 = (bf16[64,2048]{1,0:T(8,128)(2,1)S(1)}, bf16[64,2048]{1,0:T(8,128)(2,1)S(1)}, u32[]{:S(2)}, u32[]{:S(2)}) collective-permute-start(bf16[64,2048]{1,0:T(8,128)(2,1)S(1)} %add_convert_fusion.refs_0_), channel_id=1, source_target_pairs={{0,8},{4,12},{8,0},{12,4},{16,24},{20,28},{24,16},{28,20},{1,9},{5... | collective-permute-start | bytes 786440 | tf_op jit(solution)/shard_map/ppermute | solution.py:259
  70.2 5.5 %collective-permute-start.11 = (bf16[64,2048]{1,0:T(8,128)(2,1)S(1)}, bf16[64,2048]{1,0:T(8,128)(2,1)S(1)}, u32[]{:S(2)}, u32[]{:S(2)}) collective-permute-start(bf16[64,2048]{1,0:T(8,128)(2,1)S(1)} %collective-permute-done.10.refs_2_), channel_id=1, source_target_pairs={{0,8},{4,12},{8,0},{12,4},{16,24},{20,28},{24,16},{28,20},{1,9},{5... | collective-permute-start | bytes 786440 | tf_op jit(solution)/shard_map/ppermute | solution.py:259
  71.7 8.3 %collective-permute-start.12 = (bf16[64,2048]{1,0:T(8,128)(2,1)S(1)}, bf16[64,2048]{1,0:T(8,128)(2,1)S(1)}, u32[]{:S(2)}, u32[]{:S(2)}) collective-permute-start(bf16[64,2048]{1,0:T(8,128)(2,1)S(1)} %add_convert_fusion.refs_0_), channel_id=1, source_target_pairs={{0,4},{4,0},{8,12},{12,8},{16,20},{20,16},{24,28},{28,24},{1,5},{5... | collective-permute-start | bytes 786440 | tf_op jit(solution)/shard_map/ppermute | solution.py:259
  73.6 6.4 %collective-permute-start.14 = (bf16[64,2048]{1,0:T(8,128)(2,1)S(1)}, bf16[64,2048]{1,0:T(8,128)(2,1)S(1)}, u32[]{:S(2)}, u32[]{:S(2)}) collective-permute-start(bf16[64,2048]{1,0:T(8,128)(2,1)S(1)} %collective-permute-done.10.refs_2_), channel_id=1, source_target_pairs={{0,4},{4,0},{8,12},{12,8},{16,20},{20,16},{24,28},{28,24},{1,5},{5... | collective-permute-start | bytes 786440 | tf_op jit(solution)/shard_map/ppermute | solution.py:259
  73.7 6.4 %collective-permute-start.13 = (bf16[64,2048]{1,0:T(8,128)(2,1)S(1)}, bf16[64,2048]{1,0:T(8,128)(2,1)S(1)}, u32[]{:S(2)}, u32[]{:S(2)}) collective-permute-start(bf16[64,2048]{1,0:T(8,128)(2,1)S(1)} %collective-permute-done.9.refs_1_), channel_id=1, source_target_pairs={{0,4},{4,0},{8,12},{12,8},{16,20},{20,16},{24,28},{28,24},{1,5},{5... | collective-permute-start | bytes 786440 | tf_op jit(solution)/shard_map/ppermute | solution.py:259
  75.7 5.4 %collective-permute-start.15 = (bf16[64,2048]{1,0:T(8,128)(2,1)S(1)}, bf16[64,2048]{1,0:T(8,128)(2,1)S(1)}, u32[]{:S(2)}, u32[]{:S(2)}) collective-permute-start(bf16[64,2048]{1,0:T(8,128)(2,1)S(1)} %collective-permute-done.11.refs_3_), channel_id=1, source_target_pairs={{0,4},{4,0},{8,12},{12,8},{16,20},{20,16},{24,28},{28,24},{1,5},{5... | collective-permute-start | bytes 786440 | tf_op jit(solution)/shard_map/ppermute | solution.py:259

commit v4 on v3

--- a/solution.py
+++ b/solution.py
@@ -194,41 +194,43 @@
     )(me, far_node, *heads, transfer, coupling, target_basis, near)
 
 
-def gather_kernel(parts, tile, me_ref, core_ref, tgt_ref, far_ref, *refs):
-    got_refs, (acc, send_ref) = refs[:-2], refs[-2:]
+def gather_kernel(parts, tile, me_ref, tgt_ref, far_ref, *refs):
+    got_refs, (acc, first_ref, rest_ref) = refs[:-3], refs[-3:]
     add_products(acc, tgt_ref, me_ref[0], parts, got_refs, tile)
-    for z in range(send_ref.shape[0]):
-        send_ref[z] = acc[2 * z + 1 - core_ref[0]].astype(BF16)
-
-
-def gather_near(parts, me, core, tgt, far, got, tile):
+    z, core = me_ref[1] // 2, me_ref[1] % 2
+    chips = acc.shape[0] // 2
+    for n in range(chips):
+        m = chips - 1 - 2 * n if n < chips // 2 else 2 * (chips - 1 - n)
+        out = first_ref.at[n] if n < chips // 2 else rest_ref.at[n - chips // 2]
+        out[...] = acc[2 * (z ^ m) + 1 - core].astype(BF16)
+
+
+def gather_near(parts, me, tgt, far, got, tile):
     pieces, rows, width = far.shape
     return pl.pallas_call(
         functools.partial(gather_kernel, parts, tile),
         out_shape=[
             jax.ShapeDtypeStruct(far.shape, F32),
-            jax.ShapeDtypeStruct((pieces // 2, rows, width), BF16),
+            jax.ShapeDtypeStruct((pieces // 4, rows, width), BF16),
+            jax.ShapeDtypeStruct((pieces // 4, rows, width), BF16),
         ],
-        in_specs=[SMEM] * 3 + [VMEM] * (1 + len(got)),
-        out_specs=[VMEM, VMEM],
-        input_output_aliases={3: 0},
-        compiler_params=pltpu.CompilerParams(vmem_limit_bytes=16 * 2**20),
-    )(me, core, tgt, far, *got)
+        in_specs=[SMEM] * 2 + [VMEM] * (1 + len(got)),
+        out_specs=[VMEM] * 3,
+        input_output_aliases={2: 0},
+        compiler_params=pltpu.CompilerParams(vmem_limit_bytes=16 * 2**20),
+    )(me, tgt, far, *got)
 
 
 def split_kernel(masks, me_ref, acc_ref, got_ref, *out_refs):
     z, core = me_ref[0] // 2, me_ref[0] % 2
-    for m, out_ref in zip(masks, out_refs):
-        piece = z ^ m
-        out_ref[...] = (acc_ref[2 * piece + core] + got_ref[piece].astype(F32)).astype(
-            out_ref.dtype
-        )
+    for n, (m, out_ref) in enumerate(zip(masks, out_refs)):
+        out_ref[...] = (acc_ref[2 * (z ^ m) + core] + got_ref[n].astype(F32)).astype(out_ref.dtype)
 
 
 def split(masks, dtypes, me, acc, got):
     return pl.pallas_call(
         functools.partial(split_kernel, masks),
-        out_shape=[jax.ShapeDtypeStruct(got.shape[1:], d) for d in dtypes],
+        out_shape=[jax.ShapeDtypeStruct(got.shape[-2:], d) for d in dtypes],
         in_specs=[SMEM, VMEM, VMEM],
         out_specs=[VMEM] * len(masks),
         compiler_params=pltpu.CompilerParams(vmem_limit_bytes=16 * 2**20),
@@ -236,22 +238,30 @@
 
 
 def place_kernel(masks, me_ref, *refs):
-    out_ref = refs[-1]
-    for m, piece_ref in zip(masks, refs):
+    piece_refs, (out_ref, sems) = refs[: len(masks)], refs[-2:]
+    copies = []
+    for n, (m, piece_ref) in enumerate(zip(masks, piece_refs)):
         width = piece_ref.shape[1]
         spot = pl.ds(pl.multiple_of((me_ref[0] ^ m) * width, width), width)
-        out_ref[:, spot] = piece_ref[...]
-
-
-def place(masks, me, parts):
+        copies.append(pltpu.make_async_copy(piece_ref, out_ref.at[:, spot], sems.at[n]))
+    for copy in copies:
+        copy.start()
+    for copy in copies:
+        copy.wait()
+
+
+def place(masks, me, parts, count, out=None):
     rows, width = parts[0].shape
     return pl.pallas_call(
         functools.partial(place_kernel, masks),
-        out_shape=jax.ShapeDtypeStruct((rows, width * len(parts)), BF16),
-        in_specs=[SMEM] + [VMEM] * len(parts),
-        out_specs=VMEM,
-        compiler_params=pltpu.CompilerParams(vmem_limit_bytes=16 * 2**20),
-    )(me, *parts)
+        out_shape=jax.ShapeDtypeStruct((rows, width * count), BF16),
+        in_specs=[SMEM] + [VMEM] * len(parts) + [ANY] * (out is not None),
+        out_specs=ANY,
+        scratch_shapes=[pltpu.SemaphoreType.DMA((len(parts),))],
+        input_output_aliases={} if out is None else {len(parts) + 1: 0},
+        cost_estimate=LONG if out is None else None,
+        compiler_params=pltpu.CompilerParams(vmem_limit_bytes=16 * 2**20),
+    )(me, *parts, *(() if out is None else (out,)))
 
 
 def swap(value, axis, mask):
@@ -263,23 +273,24 @@
     return lax.optimization_barrier((value,) + others)[0]
 
 
-def sum_and_share(me, acc, got):
+def sum_and_share(me, acc, got_first, got_rest):
     chips = acc.shape[0] // 2
     if chips == 4:
-        masks = (3, 2, 1, 0)
-        first, cross, near, own = split(masks, (BF16, F32, BF16, F32), me, acc, got)
+        first, near = split((3, 1), (BF16, BF16), me, acc, got_first)
+        cross, own = split((2, 0), (F32, F32), me, acc, got_rest)
         a = swap(first, "src", 2)
         cross = (cross + a.astype(F32)).astype(BF16)
         b = swap(cross, "src", 4)
-        c = swap(tied(near, cross), "src", 2)
+        c = swap(near, "src", 2)
         own = (own + b.astype(F32) + c.astype(F32)).astype(BF16)
         d = swap(own, "src", 4)
         e = swap(own, "src", 2)
         return (0, 1, 2, 3), [own, e, d, swap(d, "src", 2)]
     masks = tuple(range(chips))
-    dtypes = (F32,) + (BF16,) * (chips - 1)
-    own, *rest = split(masks, dtypes, me, acc, got)
-    for m, part in zip(masks[1:], rest):
+    odd, even = masks[::-2], masks[-2::-2]
+    first = split(odd, (BF16,) * len(odd), me, acc, got_first)
+    *rest, own = split(even, (BF16,) * (len(even) - 1) + (F32,), me, acc, got_rest)
+    for m, part in zip(odd + even[:-1], [*first, *rest]):
         own = own + swap(part, "src", 2 * m).astype(F32)
     own = own.astype(BF16)
     return masks, [own] + [swap(own, "src", 2 * m) for m in masks[1:]]
@@ -295,7 +306,7 @@
     count, tile, _ = near_tiles.shape
     slots = count // groups
     x = charges.T
-    me, core = me_t.reshape(1), (me_s % 2).reshape(1)
+    me = me_t.reshape(1)
 
     masks = sorted(range(groups), key=lambda m: -bin(m).count("1"))
     ends = [min(FIRST_HEAD, slots)] + [min(HEAD, slots)] * (groups - 2) + [slots]
@@ -337,13 +348,23 @@
         acc,
         count,
     )
-    acc, send = gather_near(
-        late, me, core, targets(late), acc, [got[part] for part in late], tile
-    )
-    owners, mine = sum_and_share(me_s.reshape(1), acc, swap(send, "src", 1))
+    here = jnp.stack([me_t, me_s])
+    acc, first, rest = gather_near(
+        late, here, targets(late), acc, [got[part] for part in late], tile
+    )
+    owners, mine = sum_and_share(
+        me_s.reshape(1), acc, swap(first, "src", 1), swap(rest, "src", 1)
+    )
     other = [swap(p, "src", 1) for p in mine]
-    spots = [2 * m for m in owners] + [2 * m + 1 for m in owners]
-    return place(spots, me_s.reshape(1), mine + other).T
+    parts = [(2 * m, q) for m, q in zip(owners, mine)]
+    parts += [(2 * m + 1, q) for m, q in zip(owners, other)]
+    early = [part for part in parts if part[0] // 2 != owners[-1]]
+    late = [part for part in parts if part[0] // 2 == owners[-1]]
+    out = None
+    for some in (early, late):
+        spots, values = zip(*some)
+        out = place(spots, me_s.reshape(1), values, sources, out)
+    return out.T
 
 
 def solution(mesh):

time: 83.2 us -> 81.4 us (0.978)
  waiting for transfers between devices: 35.2 us -> 26.7 us
  starting transfers between devices: 24.2 us -> 29.6 us
    ppermute x16 -> x17, waiting for transfers between devices: 35.2 us -> 26.7 us  [swap(): return lax.ppermute(value, axis, [(i, i ^ mask) for i in range(size)])]
    ppermute x16 -> x17, starting transfers between devices: 24.2 us -> 29.6 us  [swap(): return lax.ppermute(value, axis, [(i, i ^ mask) for i in range(size)])]
    pallas_call x1 -> x2, Pallas kernels: 1.46 us -> 2 us  [place(): pl.pallas_call(functools.partial(place_kernel, masks), out_shape=jax.Shap...]
  transfers between devices with their start and end apart: 16 -> 17, of which waited for: 9 -> 8; matrix products, arithmetic and copies ran while one was open for 1% -> 1% of each run, Pallas kernels for 15% -> 17%
where the time goes in v4:
time: 81.4 us; the launch traced here: 80.3 us
  starting transfers between devices  29.6 us (36%)
  waiting for transfers between devices  26.7 us (33%)
  Pallas kernels  20.2 us (25%)
  local copies, waits for them, and re-layouts  3.44 us (4%)
    ppermute x17, starting transfers between devices, swap(): return lax.ppermute(value, axis, [(i, i ^ mask) for i in range(size)])  29.6 us
    ppermute x17, waiting for transfers between devices, swap(): return lax.ppermute(value, axis, [(i, i ^ mask) for i in range(size)])  26.7 us
    pallas_call x2, Pallas kernels, near_products(): pl.pallas_call(functools.partial(near_kernel, parts), out_shape=[jax.Shap...  11.1 us
    pallas_call x1, Pallas kernels, far_field(): pl.pallas_call(functools.partial(far_kernel, groups, count), out_shape=ja...  4.16 us
    unnamed x11, local copies, waits for them, and re-layouts  2.64 us
    pallas_call x2, Pallas kernels, place(): pl.pallas_call(functools.partial(place_kernel, masks), out_shape=jax.Shap...  2 us
  transfers between devices with their start and end apart: 17, of which 8 were waited for; matrix products, arithmetic and copies ran while one was open for 1% of the time, Pallas kernels for 17%

profile of v4, /device:TPU:1, one launch (start us, length us, event | category | flops | bytes accessed | tf_op | source)
XLA Modules:
  0.0 80.3 jit_solution(16601685556772303375)
XLA Ops:
  0.0 4.4 %shard_map.91 = bf16[64,4352]{1,0:T(8,128)(2,1)} custom-call(s32[1]{0:T(128)} %bitcast.1.me_ref, s32[128]{0:T(128)} %src_ref.3, s32[1,128]{1,0:T(1,128)} %bitcast.11, bf16[64,2048]{1,0:T(8,128)(2,1)} %bitcast.9, bf16[16,64,128]{2,1,0:T(8,128)(2,1)} %basis_ref.3, bf16[128,128,128]{2,1,0:T(8,128)(2,1)} %tiles_ref.3), custom_call_target="tpu_custom_call" | custom-call | tf_op jit(solution)/shard_map/pallas_call | solution.py:93
  4.4 3.1 %collective-permute-start.2 = (bf16[64,4352]{1,0:T(8,128)(2,1)}, bf16[64,4352]{1,0:T(8,128)(2,1)S(1)}, u32[]{:S(2)}, u32[]{:S(2)}) collective-permute-start(bf16[64,4352]{1,0:T(8,128)(2,1)} %shard_map.91), channel_id=1, source_target_pairs={{0,3},{1,2},{2,1},{3,0},{4,7},{5,6},{6,5},{7,4},{8,11},{9,10},{10,... | collective-permute-start | bytes 1671176 | tf_op jit(solution)/shard_map/ppermute | solution.py:269
  7.5 6.7 %shard_map.92 = (bf16[64,1280]{1,0:T(8,128)(2,1)}, bf16[64,1280]{1,0:T(8,128)(2,1)}, bf16[64,4352]{1,0:T(8,128)(2,1)}, bf16[64,3072]{1,0:T(8,128)(2,1)}, bf16[64,3072]{1,0:T(8,128)(2,1)}) custom-call(s32[1]{0:T(128)} %bitcast.1.me_ref, s32[128]{0:T(128)} %src_ref.3, s32[1,128]{1,0:T(1,128)} %bitcast.12, bf16[64,2048]{1,0:T(8,128)(2,1)} %bitcast.10, ...), custom_call_target="tpu_custom_call" | custom-call | tf_op jit(solution)/shard_map/pallas_call | solution.py:93
  14.2 0.3 collective-permute-start
  14.6 1.4 %collective-permute-start.3 = (bf16[64,3072]{1,0:T(8,128)(2,1)}, bf16[64,3072]{1,0:T(8,128)(2,1)S(1)}, u32[]{:S(2)}, u32[]{:S(2)}) collective-permute-start(bf16[64,3072]{1,0:T(8,128)(2,1)} %get-tuple-element.22), channel_id=1, source_target_pairs={{0,1},{1,0},{2,3},{3,2},{4,5},{5,4},{6,7},{7,6},{8,9},{9,8},{10,11... | collective-permute-start | bytes 1179656 | tf_op jit(solution)/shard_map/ppermute | solution.py:269
  16.0 1.2 %collective-permute-start.4 = (bf16[64,3072]{1,0:T(8,128)(2,1)}, bf16[64,3072]{1,0:T(8,128)(2,1)S(1)}, u32[]{:S(2)}, u32[]{:S(2)}) collective-permute-start(bf16[64,3072]{1,0:T(8,128)(2,1)} %get-tuple-element.23), channel_id=1, source_target_pairs={{0,2},{1,3},{2,0},{3,1},{4,6},{5,7},{6,4},{7,5},{8,10},{9,11},{10,... | collective-permute-start | bytes 1179656 | tf_op jit(solution)/shard_map/ppermute | solution.py:269
  17.2 0.7 slice.17
  18.2 5.3 %collective-permute-done.refs_1_.refs_0_ = bf16[64,1280]{1,0:T(8,128)(2,1)S(1)} collective-permute-done((bf16[64,1280]{1,0:T(8,128)(2,1)}, bf16[64,1280]{1,0:T(8,128)(2,1)S(1)}, u32[]{:S(2)}, u32[]{:S(2)}) %collective-permute-start) | collective-permute-done | bytes 163872 | tf_op jit(solution)/shard_map/ppermute | solution.py:269
  23.5 0.8 collective-permute-done.1.refs_2_.refs_1_
  24.4 1.0 %copy-done.2 = bf16[64,4352]{1,0:T(8,128)(2,1)S(1)} copy-done((bf16[64,4352]{1,0:T(8,128)(2,1)S(1)}, bf16[64,4352]{1,0:T(8,128)(2,1)}, u32[]{:S(2)}) %copy-start.2) | copy-done | bytes 557080
  25.4 1.4 %shard_map.93.refs_7_ = f32[8,64,2048]{2,1,0:T(8,128)S(1)} custom-call(s32[1]{0:T(128)} %bitcast.1.me_ref, s32[2,128]{1,0:T(2,128)S(1)} %convert_convert_fusion.1.tgt_ref, bf16[64,4352]{1,0:T(8,128)(2,1)S(1)} %collective-permute-done.2.refs_0_.refs_3_, bf16[64,4352]{1,0:T(8,128)(2,1)S(1)} %copy-done.2), custom_call_target="tpu_custom_call" | custom-call | flops 68719476736 | bytes 16777216 | tf_op jit(solution)/shard_map/pallas_call | solution.py:127
  26.8 0.8 copy-done
  27.6 0.7 copy-done.1
  28.3 4.2 %shard_map.94.far_ref = f32[8,64,2048]{2,1,0:T(8,128)S(1)} custom-call(s32[1]{0:T(128)} %bitcast.1.me_ref, s32[512]{0:T(512)S(1)} %reshape_squeeze.3.node_ref, bf16[64,4352]{1,0:T(8,128)(2,1)S(1)} %copy-done.2, bf16[64,1280]{1,0:T(8,128)(2,1)S(1)} %collective-permute-done.refs_1_.refs_0_, ...), custom_call_target="tpu_custom_call", output_to_operand_aliasing={{}: (9, {})} | custom-call | tf_op jit(solution)/shard_map/pallas_call | solution.py:182
  32.4 0.3 collective-permute-done.4.refs_3_
  32.7 1.3 %shard_map.95 = (f32[8,64,2048]{2,1,0:T(8,128)S(1)}, bf16[2,64,2048]{2,1,0:T(8,128)(2,1)S(1)}, bf16[2,64,2048]{2,1,0:T(8,128)(2,1)S(1)}) custom-call(s32[2]{0:T(128)S(1)} %pad_add_fusion.me_ref, s32[4,128]{1,0:T(4,128)S(1)} %convert_convert_fusion.tgt_ref, f32[8,64,2048]{2,1,0:T(8,128)S(1)} %shard_map.94.far_ref, ...), custom_call_target="tpu_custom_call", output_to_operand_aliasing={{0}: (2, {})} | custom-call | tf_op jit(solution)/shard_map/pallas_call | solution.py:210
  34.0 1.8 %collective-permute-start.6 = (bf16[2,64,2048]{2,1,0:T(8,128)(2,1)S(1)}, bf16[2,64,2048]{2,1,0:T(8,128)(2,1)S(1)}, u32[]{:S(2)}, u32[]{:S(2)}) collective-permute-start(bf16[2,64,2048]{2,1,0:T(8,128)(2,1)S(1)} %get-tuple-element.28), channel_id=1, source_target_pairs={{0,4},{4,0},{8,12},{12,8},{16,20},{20,16},{24,28},{28,24},{1,5},{5... | collective-permute-start | bytes 1572872 | tf_op jit(solution)/shard_map/ppermute | solution.py:269
  35.8 1.5 %collective-permute-done.6.got_ref = bf16[2,64,2048]{2,1,0:T(8,128)(2,1)S(1)} collective-permute-done((bf16[2,64,2048]{2,1,0:T(8,128)(2,1)S(1)}, bf16[2,64,2048]{2,1,0:T(8,128)(2,1)S(1)}, u32[]{:S(2)}, u32[]{:S(2)}) %collective-permute-start.6) | collective-permute-done | bytes 524320 | tf_op jit(solution)/shard_map/ppermute | solution.py:269
  37.4 1.4 %collective-permute-start.7 = (bf16[64,2048]{1,0:T(8,128)(2,1)S(1)}, bf16[64,2048]{1,0:T(8,128)(2,1)S(1)}, u32[]{:S(2)}, u32[]{:S(2)}) collective-permute-start(bf16[64,2048]{1,0:T(8,128)(2,1)S(1)} %get-tuple-element.29), channel_id=1, source_target_pairs={{0,8},{4,12},{8,0},{12,4},{16,24},{20,28},{24,16},{28,20},{1,9},{5... | collective-permute-start | bytes 786440 | tf_op jit(solution)/shard_map/ppermute | solution.py:269
  39.0 5.9 %collective-permute-done.7 = bf16[64,2048]{1,0:T(8,128)(2,1)S(1)} collective-permute-done((bf16[64,2048]{1,0:T(8,128)(2,1)S(1)}, bf16[64,2048]{1,0:T(8,128)(2,1)S(1)}, u32[]{:S(2)}, u32[]{:S(2)}) %collective-permute-start.7) | collective-permute-done | bytes 262176 | tf_op jit(solution)/shard_map/ppermute | solution.py:269
  45.0 2.4 %collective-permute-start.8 = (bf16[64,2048]{1,0:T(8,128)(2,1)S(1)}, bf16[64,2048]{1,0:T(8,128)(2,1)S(1)}, u32[]{:S(2)}, u32[]{:S(2)}) collective-permute-start(bf16[64,2048]{1,0:T(8,128)(2,1)S(1)} %add_convert_fusion.1), channel_id=1, source_target_pairs={{0,16},{4,20},{8,24},{12,28},{16,0},{20,4},{24,8},{28,12},{1,17},{... | collective-permute-start | bytes 786440 | tf_op jit(solution)/shard_map/ppermute | solution.py:269
  47.4 8.0 %collective-permute-done.9 = bf16[64,2048]{1,0:T(8,128)(2,1)S(1)} collective-permute-done((bf16[64,2048]{1,0:T(8,128)(2,1)S(1)}, bf16[64,2048]{1,0:T(8,128)(2,1)S(1)}, u32[]{:S(2)}, u32[]{:S(2)}) %collective-permute-start.9) | collective-permute-done | bytes 262176 | tf_op jit(solution)/shard_map/ppermute | solution.py:269
  55.5 3.2 %collective-permute-start.10 = (bf16[64,2048]{1,0:T(8,128)(2,1)S(1)}, bf16[64,2048]{1,0:T(8,128)(2,1)S(1)}, u32[]{:S(2)}, u32[]{:S(2)}) collective-permute-start(bf16[64,2048]{1,0:T(8,128)(2,1)S(1)} %add_convert_fusion.refs_0_), channel_id=1, source_target_pairs={{0,16},{4,20},{8,24},{12,28},{16,0},{20,4},{24,8},{28,12},{1,17},{... | collective-permute-start | bytes 786440 | tf_op jit(solution)/shard_map/ppermute | solution.py:269
  58.6 3.0 %collective-permute-start.13 = (bf16[64,2048]{1,0:T(8,128)(2,1)S(1)}, bf16[64,2048]{1,0:T(8,128)(2,1)S(1)}, u32[]{:S(2)}, u32[]{:S(2)}) collective-permute-start(bf16[64,2048]{1,0:T(8,128)(2,1)S(1)} %add_convert_fusion.refs_0_), channel_id=1, source_target_pairs={{0,8},{4,12},{8,0},{12,4},{16,24},{20,28},{24,16},{28,20},{1,9},{5... | collective-permute-start | bytes 786440 | tf_op jit(solution)/shard_map/ppermute | solution.py:269
  61.6 3.9 %collective-permute-done.10.refs_2_ = bf16[64,2048]{1,0:T(8,128)(2,1)S(1)} collective-permute-done((bf16[64,2048]{1,0:T(8,128)(2,1)S(1)}, bf16[64,2048]{1,0:T(8,128)(2,1)S(1)}, u32[]{:S(2)}, u32[]{:S(2)}) %collective-permute-start.10) | collective-permute-done | bytes 262176 | tf_op jit(solution)/shard_map/ppermute | solution.py:269
  65.6 3.3 %collective-permute-start.11 = (bf16[64,2048]{1,0:T(8,128)(2,1)S(1)}, bf16[64,2048]{1,0:T(8,128)(2,1)S(1)}, u32[]{:S(2)}, u32[]{:S(2)}) collective-permute-start(bf16[64,2048]{1,0:T(8,128)(2,1)S(1)} %collective-permute-done.10.refs_2_), channel_id=1, source_target_pairs={{0,8},{4,12},{8,0},{12,4},{16,24},{20,28},{24,16},{28,20},{1,9},{5... | collective-permute-start | bytes 786440 | tf_op jit(solution)/shard_map/ppermute | solution.py:269
  68.9 3.7 %collective-permute-start.14 = (bf16[64,2048]{1,0:T(8,128)(2,1)S(1)}, bf16[64,2048]{1,0:T(8,128)(2,1)S(1)}, u32[]{:S(2)}, u32[]{:S(2)}) collective-permute-start(bf16[64,2048]{1,0:T(8,128)(2,1)S(1)} %add_convert_fusion.refs_0_), channel_id=1, source_target_pairs={{0,4},{4,0},{8,12},{12,8},{16,20},{20,16},{24,28},{28,24},{1,5},{5... | collective-permute-start | bytes 786440 | tf_op jit(solution)/shard_map/ppermute | solution.py:269
  72.6 2.1 %collective-permute-start.15 = (bf16[64,2048]{1,0:T(8,128)(2,1)S(1)}, bf16[64,2048]{1,0:T(8,128)(2,1)S(1)}, u32[]{:S(2)}, u32[]{:S(2)}) collective-permute-start(bf16[64,2048]{1,0:T(8,128)(2,1)S(1)} %collective-permute-done.13.refs_1_), channel_id=1, source_target_pairs={{0,4},{4,0},{8,12},{12,8},{16,20},{20,16},{24,28},{28,24},{1,5},{5... | collective-permute-start | bytes 786440 | tf_op jit(solution)/shard_map/ppermute | solution.py:269
  74.7 1.0 %collective-permute-done.11.refs_0_ = bf16[64,2048]{1,0:T(8,128)(2,1)S(1)} collective-permute-done((bf16[64,2048]{1,0:T(8,128)(2,1)S(1)}, bf16[64,2048]{1,0:T(8,128)(2,1)S(1)}, u32[]{:S(2)}, u32[]{:S(2)}) %collective-permute-start.11) | collective-permute-done | bytes 262176 | tf_op jit(solution)/shard_map/ppermute | solution.py:269
  75.7 2.5 %collective-permute-start.12 = (bf16[64,2048]{1,0:T(8,128)(2,1)S(1)}, bf16[64,2048]{1,0:T(8,128)(2,1)S(1)}, u32[]{:S(2)}, u32[]{:S(2)}) collective-permute-start(bf16[64,2048]{1,0:T(8,128)(2,1)S(1)} %collective-permute-done.11.refs_0_), channel_id=1, source_target_pairs={{0,4},{4,0},{8,12},{12,8},{16,20},{20,16},{24,28},{28,24},{1,5},{5... | collective-permute-start | bytes 786440 | tf_op jit(solution)/shard_map/ppermute | solution.py:269
  78.2 1.2 %shard_map.98.refs_2_ = bf16[64,16384]{1,0:T(8,128)(2,1)} custom-call(s32[1]{0:T(128)} %bitcast.me_ref, bf16[64,2048]{1,0:T(8,128)(2,1)S(1)} %add_convert_fusion.refs_0_, bf16[64,2048]{1,0:T(8,128)(2,1)S(1)} %collective-permute-done.13.refs_1_, bf16[64,2048]{1,0:T(8,128)(2,1)S(1)} %collective-permute-done.10.refs_2_, ...), custom_call_target="tpu_custom_call" | custom-call | flops 68719476736 | bytes 16777216 | tf_op jit(solution)/shard_map/pallas_call | solution.py:255
  79.5 0.8 %shard_map.99 = bf16[64,16384]{1,0:T(8,128)(2,1)} custom-call(s32[1]{0:T(128)} %bitcast.me_ref, bf16[64,2048]{1,0:T(8,128)(2,1)S(1)} %collective-permute-done.11.refs_0_, bf16[64,2048]{1,0:T(8,128)(2,1)S(1)} %collective-permute-done.12.refs_1_, bf16[64,16384]{1,0:T(8,128)(2,1)} %shard_map.98.refs_2_), custom_call_target="tpu_custom_call", output_to_operand_aliasing={{}: (3, {})} | custom-call | tf_op jit(solution)/shard_map/pallas_call | solution.py:255
  (32 shorter events, 1.0 us)
Async XLA Ops:
  0.0 17.9 %copy-start.4 = (s32[1,128,4]{1,2,0:T(4,128)S(1)}, s32[1,128,4]{1,2,0:T(4,128)}, u32[]{:S(2)}) copy-start(s32[1,128,4]{1,2,0:T(4,128)} %param.16) | copy-start | bytes 6148
  4.4 19.9 %collective-permute-start.2 = (bf16[64,4352]{1,0:T(8,128)(2,1)}, bf16[64,4352]{1,0:T(8,128)(2,1)S(1)}, u32[]{:S(2)}, u32[]{:S(2)}) collective-permute-start(bf16[64,4352]{1,0:T(8,128)(2,1)} %shard_map.91), channel_id=1, source_target_pairs={{0,3},{1,2},{2,1},{3,0},{4,7},{5,6},{6,5},{7,4},{8,11},{9,10},{10,... | collective-permute-start | bytes 1671176 | tf_op jit(solution)/shard_map/ppermute | solution.py:269
  14.2 9.3 %collective-permute-start = (bf16[64,1280]{1,0:T(8,128)(2,1)}, bf16[64,1280]{1,0:T(8,128)(2,1)S(1)}, u32[]{:S(2)}, u32[]{:S(2)}) collective-permute-start(bf16[64,1280]{1,0:T(8,128)(2,1)} %get-tuple-element.19), channel_id=1, source_target_pairs={{0,1},{1,0},{2,3},{3,2},{4,5},{5,4},{6,7},{7,6},{8,9},{9,8},{10,11... | collective-permute-start | bytes 491528 | tf_op jit(solution)/shard_map/ppermute | solution.py:269
  14.5 9.8 %collective-permute-start.1 = (bf16[64,1280]{1,0:T(8,128)(2,1)}, bf16[64,1280]{1,0:T(8,128)(2,1)S(1)}, u32[]{:S(2)}, u32[]{:S(2)}) collective-permute-start(bf16[64,1280]{1,0:T(8,128)(2,1)} %get-tuple-element.20), channel_id=1, source_target_pairs={{0,2},{1,3},{2,0},{3,1},{4,6},{5,7},{6,4},{7,5},{8,10},{9,11},{10,... | collective-permute-start | bytes 491528 | tf_op jit(solution)/shard_map/ppermute | solution.py:269
  14.6 17.9 %collective-permute-start.3 = (bf16[64,3072]{1,0:T(8,128)(2,1)}, bf16[64,3072]{1,0:T(8,128)(2,1)S(1)}, u32[]{:S(2)}, u32[]{:S(2)}) collective-permute-start(bf16[64,3072]{1,0:T(8,128)(2,1)} %get-tuple-element.22), channel_id=1, source_target_pairs={{0,1},{1,0},{2,3},{3,2},{4,5},{5,4},{6,7},{7,6},{8,9},{9,8},{10,11... | collective-permute-start | bytes 1179656 | tf_op jit(solution)/shard_map/ppermute | solution.py:269
  16.0 16.7 %collective-permute-start.4 = (bf16[64,3072]{1,0:T(8,128)(2,1)}, bf16[64,3072]{1,0:T(8,128)(2,1)S(1)}, u32[]{:S(2)}, u32[]{:S(2)}) collective-permute-start(bf16[64,3072]{1,0:T(8,128)(2,1)} %get-tuple-element.23), channel_id=1, source_target_pairs={{0,2},{1,3},{2,0},{3,1},{4,6},{5,7},{6,4},{7,5},{8,10},{9,11},{10,... | collective-permute-start | bytes 1179656 | tf_op jit(solution)/shard_map/ppermute | solution.py:269
  24.3 1.1 %copy-start.2 = (bf16[64,4352]{1,0:T(8,128)(2,1)S(1)}, bf16[64,4352]{1,0:T(8,128)(2,1)}, u32[]{:S(2)}) copy-start(bf16[64,4352]{1,0:T(8,128)(2,1)} %get-tuple-element.21.refs_1_.refs_0_) | copy-start | bytes 1671172
  25.4 2.2 %copy-start = (bf16[1,128,64,256]{3,2,1,0:T(8,128)(2,1)S(1)}, bf16[1,128,64,256]{3,2,1,0:T(8,128)(2,1)}, u32[]{:S(2)}) copy-start(bf16[1,128,64,256]{3,2,1,0:T(8,128)(2,1)} %param.15) | copy-start | bytes 12582916
  25.4 2.9 %copy-start.1 = (bf16[128,64,128]{2,1,0:T(8,128)(2,1)S(1)}, bf16[128,64,128]{2,1,0:T(8,128)(2,1)}, u32[]{:S(2)}) copy-start(bf16[128,64,128]{2,1,0:T(8,128)(2,1)} %refs_6_.1) | copy-start | bytes 6291460
  25.4 2.9 %copy-start.3 = (f32[1,3,64,128]{3,2,1,0:T(8,128)S(1)}, f32[1,3,64,128]{3,2,1,0:T(8,128)}, u32[]{:S(2)}) copy-start(f32[1,3,64,128]{3,2,1,0:T(8,128)} %param.14) | copy-start | bytes 294916
  34.0 3.3 %collective-permute-start.6 = (bf16[2,64,2048]{2,1,0:T(8,128)(2,1)S(1)}, bf16[2,64,2048]{2,1,0:T(8,128)(2,1)S(1)}, u32[]{:S(2)}, u32[]{:S(2)}) collective-permute-start(bf16[2,64,2048]{2,1,0:T(8,128)(2,1)S(1)} %get-tuple-element.28), channel_id=1, source_target_pairs={{0,4},{4,0},{8,12},{12,8},{16,20},{20,16},{24,28},{28,24},{1,5},{5... | collective-permute-start | bytes 1572872 | tf_op jit(solution)/shard_map/ppermute | solution.py:269
  35.7 3.2 %collective-permute-start.5 = (bf16[2,64,2048]{2,1,0:T(8,128)(2,1)S(1)}, bf16[2,64,2048]{2,1,0:T(8,128)(2,1)S(1)}, u32[]{:S(2)}, u32[]{:S(2)}) collective-permute-start(bf16[2,64,2048]{2,1,0:T(8,128)(2,1)S(1)} %get-tuple-element.25), channel_id=1, source_target_pairs={{0,4},{4,0},{8,12},{12,8},{16,20},{20,16},{24,28},{28,24},{1,5},{5... | collective-permute-start | bytes 1572872 | tf_op jit(solution)/shard_map/ppermute | solution.py:269
  37.4 7.6 %collective-permute-start.7 = (bf16[64,2048]{1,0:T(8,128)(2,1)S(1)}, bf16[64,2048]{1,0:T(8,128)(2,1)S(1)}, u32[]{:S(2)}, u32[]{:S(2)}) collective-permute-start(bf16[64,2048]{1,0:T(8,128)(2,1)S(1)} %get-tuple-element.29), channel_id=1, source_target_pairs={{0,8},{4,12},{8,0},{12,4},{16,24},{20,28},{24,16},{28,20},{1,9},{5... | collective-permute-start | bytes 786440 | tf_op jit(solution)/shard_map/ppermute | solution.py:269
  38.8 16.6 %collective-permute-start.9 = (bf16[64,2048]{1,0:T(8,128)(2,1)S(1)}, bf16[64,2048]{1,0:T(8,128)(2,1)S(1)}, u32[]{:S(2)}, u32[]{:S(2)}) collective-permute-start(bf16[64,2048]{1,0:T(8,128)(2,1)S(1)} %get-tuple-element.30), channel_id=1, source_target_pairs={{0,8},{4,12},{8,0},{12,4},{16,24},{20,28},{24,16},{28,20},{1,9},{5... | collective-permute-start | bytes 786440 | tf_op jit(solution)/shard_map/ppermute | solution.py:269
  45.0 10.3 %collective-permute-start.8 = (bf16[64,2048]{1,0:T(8,128)(2,1)S(1)}, bf16[64,2048]{1,0:T(8,128)(2,1)S(1)}, u32[]{:S(2)}, u32[]{:S(2)}) collective-permute-start(bf16[64,2048]{1,0:T(8,128)(2,1)S(1)} %add_convert_fusion.1), channel_id=1, source_target_pairs={{0,16},{4,20},{8,24},{12,28},{16,0},{20,4},{24,8},{28,12},{1,17},{... | collective-permute-start | bytes 786440 | tf_op jit(solution)/shard_map/ppermute | solution.py:269
  55.5 10.1 %collective-permute-start.10 = (bf16[64,2048]{1,0:T(8,128)(2,1)S(1)}, bf16[64,2048]{1,0:T(8,128)(2,1)S(1)}, u32[]{:S(2)}, u32[]{:S(2)}) collective-permute-start(bf16[64,2048]{1,0:T(8,128)(2,1)S(1)} %add_convert_fusion.refs_0_), channel_id=1, source_target_pairs={{0,16},{4,20},{8,24},{12,28},{16,0},{20,4},{24,8},{28,12},{1,17},{... | collective-permute-start | bytes 786440 | tf_op jit(solution)/shard_map/ppermute | solution.py:269
  58.6 14.0 %collective-permute-start.13 = (bf16[64,2048]{1,0:T(8,128)(2,1)S(1)}, bf16[64,2048]{1,0:T(8,128)(2,1)S(1)}, u32[]{:S(2)}, u32[]{:S(2)}) collective-permute-start(bf16[64,2048]{1,0:T(8,128)(2,1)S(1)} %add_convert_fusion.refs_0_), channel_id=1, source_target_pairs={{0,8},{4,12},{8,0},{12,4},{16,24},{20,28},{24,16},{28,20},{1,9},{5... | collective-permute-start | bytes 786440 | tf_op jit(solution)/shard_map/ppermute | solution.py:269
  65.6 10.1 %collective-permute-start.11 = (bf16[64,2048]{1,0:T(8,128)(2,1)S(1)}, bf16[64,2048]{1,0:T(8,128)(2,1)S(1)}, u32[]{:S(2)}, u32[]{:S(2)}) collective-permute-start(bf16[64,2048]{1,0:T(8,128)(2,1)S(1)} %collective-permute-done.10.refs_2_), channel_id=1, source_target_pairs={{0,8},{4,12},{8,0},{12,4},{16,24},{20,28},{24,16},{28,20},{1,9},{5... | collective-permute-start | bytes 786440 | tf_op jit(solution)/shard_map/ppermute | solution.py:269
  68.9 9.3 %collective-permute-start.14 = (bf16[64,2048]{1,0:T(8,128)(2,1)S(1)}, bf16[64,2048]{1,0:T(8,128)(2,1)S(1)}, u32[]{:S(2)}, u32[]{:S(2)}) collective-permute-start(bf16[64,2048]{1,0:T(8,128)(2,1)S(1)} %add_convert_fusion.refs_0_), channel_id=1, source_target_pairs={{0,4},{4,0},{8,12},{12,8},{16,20},{20,16},{24,28},{28,24},{1,5},{5... | collective-permute-start | bytes 786440 | tf_op jit(solution)/shard_map/ppermute | solution.py:269
  72.6 5.6 %collective-permute-start.15 = (bf16[64,2048]{1,0:T(8,128)(2,1)S(1)}, bf16[64,2048]{1,0:T(8,128)(2,1)S(1)}, u32[]{:S(2)}, u32[]{:S(2)}) collective-permute-start(bf16[64,2048]{1,0:T(8,128)(2,1)S(1)} %collective-permute-done.13.refs_1_), channel_id=1, source_target_pairs={{0,4},{4,0},{8,12},{12,8},{16,20},{20,16},{24,28},{28,24},{1,5},{5... | collective-permute-start | bytes 786440 | tf_op jit(solution)/shard_map/ppermute | solution.py:269
  74.7 3.5 %collective-permute-start.16 = (bf16[64,2048]{1,0:T(8,128)(2,1)S(1)}, bf16[64,2048]{1,0:T(8,128)(2,1)S(1)}, u32[]{:S(2)}, u32[]{:S(2)}) collective-permute-start(bf16[64,2048]{1,0:T(8,128)(2,1)S(1)} %collective-permute-done.10.refs_2_), channel_id=1, source_target_pairs={{0,4},{4,0},{8,12},{12,8},{16,20},{20,16},{24,28},{28,24},{1,5},{5... | collective-permute-start | bytes 786440 | tf_op jit(solution)/shard_map/ppermute | solution.py:269
  75.7 3.7 %collective-permute-start.12 = (bf16[64,2048]{1,0:T(8,128)(2,1)S(1)}, bf16[64,2048]{1,0:T(8,128)(2,1)S(1)}, u32[]{:S(2)}, u32[]{:S(2)}) collective-permute-start(bf16[64,2048]{1,0:T(8,128)(2,1)S(1)} %collective-permute-done.11.refs_0_), channel_id=1, source_target_pairs={{0,4},{4,0},{8,12},{12,8},{16,20},{20,16},{24,28},{28,24},{1,5},{5... | collective-permute-start | bytes 786440 | tf_op jit(solution)/shard_map/ppermute | solution.py:269

commit v5 on v4

--- a/solution.py
+++ b/solution.py
@@ -12,6 +12,7 @@
 HEAD = 8
 FIRST_HEAD = 32
 FAR_PIECES = 2
+HALVES = 2
 NEAR_VMEM = 60
 F32, BF16 = jnp.float32, jnp.bfloat16
 NT = (((1,), (1,)), ((), ()))
@@ -195,14 +196,14 @@
 
 
 def gather_kernel(parts, tile, me_ref, tgt_ref, far_ref, *refs):
-    got_refs, (acc, first_ref, rest_ref) = refs[:-3], refs[-3:]
+    got_refs, acc, send_refs = refs[: len(parts)], refs[len(parts)], refs[len(parts) + 1 :]
     add_products(acc, tgt_ref, me_ref[0], parts, got_refs, tile)
-    z, core = me_ref[1] // 2, me_ref[1] % 2
-    chips = acc.shape[0] // 2
-    for n in range(chips):
-        m = chips - 1 - 2 * n if n < chips // 2 else 2 * (chips - 1 - n)
-        out = first_ref.at[n] if n < chips // 2 else rest_ref.at[n - chips // 2]
-        out[...] = acc[2 * (z ^ m) + 1 - core].astype(BF16)
+    core = me_ref[1] % 2
+    rows = send_refs[0].shape[1]
+    for c, send_ref in enumerate(send_refs):
+        for z in range(send_ref.shape[0]):
+            send = acc[2 * z + 1 - core, c * rows : (c + 1) * rows]
+            send_ref[z] = send.astype(BF16)
 
 
 def gather_near(parts, me, tgt, far, got, tile):
@@ -211,26 +212,27 @@
         functools.partial(gather_kernel, parts, tile),
         out_shape=[
             jax.ShapeDtypeStruct(far.shape, F32),
-            jax.ShapeDtypeStruct((pieces // 4, rows, width), BF16),
-            jax.ShapeDtypeStruct((pieces // 4, rows, width), BF16),
-        ],
+        ]
+        + [jax.ShapeDtypeStruct((pieces // 2, rows // HALVES, width), BF16)] * HALVES,
         in_specs=[SMEM] * 2 + [VMEM] * (1 + len(got)),
-        out_specs=[VMEM] * 3,
+        out_specs=[VMEM] * (1 + HALVES),
         input_output_aliases={2: 0},
         compiler_params=pltpu.CompilerParams(vmem_limit_bytes=16 * 2**20),
     )(me, tgt, far, *got)
 
 
-def split_kernel(masks, me_ref, acc_ref, got_ref, *out_refs):
+def split_kernel(half, masks, me_ref, acc_ref, got_ref, *out_refs):
     z, core = me_ref[0] // 2, me_ref[0] % 2
-    for n, (m, out_ref) in enumerate(zip(masks, out_refs)):
-        out_ref[...] = (acc_ref[2 * (z ^ m) + core] + got_ref[n].astype(F32)).astype(out_ref.dtype)
-
-
-def split(masks, dtypes, me, acc, got):
-    return pl.pallas_call(
-        functools.partial(split_kernel, masks),
-        out_shape=[jax.ShapeDtypeStruct(got.shape[-2:], d) for d in dtypes],
+    rows = got_ref.shape[1]
+    for m, out_ref in zip(masks, out_refs):
+        here = acc_ref[2 * (z ^ m) + core, half * rows : (half + 1) * rows]
+        out_ref[...] = (here + got_ref[z ^ m].astype(F32)).astype(out_ref.dtype)
+
+
+def split(half, masks, dtypes, me, acc, got):
+    return pl.pallas_call(
+        functools.partial(split_kernel, half, masks),
+        out_shape=[jax.ShapeDtypeStruct(got.shape[1:], d) for d in dtypes],
         in_specs=[SMEM, VMEM, VMEM],
         out_specs=[VMEM] * len(masks),
         compiler_params=pltpu.CompilerParams(vmem_limit_bytes=16 * 2**20),
@@ -240,10 +242,11 @@
 def place_kernel(masks, me_ref, *refs):
     piece_refs, (out_ref, sems) = refs[: len(masks)], refs[-2:]
     copies = []
-    for n, (m, piece_ref) in enumerate(zip(masks, piece_refs)):
-        width = piece_ref.shape[1]
+    for n, ((half, m), piece_ref) in enumerate(zip(masks, piece_refs)):
+        rows, width = piece_ref.shape
         spot = pl.ds(pl.multiple_of((me_ref[0] ^ m) * width, width), width)
-        copies.append(pltpu.make_async_copy(piece_ref, out_ref.at[:, spot], sems.at[n]))
+        out = out_ref.at[pl.ds(half * rows, rows), spot]
+        copies.append(pltpu.make_async_copy(piece_ref, out, sems.at[n]))
     for copy in copies:
         copy.start()
     for copy in copies:
@@ -254,7 +257,7 @@
     rows, width = parts[0].shape
     return pl.pallas_call(
         functools.partial(place_kernel, masks),
-        out_shape=jax.ShapeDtypeStruct((rows, width * count), BF16),
+        out_shape=jax.ShapeDtypeStruct((HALVES * rows, width * count), BF16),
         in_specs=[SMEM] + [VMEM] * len(parts) + [ANY] * (out is not None),
         out_specs=ANY,
         scratch_shapes=[pltpu.SemaphoreType.DMA((len(parts),))],
@@ -273,24 +276,23 @@
     return lax.optimization_barrier((value,) + others)[0]
 
 
-def sum_and_share(me, acc, got_first, got_rest):
+def sum_and_share(half, me, acc, got):
     chips = acc.shape[0] // 2
     if chips == 4:
-        first, near = split((3, 1), (BF16, BF16), me, acc, got_first)
-        cross, own = split((2, 0), (F32, F32), me, acc, got_rest)
+        first, near, cross, own = split(half, (3, 1, 2, 0), (BF16, BF16, F32, F32), me, acc, got)
         a = swap(first, "src", 2)
         cross = (cross + a.astype(F32)).astype(BF16)
         b = swap(cross, "src", 4)
-        c = swap(near, "src", 2)
-        own = (own + b.astype(F32) + c.astype(F32)).astype(BF16)
+        c = swap(tied(near, cross), "src", 2)
+        own = own + b.astype(F32)
+        own = (own + c.astype(F32)).astype(BF16)
         d = swap(own, "src", 4)
         e = swap(own, "src", 2)
         return (0, 1, 2, 3), [own, e, d, swap(d, "src", 2)]
     masks = tuple(range(chips))
-    odd, even = masks[::-2], masks[-2::-2]
-    first = split(odd, (BF16,) * len(odd), me, acc, got_first)
-    *rest, own = split(even, (BF16,) * (len(even) - 1) + (F32,), me, acc, got_rest)
-    for m, part in zip(odd + even[:-1], [*first, *rest]):
+    dtypes = (F32,) + (BF16,) * (chips - 1)
+    own, *rest = split(half, masks, dtypes, me, acc, got)
+    for m, part in zip(masks[1:], rest):
         own = own + swap(part, "src", 2 * m).astype(F32)
     own = own.astype(BF16)
     return masks, [own] + [swap(own, "src", 2 * m) for m in masks[1:]]
@@ -349,21 +351,20 @@
         count,
     )
     here = jnp.stack([me_t, me_s])
-    acc, first, rest = gather_near(
+    acc, *sends = gather_near(
         late, here, targets(late), acc, [got[part] for part in late], tile
     )
-    owners, mine = sum_and_share(
-        me_s.reshape(1), acc, swap(first, "src", 1), swap(rest, "src", 1)
-    )
-    other = [swap(p, "src", 1) for p in mine]
-    parts = [(2 * m, q) for m, q in zip(owners, mine)]
-    parts += [(2 * m + 1, q) for m, q in zip(owners, other)]
-    early = [part for part in parts if part[0] // 2 != owners[-1]]
-    late = [part for part in parts if part[0] // 2 == owners[-1]]
+    me = me_s.reshape(1)
+    parts = []
+    for half, send in enumerate(sends):
+        owners, mine = sum_and_share(half, me, acc, swap(send, "src", 1))
+        parts += [((half, 2 * m), q) for m, q in zip(owners, mine)]
+        parts += [((half, 2 * m + 1), swap(q, "src", 1)) for m, q in zip(owners, mine)]
+    last = parts[-len(owners) - 1], parts[-1]
     out = None
-    for some in (early, late):
+    for some in ([part for part in parts if part[0] not in (last[0][0], last[1][0])], last):
         spots, values = zip(*some)
-        out = place(spots, me_s.reshape(1), values, sources, out)
+        out = place(spots, me, values, sources, out)
     return out.T
 
 

time: 81.4 us -> 78.5 us (0.964); the launches traced: 80.3 us -> 78.2 us
  waiting for transfers between devices: 26.7 us -> 13.8 us
  starting transfers between devices: 29.6 us -> 40.6 us
    ppermute x17 -> x27, waiting for transfers between devices: 26.7 us -> 13.8 us  [swap(): return lax.ppermute(value, axis, [(i, i ^ mask) for i in range(size)])]
    ppermute x17 -> x27, starting transfers between devices: 29.6 us -> 40.6 us  [swap(): return lax.ppermute(value, axis, [(i, i ^ mask) for i in range(size)])]
  transfers between devices with their start and end apart: 17 -> 27, of which waited for: 8 -> 7; matrix products, arithmetic and copies ran while one was open for 1% -> 1% of each run, Pallas kernels for 17% -> 17%
where the time goes in v5:
time: 78.5 us; the launch traced here: 78.2 us
  starting transfers between devices  40.6 us (52%)
  Pallas kernels  20 us (25%)
  waiting for transfers between devices  13.8 us (18%)
  local copies, waits for them, and re-layouts  3.44 us (4%)
    ppermute x27, starting transfers between devices, swap(): return lax.ppermute(value, axis, [(i, i ^ mask) for i in range(size)])  40.6 us
    ppermute x27, waiting for transfers between devices, swap(): return lax.ppermute(value, axis, [(i, i ^ mask) for i in range(size)])  13.8 us
    pallas_call x2, Pallas kernels, near_products(): pl.pallas_call(functools.partial(near_kernel, parts), out_shape=[jax.Shap...  11.1 us
    pallas_call x1, Pallas kernels, far_field(): pl.pallas_call(functools.partial(far_kernel, groups, count), out_shape=ja...  4.01 us
    unnamed x11, local copies, waits for them, and re-layouts  2.64 us
    pallas_call x2, Pallas kernels, place(): pl.pallas_call(functools.partial(place_kernel, masks), out_shape=jax.Shap...  2.06 us
  transfers between devices with their start and end apart: 27, of which 7 were waited for; matrix products, arithmetic and copies ran while one was open for 1% of the time, Pallas kernels for 17%

profile of v5, /device:TPU:1, one launch (start us, length us, event | category | flops | bytes accessed | tf_op | source)
XLA Modules:
  0.0 78.2 jit_solution(10380886141243293006)
XLA Ops:
  0.0 4.4 %shard_map.91 = bf16[64,4352]{1,0:T(8,128)(2,1)} custom-call(s32[1]{0:T(128)} %bitcast.1.me_ref, s32[128]{0:T(128)} %src_ref.3, s32[1,128]{1,0:T(1,128)} %bitcast.11, bf16[64,2048]{1,0:T(8,128)(2,1)} %bitcast.9, bf16[16,64,128]{2,1,0:T(8,128)(2,1)} %basis_ref.3, bf16[128,128,128]{2,1,0:T(8,128)(2,1)} %tiles_ref.3), custom_call_target="tpu_custom_call" | custom-call | tf_op jit(solution)/shard_map/pallas_call | solution.py:94
  4.4 3.1 %collective-permute-start.2 = (bf16[64,4352]{1,0:T(8,128)(2,1)}, bf16[64,4352]{1,0:T(8,128)(2,1)S(1)}, u32[]{:S(2)}, u32[]{:S(2)}) collective-permute-start(bf16[64,4352]{1,0:T(8,128)(2,1)} %shard_map.91), channel_id=1, source_target_pairs={{0,3},{1,2},{2,1},{3,0},{4,7},{5,6},{6,5},{7,4},{8,11},{9,10},{10,... | collective-permute-start | bytes 1671176 | tf_op jit(solution)/shard_map/ppermute | solution.py:272
  7.5 6.7 %shard_map.92 = (bf16[64,1280]{1,0:T(8,128)(2,1)}, bf16[64,1280]{1,0:T(8,128)(2,1)}, bf16[64,4352]{1,0:T(8,128)(2,1)}, bf16[64,3072]{1,0:T(8,128)(2,1)}, bf16[64,3072]{1,0:T(8,128)(2,1)}) custom-call(s32[1]{0:T(128)} %bitcast.1.me_ref, s32[128]{0:T(128)} %src_ref.3, s32[1,128]{1,0:T(1,128)} %bitcast.12, bf16[64,2048]{1,0:T(8,128)(2,1)} %bitcast.10, ...), custom_call_target="tpu_custom_call" | custom-call | tf_op jit(solution)/shard_map/pallas_call | solution.py:94
  14.5 1.4 %collective-permute-start.3 = (bf16[64,3072]{1,0:T(8,128)(2,1)}, bf16[64,3072]{1,0:T(8,128)(2,1)S(1)}, u32[]{:S(2)}, u32[]{:S(2)}) collective-permute-start(bf16[64,3072]{1,0:T(8,128)(2,1)} %get-tuple-element.28), channel_id=1, source_target_pairs={{0,1},{1,0},{2,3},{3,2},{4,5},{5,4},{6,7},{7,6},{8,9},{9,8},{10,11... | collective-permute-start | bytes 1179656 | tf_op jit(solution)/shard_map/ppermute | solution.py:272
  15.9 1.2 %collective-permute-start.4 = (bf16[64,3072]{1,0:T(8,128)(2,1)}, bf16[64,3072]{1,0:T(8,128)(2,1)S(1)}, u32[]{:S(2)}, u32[]{:S(2)}) collective-permute-start(bf16[64,3072]{1,0:T(8,128)(2,1)} %get-tuple-element.29), channel_id=1, source_target_pairs={{0,2},{1,3},{2,0},{3,1},{4,6},{5,7},{6,4},{7,5},{8,10},{9,11},{10,... | collective-permute-start | bytes 1179656 | tf_op jit(solution)/shard_map/ppermute | solution.py:272
  18.2 5.4 %collective-permute-done.refs_1_.refs_0_ = bf16[64,1280]{1,0:T(8,128)(2,1)S(1)} collective-permute-done((bf16[64,1280]{1,0:T(8,128)(2,1)}, bf16[64,1280]{1,0:T(8,128)(2,1)S(1)}, u32[]{:S(2)}, u32[]{:S(2)}) %collective-permute-start) | collective-permute-done | bytes 163872 | tf_op jit(solution)/shard_map/ppermute | solution.py:272
  23.5 0.8 collective-permute-done.1.refs_2_.refs_1_
  24.3 1.0 %copy-done.2 = bf16[64,4352]{1,0:T(8,128)(2,1)S(1)} copy-done((bf16[64,4352]{1,0:T(8,128)(2,1)S(1)}, bf16[64,4352]{1,0:T(8,128)(2,1)}, u32[]{:S(2)}) %copy-start.2) | copy-done | bytes 557080
  25.4 1.4 %shard_map.93.refs_7_ = f32[8,64,2048]{2,1,0:T(8,128)S(1)} custom-call(s32[1]{0:T(128)} %bitcast.1.me_ref, s32[2,128]{1,0:T(2,128)S(1)} %convert_convert_fusion.1.tgt_ref, bf16[64,4352]{1,0:T(8,128)(2,1)S(1)} %collective-permute-done.2.refs_0_.refs_3_, bf16[64,4352]{1,0:T(8,128)(2,1)S(1)} %copy-done.2), custom_call_target="tpu_custom_call" | custom-call | flops 68719476736 | bytes 16777216 | tf_op jit(solution)/shard_map/pallas_call | solution.py:128
  26.8 0.8 %copy-done = bf16[1,128,64,256]{3,2,1,0:T(8,128)(2,1)S(1)} copy-done((bf16[1,128,64,256]{3,2,1,0:T(8,128)(2,1)S(1)}, bf16[1,128,64,256]{3,2,1,0:T(8,128)(2,1)}, u32[]{:S(2)}) %copy-start) | copy-done | bytes 4194328
  28.3 4.0 %shard_map.94.far_ref = f32[8,64,2048]{2,1,0:T(8,128)S(1)} custom-call(s32[1]{0:T(128)} %bitcast.1.me_ref, s32[512]{0:T(512)S(1)} %reshape_squeeze.3.node_ref, bf16[64,4352]{1,0:T(8,128)(2,1)S(1)} %copy-done.2, bf16[64,1280]{1,0:T(8,128)(2,1)S(1)} %collective-permute-done.refs_1_.refs_0_, ...), custom_call_target="tpu_custom_call", output_to_operand_aliasing={{}: (9, {})} | custom-call | tf_op jit(solution)/shard_map/pallas_call | solution.py:183
  32.7 1.3 %shard_map.95 = (f32[8,64,2048]{2,1,0:T(8,128)S(1)}, bf16[4,32,2048]{2,1,0:T(8,128)(2,1)S(1)}, bf16[4,32,2048]{2,1,0:T(8,128)(2,1)S(1)}) custom-call(s32[2]{0:T(128)S(1)} %pad_add_fusion.me_ref, s32[4,128]{1,0:T(4,128)S(1)} %convert_convert_fusion.tgt_ref, f32[8,64,2048]{2,1,0:T(8,128)S(1)} %shard_map.94.far_ref, ...), custom_call_target="tpu_custom_call", output_to_operand_aliasing={{0}: (2, {})} | custom-call | tf_op jit(solution)/shard_map/pallas_call | solution.py:211
  34.0 1.6 %collective-permute-start.12 = (bf16[4,32,2048]{2,1,0:T(8,128)(2,1)S(1)}, bf16[4,32,2048]{2,1,0:T(8,128)(2,1)S(1)}, u32[]{:S(2)}, u32[]{:S(2)}) collective-permute-start(bf16[4,32,2048]{2,1,0:T(8,128)(2,1)S(1)} %get-tuple-element.37), channel_id=1, source_target_pairs={{0,4},{4,0},{8,12},{12,8},{16,20},{20,16},{24,28},{28,24},{1,5},{5... | collective-permute-start | bytes 1572872 | tf_op jit(solution)/shard_map/ppermute | solution.py:272
  35.6 1.5 %collective-permute-done.12.got_ref = bf16[4,32,2048]{2,1,0:T(8,128)(2,1)S(1)} collective-permute-done((bf16[4,32,2048]{2,1,0:T(8,128)(2,1)S(1)}, bf16[4,32,2048]{2,1,0:T(8,128)(2,1)S(1)}, u32[]{:S(2)}, u32[]{:S(2)}) %collective-permute-start.12) | collective-permute-done | bytes 524320 | tf_op jit(solution)/shard_map/ppermute | solution.py:272
  37.2 1.4 %collective-permute-start.13 = (bf16[32,2048]{1,0:T(8,128)(2,1)S(1)}, bf16[32,2048]{1,0:T(8,128)(2,1)S(1)}, u32[]{:S(2)}, u32[]{:S(2)}) collective-permute-start(bf16[32,2048]{1,0:T(8,128)(2,1)S(1)} %get-tuple-element.40), channel_id=1, source_target_pairs={{0,8},{4,12},{8,0},{12,4},{16,24},{20,28},{24,16},{28,20},{1,9},{5... | collective-permute-start | bytes 393224 | tf_op jit(solution)/shard_map/ppermute | solution.py:272
  39.3 2.7 %collective-permute-done.13 = bf16[32,2048]{1,0:T(8,128)(2,1)S(1)} collective-permute-done((bf16[32,2048]{1,0:T(8,128)(2,1)S(1)}, bf16[32,2048]{1,0:T(8,128)(2,1)S(1)}, u32[]{:S(2)}, u32[]{:S(2)}) %collective-permute-start.13) | collective-permute-done | bytes 131104 | tf_op jit(solution)/shard_map/ppermute | solution.py:272
  42.0 2.4 %collective-permute-start.14 = (bf16[32,2048]{1,0:T(8,128)(2,1)S(1)}, bf16[32,2048]{1,0:T(8,128)(2,1)S(1)}, u32[]{:S(2)}, u32[]{:S(2)}) collective-permute-start(bf16[32,2048]{1,0:T(8,128)(2,1)S(1)} %add_convert_fusion.1), channel_id=1, source_target_pairs={{0,16},{4,20},{8,24},{12,28},{16,0},{20,4},{24,8},{28,12},{1,17},{... | collective-permute-start | bytes 393224 | tf_op jit(solution)/shard_map/ppermute | solution.py:272
  44.4 1.3 %collective-permute-start.15 = (bf16[32,2048]{1,0:T(8,128)(2,1)S(1)}, bf16[32,2048]{1,0:T(8,128)(2,1)S(1)}, u32[]{:S(2)}, u32[]{:S(2)}) collective-permute-start(bf16[32,2048]{1,0:T(8,128)(2,1)S(1)} %get-tuple-element.42), channel_id=1, source_target_pairs={{0,8},{4,12},{8,0},{12,4},{16,24},{20,28},{24,16},{28,20},{1,9},{5... | collective-permute-start | bytes 393224 | tf_op jit(solution)/shard_map/ppermute | solution.py:272
  45.7 1.5 %collective-permute-start.7 = (bf16[32,2048]{1,0:T(8,128)(2,1)S(1)}, bf16[32,2048]{1,0:T(8,128)(2,1)S(1)}, u32[]{:S(2)}, u32[]{:S(2)}) collective-permute-start(bf16[32,2048]{1,0:T(8,128)(2,1)S(1)} %add_convert_fusion.3), channel_id=1, source_target_pairs={{0,16},{4,20},{8,24},{12,28},{16,0},{20,4},{24,8},{28,12},{1,17},{... | collective-permute-start | bytes 393224 | tf_op jit(solution)/shard_map/ppermute | solution.py:272
  47.2 1.3 %collective-permute-start.8 = (bf16[32,2048]{1,0:T(8,128)(2,1)S(1)}, bf16[32,2048]{1,0:T(8,128)(2,1)S(1)}, u32[]{:S(2)}, u32[]{:S(2)}) collective-permute-start(bf16[32,2048]{1,0:T(8,128)(2,1)S(1)} %get-tuple-element.36), channel_id=1, source_target_pairs={{0,8},{4,12},{8,0},{12,4},{16,24},{20,28},{24,16},{28,20},{1,9},{5... | collective-permute-start | bytes 393224 | tf_op jit(solution)/shard_map/ppermute | solution.py:272
  48.9 3.1 %collective-permute-start.17 = (bf16[32,2048]{1,0:T(8,128)(2,1)S(1)}, bf16[32,2048]{1,0:T(8,128)(2,1)S(1)}, u32[]{:S(2)}, u32[]{:S(2)}) collective-permute-start(bf16[32,2048]{1,0:T(8,128)(2,1)S(1)} %add_convert_fusion.refs_0_), channel_id=1, source_target_pairs={{0,16},{4,20},{8,24},{12,28},{16,0},{20,4},{24,8},{28,12},{1,17},{... | collective-permute-start | bytes 393224 | tf_op jit(solution)/shard_map/ppermute | solution.py:272
  52.0 2.9 %collective-permute-start.16 = (bf16[32,2048]{1,0:T(8,128)(2,1)S(1)}, bf16[32,2048]{1,0:T(8,128)(2,1)S(1)}, u32[]{:S(2)}, u32[]{:S(2)}) collective-permute-start(bf16[32,2048]{1,0:T(8,128)(2,1)S(1)} %add_convert_fusion.refs_0_), channel_id=1, source_target_pairs={{0,8},{4,12},{8,0},{12,4},{16,24},{20,28},{24,16},{28,20},{1,9},{5... | collective-permute-start | bytes 393224 | tf_op jit(solution)/shard_map/ppermute | solution.py:272
  54.9 3.6 %collective-permute-start.19 = (bf16[32,2048]{1,0:T(8,128)(2,1)S(1)}, bf16[32,2048]{1,0:T(8,128)(2,1)S(1)}, u32[]{:S(2)}, u32[]{:S(2)}) collective-permute-start(bf16[32,2048]{1,0:T(8,128)(2,1)S(1)} %add_convert_fusion.refs_0_), channel_id=1, source_target_pairs={{0,4},{4,0},{8,12},{12,8},{16,20},{20,16},{24,28},{28,24},{1,5},{5... | collective-permute-start | bytes 393224 | tf_op jit(solution)/shard_map/ppermute | solution.py:272
  58.7 1.9 %collective-permute-start.9 = (bf16[32,2048]{1,0:T(8,128)(2,1)S(1)}, bf16[32,2048]{1,0:T(8,128)(2,1)S(1)}, u32[]{:S(2)}, u32[]{:S(2)}) collective-permute-start(bf16[32,2048]{1,0:T(8,128)(2,1)S(1)} %add_convert_fusion.2.refs_8_), channel_id=1, source_target_pairs={{0,16},{4,20},{8,24},{12,28},{16,0},{20,4},{24,8},{28,12},{1,17},{... | collective-permute-start | bytes 393224 | tf_op jit(solution)/shard_map/ppermute | solution.py:272
  60.6 3.6 %collective-permute-start.24 = (bf16[32,2048]{1,0:T(8,128)(2,1)S(1)}, bf16[32,2048]{1,0:T(8,128)(2,1)S(1)}, u32[]{:S(2)}, u32[]{:S(2)}) collective-permute-start(bf16[32,2048]{1,0:T(8,128)(2,1)S(1)} %add_convert_fusion.2.refs_8_), channel_id=1, source_target_pairs={{0,4},{4,0},{8,12},{12,8},{16,20},{20,16},{24,28},{28,24},{1,5},{5... | collective-permute-start | bytes 393224 | tf_op jit(solution)/shard_map/ppermute | solution.py:272
  64.4 2.8 %collective-permute-start.20 = (bf16[32,2048]{1,0:T(8,128)(2,1)S(1)}, bf16[32,2048]{1,0:T(8,128)(2,1)S(1)}, u32[]{:S(2)}, u32[]{:S(2)}) collective-permute-start(bf16[32,2048]{1,0:T(8,128)(2,1)S(1)} %collective-permute-done.16.refs_1_), channel_id=1, source_target_pairs={{0,4},{4,0},{8,12},{12,8},{16,20},{20,16},{24,28},{28,24},{1,5},{5... | collective-permute-start | bytes 393224 | tf_op jit(solution)/shard_map/ppermute | solution.py:272
  67.2 3.0 %collective-permute-start.21 = (bf16[32,2048]{1,0:T(8,128)(2,1)S(1)}, bf16[32,2048]{1,0:T(8,128)(2,1)S(1)}, u32[]{:S(2)}, u32[]{:S(2)}) collective-permute-start(bf16[32,2048]{1,0:T(8,128)(2,1)S(1)} %collective-permute-done.17.refs_2_), channel_id=1, source_target_pairs={{0,4},{4,0},{8,12},{12,8},{16,20},{20,16},{24,28},{28,24},{1,5},{5... | collective-permute-start | bytes 393224 | tf_op jit(solution)/shard_map/ppermute | solution.py:272
  70.2 1.9 %collective-permute-start.26 = (bf16[32,2048]{1,0:T(8,128)(2,1)S(1)}, bf16[32,2048]{1,0:T(8,128)(2,1)S(1)}, u32[]{:S(2)}, u32[]{:S(2)}) collective-permute-start(bf16[32,2048]{1,0:T(8,128)(2,1)S(1)} %collective-permute-done.9.refs_10_), channel_id=1, source_target_pairs={{0,4},{4,0},{8,12},{12,8},{16,20},{20,16},{24,28},{28,24},{1,5},{5... | collective-permute-start | bytes 393224 | tf_op jit(solution)/shard_map/ppermute | solution.py:272
  72.6 2.7 %collective-permute-done.10.refs_0_ = bf16[32,2048]{1,0:T(8,128)(2,1)S(1)} collective-permute-done((bf16[32,2048]{1,0:T(8,128)(2,1)S(1)}, bf16[32,2048]{1,0:T(8,128)(2,1)S(1)}, u32[]{:S(2)}, u32[]{:S(2)}) %collective-permute-start.10) | collective-permute-done | bytes 131104 | tf_op jit(solution)/shard_map/ppermute | solution.py:272
  75.3 0.8 %collective-permute-start.11 = (bf16[32,2048]{1,0:T(8,128)(2,1)S(1)}, bf16[32,2048]{1,0:T(8,128)(2,1)S(1)}, u32[]{:S(2)}, u32[]{:S(2)}) collective-permute-start(bf16[32,2048]{1,0:T(8,128)(2,1)S(1)} %collective-permute-done.10.refs_0_), channel_id=1, source_target_pairs={{0,4},{4,0},{8,12},{12,8},{16,20},{20,16},{24,28},{28,24},{1,5},{5... | collective-permute-start | bytes 393224 | tf_op jit(solution)/shard_map/ppermute | solution.py:272
  76.1 1.3 %shard_map.98.refs_2_ = bf16[64,16384]{1,0:T(8,128)(2,1)} custom-call(s32[1]{0:T(128)} %bitcast.me_ref, bf16[32,2048]{1,0:T(8,128)(2,1)S(1)} %add_convert_fusion.refs_0_, bf16[32,2048]{1,0:T(8,128)(2,1)S(1)} %collective-permute-done.16.refs_1_, bf16[32,2048]{1,0:T(8,128)(2,1)S(1)} %collective-permute-done.17.refs_2_, ...), custom_call_target="tpu_custom_call" | custom-call | flops 68719476736 | bytes 16777216 | tf_op jit(solution)/shard_map/pallas_call | solution.py:258
  77.5 0.7 shard_map.99
  (54 shorter events, 4.7 us)
Async XLA Ops:
  0.0 17.9 %copy-start.4 = (s32[1,128,4]{1,2,0:T(4,128)S(1)}, s32[1,128,4]{1,2,0:T(4,128)}, u32[]{:S(2)}) copy-start(s32[1,128,4]{1,2,0:T(4,128)} %param.16) | copy-start | bytes 6148
  4.4 19.9 %collective-permute-start.2 = (bf16[64,4352]{1,0:T(8,128)(2,1)}, bf16[64,4352]{1,0:T(8,128)(2,1)S(1)}, u32[]{:S(2)}, u32[]{:S(2)}) collective-permute-start(bf16[64,4352]{1,0:T(8,128)(2,1)} %shard_map.91), channel_id=1, source_target_pairs={{0,3},{1,2},{2,1},{3,0},{4,7},{5,6},{6,5},{7,4},{8,11},{9,10},{10,... | collective-permute-start | bytes 1671176 | tf_op jit(solution)/shard_map/ppermute | solution.py:272
  14.2 9.3 %collective-permute-start = (bf16[64,1280]{1,0:T(8,128)(2,1)}, bf16[64,1280]{1,0:T(8,128)(2,1)S(1)}, u32[]{:S(2)}, u32[]{:S(2)}) collective-permute-start(bf16[64,1280]{1,0:T(8,128)(2,1)} %get-tuple-element.25), channel_id=1, source_target_pairs={{0,1},{1,0},{2,3},{3,2},{4,5},{5,4},{6,7},{7,6},{8,9},{9,8},{10,11... | collective-permute-start | bytes 491528 | tf_op jit(solution)/shard_map/ppermute | solution.py:272
  14.5 9.8 %collective-permute-start.1 = (bf16[64,1280]{1,0:T(8,128)(2,1)}, bf16[64,1280]{1,0:T(8,128)(2,1)S(1)}, u32[]{:S(2)}, u32[]{:S(2)}) collective-permute-start(bf16[64,1280]{1,0:T(8,128)(2,1)} %get-tuple-element.26), channel_id=1, source_target_pairs={{0,2},{1,3},{2,0},{3,1},{4,6},{5,7},{6,4},{7,5},{8,10},{9,11},{10,... | collective-permute-start | bytes 491528 | tf_op jit(solution)/shard_map/ppermute | solution.py:272
  14.5 17.7 %collective-permute-start.3 = (bf16[64,3072]{1,0:T(8,128)(2,1)}, bf16[64,3072]{1,0:T(8,128)(2,1)S(1)}, u32[]{:S(2)}, u32[]{:S(2)}) collective-permute-start(bf16[64,3072]{1,0:T(8,128)(2,1)} %get-tuple-element.28), channel_id=1, source_target_pairs={{0,1},{1,0},{2,3},{3,2},{4,5},{5,4},{6,7},{7,6},{8,9},{9,8},{10,11... | collective-permute-start | bytes 1179656 | tf_op jit(solution)/shard_map/ppermute | solution.py:272
  15.9 16.8 %collective-permute-start.4 = (bf16[64,3072]{1,0:T(8,128)(2,1)}, bf16[64,3072]{1,0:T(8,128)(2,1)S(1)}, u32[]{:S(2)}, u32[]{:S(2)}) collective-permute-start(bf16[64,3072]{1,0:T(8,128)(2,1)} %get-tuple-element.29), channel_id=1, source_target_pairs={{0,2},{1,3},{2,0},{3,1},{4,6},{5,7},{6,4},{7,5},{8,10},{9,11},{10,... | collective-permute-start | bytes 1179656 | tf_op jit(solution)/shard_map/ppermute | solution.py:272
  24.3 1.1 %copy-start.2 = (bf16[64,4352]{1,0:T(8,128)(2,1)S(1)}, bf16[64,4352]{1,0:T(8,128)(2,1)}, u32[]{:S(2)}) copy-start(bf16[64,4352]{1,0:T(8,128)(2,1)} %get-tuple-element.27.refs_1_.refs_0_) | copy-start | bytes 1671172
  25.4 2.2 %copy-start = (bf16[1,128,64,256]{3,2,1,0:T(8,128)(2,1)S(1)}, bf16[1,128,64,256]{3,2,1,0:T(8,128)(2,1)}, u32[]{:S(2)}) copy-start(bf16[1,128,64,256]{3,2,1,0:T(8,128)(2,1)} %param.15) | copy-start | bytes 12582916
  25.4 2.9 %copy-start.1 = (bf16[128,64,128]{2,1,0:T(8,128)(2,1)S(1)}, bf16[128,64,128]{2,1,0:T(8,128)(2,1)}, u32[]{:S(2)}) copy-start(bf16[128,64,128]{2,1,0:T(8,128)(2,1)} %refs_6_.1) | copy-start | bytes 6291460
  25.4 2.9 %copy-start.3 = (f32[1,3,64,128]{3,2,1,0:T(8,128)S(1)}, f32[1,3,64,128]{3,2,1,0:T(8,128)}, u32[]{:S(2)}) copy-start(f32[1,3,64,128]{3,2,1,0:T(8,128)} %param.14) | copy-start | bytes 294916
  34.0 3.1 %collective-permute-start.12 = (bf16[4,32,2048]{2,1,0:T(8,128)(2,1)S(1)}, bf16[4,32,2048]{2,1,0:T(8,128)(2,1)S(1)}, u32[]{:S(2)}, u32[]{:S(2)}) collective-permute-start(bf16[4,32,2048]{2,1,0:T(8,128)(2,1)S(1)} %get-tuple-element.37), channel_id=1, source_target_pairs={{0,4},{4,0},{8,12},{12,8},{16,20},{20,16},{24,28},{28,24},{1,5},{5... | collective-permute-start | bytes 1572872 | tf_op jit(solution)/shard_map/ppermute | solution.py:272
  35.6 3.0 %collective-permute-start.5 = (bf16[4,32,2048]{2,1,0:T(8,128)(2,1)S(1)}, bf16[4,32,2048]{2,1,0:T(8,128)(2,1)S(1)}, u32[]{:S(2)}, u32[]{:S(2)}) collective-permute-start(bf16[4,32,2048]{2,1,0:T(8,128)(2,1)S(1)} %get-tuple-element.31), channel_id=1, source_target_pairs={{0,4},{4,0},{8,12},{12,8},{16,20},{20,16},{24,28},{28,24},{1,5},{5... | collective-permute-start | bytes 1572872 | tf_op jit(solution)/shard_map/ppermute | solution.py:272
  37.2 4.8 %collective-permute-start.13 = (bf16[32,2048]{1,0:T(8,128)(2,1)S(1)}, bf16[32,2048]{1,0:T(8,128)(2,1)S(1)}, u32[]{:S(2)}, u32[]{:S(2)}) collective-permute-start(bf16[32,2048]{1,0:T(8,128)(2,1)S(1)} %get-tuple-element.40), channel_id=1, source_target_pairs={{0,8},{4,12},{8,0},{12,4},{16,24},{20,28},{24,16},{28,20},{1,9},{5... | collective-permute-start | bytes 393224 | tf_op jit(solution)/shard_map/ppermute | solution.py:272
  38.6 7.0 %collective-permute-start.6 = (bf16[32,2048]{1,0:T(8,128)(2,1)S(1)}, bf16[32,2048]{1,0:T(8,128)(2,1)S(1)}, u32[]{:S(2)}, u32[]{:S(2)}) collective-permute-start(bf16[32,2048]{1,0:T(8,128)(2,1)S(1)} %get-tuple-element.34), channel_id=1, source_target_pairs={{0,8},{4,12},{8,0},{12,4},{16,24},{20,28},{24,16},{28,20},{1,9},{5... | collective-permute-start | bytes 393224 | tf_op jit(solution)/shard_map/ppermute | solution.py:272
  42.0 6.9 %collective-permute-start.14 = (bf16[32,2048]{1,0:T(8,128)(2,1)S(1)}, bf16[32,2048]{1,0:T(8,128)(2,1)S(1)}, u32[]{:S(2)}, u32[]{:S(2)}) collective-permute-start(bf16[32,2048]{1,0:T(8,128)(2,1)S(1)} %add_convert_fusion.1), channel_id=1, source_target_pairs={{0,16},{4,20},{8,24},{12,28},{16,0},{20,4},{24,8},{28,12},{1,17},{... | collective-permute-start | bytes 393224 | tf_op jit(solution)/shard_map/ppermute | solution.py:272
  44.4 4.5 %collective-permute-start.15 = (bf16[32,2048]{1,0:T(8,128)(2,1)S(1)}, bf16[32,2048]{1,0:T(8,128)(2,1)S(1)}, u32[]{:S(2)}, u32[]{:S(2)}) collective-permute-start(bf16[32,2048]{1,0:T(8,128)(2,1)S(1)} %get-tuple-element.42), channel_id=1, source_target_pairs={{0,8},{4,12},{8,0},{12,4},{16,24},{20,28},{24,16},{28,20},{1,9},{5... | collective-permute-start | bytes 393224 | tf_op jit(solution)/shard_map/ppermute | solution.py:272
  45.7 12.9 %collective-permute-start.7 = (bf16[32,2048]{1,0:T(8,128)(2,1)S(1)}, bf16[32,2048]{1,0:T(8,128)(2,1)S(1)}, u32[]{:S(2)}, u32[]{:S(2)}) collective-permute-start(bf16[32,2048]{1,0:T(8,128)(2,1)S(1)} %add_convert_fusion.3), channel_id=1, source_target_pairs={{0,16},{4,20},{8,24},{12,28},{16,0},{20,4},{24,8},{28,12},{1,17},{... | collective-permute-start | bytes 393224 | tf_op jit(solution)/shard_map/ppermute | solution.py:272
  47.2 11.4 %collective-permute-start.8 = (bf16[32,2048]{1,0:T(8,128)(2,1)S(1)}, bf16[32,2048]{1,0:T(8,128)(2,1)S(1)}, u32[]{:S(2)}, u32[]{:S(2)}) collective-permute-start(bf16[32,2048]{1,0:T(8,128)(2,1)S(1)} %get-tuple-element.36), channel_id=1, source_target_pairs={{0,8},{4,12},{8,0},{12,4},{16,24},{20,28},{24,16},{28,20},{1,9},{5... | collective-permute-start | bytes 393224 | tf_op jit(solution)/shard_map/ppermute | solution.py:272
  48.9 11.7 %collective-permute-start.17 = (bf16[32,2048]{1,0:T(8,128)(2,1)S(1)}, bf16[32,2048]{1,0:T(8,128)(2,1)S(1)}, u32[]{:S(2)}, u32[]{:S(2)}) collective-permute-start(bf16[32,2048]{1,0:T(8,128)(2,1)S(1)} %add_convert_fusion.refs_0_), channel_id=1, source_target_pairs={{0,16},{4,20},{8,24},{12,28},{16,0},{20,4},{24,8},{28,12},{1,17},{... | collective-permute-start | bytes 393224 | tf_op jit(solution)/shard_map/ppermute | solution.py:272
  52.0 12.2 %collective-permute-start.16 = (bf16[32,2048]{1,0:T(8,128)(2,1)S(1)}, bf16[32,2048]{1,0:T(8,128)(2,1)S(1)}, u32[]{:S(2)}, u32[]{:S(2)}) collective-permute-start(bf16[32,2048]{1,0:T(8,128)(2,1)S(1)} %add_convert_fusion.refs_0_), channel_id=1, source_target_pairs={{0,8},{4,12},{8,0},{12,4},{16,24},{20,28},{24,16},{28,20},{1,9},{5... | collective-permute-start | bytes 393224 | tf_op jit(solution)/shard_map/ppermute | solution.py:272
  54.9 9.5 %collective-permute-start.19 = (bf16[32,2048]{1,0:T(8,128)(2,1)S(1)}, bf16[32,2048]{1,0:T(8,128)(2,1)S(1)}, u32[]{:S(2)}, u32[]{:S(2)}) collective-permute-start(bf16[32,2048]{1,0:T(8,128)(2,1)S(1)} %add_convert_fusion.refs_0_), channel_id=1, source_target_pairs={{0,4},{4,0},{8,12},{12,8},{16,20},{20,16},{24,28},{28,24},{1,5},{5... | collective-permute-start | bytes 393224 | tf_op jit(solution)/shard_map/ppermute | solution.py:272
  58.6 8.6 %collective-permute-start.23 = (bf16[32,2048]{1,0:T(8,128)(2,1)S(1)}, bf16[32,2048]{1,0:T(8,128)(2,1)S(1)}, u32[]{:S(2)}, u32[]{:S(2)}) collective-permute-start(bf16[32,2048]{1,0:T(8,128)(2,1)S(1)} %add_convert_fusion.2.refs_8_), channel_id=1, source_target_pairs={{0,8},{4,12},{8,0},{12,4},{16,24},{20,28},{24,16},{28,20},{1,9},{5... | collective-permute-start | bytes 393224 | tf_op jit(solution)/shard_map/ppermute | solution.py:272
  58.7 11.5 %collective-permute-start.9 = (bf16[32,2048]{1,0:T(8,128)(2,1)S(1)}, bf16[32,2048]{1,0:T(8,128)(2,1)S(1)}, u32[]{:S(2)}, u32[]{:S(2)}) collective-permute-start(bf16[32,2048]{1,0:T(8,128)(2,1)S(1)} %add_convert_fusion.2.refs_8_), channel_id=1, source_target_pairs={{0,16},{4,20},{8,24},{12,28},{16,0},{20,4},{24,8},{28,12},{1,17},{... | collective-permute-start | bytes 393224 | tf_op jit(solution)/shard_map/ppermute | solution.py:272
  60.6 9.6 %collective-permute-start.24 = (bf16[32,2048]{1,0:T(8,128)(2,1)S(1)}, bf16[32,2048]{1,0:T(8,128)(2,1)S(1)}, u32[]{:S(2)}, u32[]{:S(2)}) collective-permute-start(bf16[32,2048]{1,0:T(8,128)(2,1)S(1)} %add_convert_fusion.2.refs_8_), channel_id=1, source_target_pairs={{0,4},{4,0},{8,12},{12,8},{16,20},{20,16},{24,28},{28,24},{1,5},{5... | collective-permute-start | bytes 393224 | tf_op jit(solution)/shard_map/ppermute | solution.py:272
  64.2 7.9 %collective-permute-start.18 = (bf16[32,2048]{1,0:T(8,128)(2,1)S(1)}, bf16[32,2048]{1,0:T(8,128)(2,1)S(1)}, u32[]{:S(2)}, u32[]{:S(2)}) collective-permute-start(bf16[32,2048]{1,0:T(8,128)(2,1)S(1)} %collective-permute-done.17.refs_2_), channel_id=1, source_target_pairs={{0,8},{4,12},{8,0},{12,4},{16,24},{20,28},{24,16},{28,20},{1,9},{5... | collective-permute-start | bytes 393224 | tf_op jit(solution)/shard_map/ppermute | solution.py:272
  64.4 7.8 %collective-permute-start.20 = (bf16[32,2048]{1,0:T(8,128)(2,1)S(1)}, bf16[32,2048]{1,0:T(8,128)(2,1)S(1)}, u32[]{:S(2)}, u32[]{:S(2)}) collective-permute-start(bf16[32,2048]{1,0:T(8,128)(2,1)S(1)} %collective-permute-done.16.refs_1_), channel_id=1, source_target_pairs={{0,4},{4,0},{8,12},{12,8},{16,20},{20,16},{24,28},{28,24},{1,5},{5... | collective-permute-start | bytes 393224 | tf_op jit(solution)/shard_map/ppermute | solution.py:272
  67.2 8.9 %collective-permute-start.21 = (bf16[32,2048]{1,0:T(8,128)(2,1)S(1)}, bf16[32,2048]{1,0:T(8,128)(2,1)S(1)}, u32[]{:S(2)}, u32[]{:S(2)}) collective-permute-start(bf16[32,2048]{1,0:T(8,128)(2,1)S(1)} %collective-permute-done.17.refs_2_), channel_id=1, source_target_pairs={{0,4},{4,0},{8,12},{12,8},{16,20},{20,16},{24,28},{28,24},{1,5},{5... | collective-permute-start | bytes 393224 | tf_op jit(solution)/shard_map/ppermute | solution.py:272
  70.2 5.1 %collective-permute-start.10 = (bf16[32,2048]{1,0:T(8,128)(2,1)S(1)}, bf16[32,2048]{1,0:T(8,128)(2,1)S(1)}, u32[]{:S(2)}, u32[]{:S(2)}) collective-permute-start(bf16[32,2048]{1,0:T(8,128)(2,1)S(1)} %collective-permute-done.9.refs_10_), channel_id=1, source_target_pairs={{0,8},{4,12},{8,0},{12,4},{16,24},{20,28},{24,16},{28,20},{1,9},{5... | collective-permute-start | bytes 393224 | tf_op jit(solution)/shard_map/ppermute | solution.py:272
  70.2 5.9 %collective-permute-start.26 = (bf16[32,2048]{1,0:T(8,128)(2,1)S(1)}, bf16[32,2048]{1,0:T(8,128)(2,1)S(1)}, u32[]{:S(2)}, u32[]{:S(2)}) collective-permute-start(bf16[32,2048]{1,0:T(8,128)(2,1)S(1)} %collective-permute-done.9.refs_10_), channel_id=1, source_target_pairs={{0,4},{4,0},{8,12},{12,8},{16,20},{20,16},{24,28},{28,24},{1,5},{5... | collective-permute-start | bytes 393224 | tf_op jit(solution)/shard_map/ppermute | solution.py:272
  72.1 4.0 %collective-permute-start.25 = (bf16[32,2048]{1,0:T(8,128)(2,1)S(1)}, bf16[32,2048]{1,0:T(8,128)(2,1)S(1)}, u32[]{:S(2)}, u32[]{:S(2)}) collective-permute-start(bf16[32,2048]{1,0:T(8,128)(2,1)S(1)} %collective-permute-done.23.refs_9_), channel_id=1, source_target_pairs={{0,4},{4,0},{8,12},{12,8},{16,20},{20,16},{24,28},{28,24},{1,5},{5... | collective-permute-start | bytes 393224 | tf_op jit(solution)/shard_map/ppermute | solution.py:272
  72.2 4.0 %collective-permute-start.22 = (bf16[32,2048]{1,0:T(8,128)(2,1)S(1)}, bf16[32,2048]{1,0:T(8,128)(2,1)S(1)}, u32[]{:S(2)}, u32[]{:S(2)}) collective-permute-start(bf16[32,2048]{1,0:T(8,128)(2,1)S(1)} %collective-permute-done.18.refs_3_), channel_id=1, source_target_pairs={{0,4},{4,0},{8,12},{12,8},{16,20},{20,16},{24,28},{28,24},{1,5},{5... | collective-permute-start | bytes 393224 | tf_op jit(solution)/shard_map/ppermute | solution.py:272
  75.3 2.2 %collective-permute-start.11 = (bf16[32,2048]{1,0:T(8,128)(2,1)S(1)}, bf16[32,2048]{1,0:T(8,128)(2,1)S(1)}, u32[]{:S(2)}, u32[]{:S(2)}) collective-permute-start(bf16[32,2048]{1,0:T(8,128)(2,1)S(1)} %collective-permute-done.10.refs_0_), channel_id=1, source_target_pairs={{0,4},{4,0},{8,12},{12,8},{16,20},{20,16},{24,28},{28,24},{1,5},{5... | collective-permute-start | bytes 393224 | tf_op jit(solution)/shard_map/ppermute | solution.py:272

commit v6 on v5

--- a/solution.py
+++ b/solution.py
@@ -8,10 +8,10 @@
 from jax.experimental.pallas import tpu as pltpu
 from jax.sharding import PartitionSpec as P
 
-STEP = 8
-HEAD = 8
+STEP = 32
+HEAD = 4
 FIRST_HEAD = 32
-FAR_PIECES = 2
+FAR_PIECES = 4
 HALVES = 2
 NEAR_VMEM = 60
 F32, BF16 = jnp.float32, jnp.bfloat16
@@ -253,7 +253,7 @@
         copy.wait()
 
 
-def place(masks, me, parts, count, out=None):
+def place(masks, me, parts, count, out, early):
     rows, width = parts[0].shape
     return pl.pallas_call(
         functools.partial(place_kernel, masks),
@@ -262,7 +262,7 @@
         out_specs=ANY,
         scratch_shapes=[pltpu.SemaphoreType.DMA((len(parts),))],
         input_output_aliases={} if out is None else {len(parts) + 1: 0},
-        cost_estimate=LONG if out is None else None,
+        cost_estimate=LONG if early else None,
         compiler_params=pltpu.CompilerParams(vmem_limit_bytes=16 * 2**20),
     )(me, *parts, *(() if out is None else (out,)))
 
@@ -361,10 +361,12 @@
         parts += [((half, 2 * m), q) for m, q in zip(owners, mine)]
         parts += [((half, 2 * m + 1), swap(q, "src", 1)) for m, q in zip(owners, mine)]
     last = parts[-len(owners) - 1], parts[-1]
+    each = 2 * len(owners)
+    steps = [parts[:-each], [part for part in parts[-each:] if part[0] not in dict(last)], last]
     out = None
-    for some in ([part for part in parts if part[0] not in (last[0][0], last[1][0])], last):
+    for some in steps:
         spots, values = zip(*some)
-        out = place(spots, me, values, sources, out)
+        out = place(spots, me, values, sources, out, some is not last)
     return out.T
 
 

time: 78.5 us -> 76.7 us (0.977)
  starting transfers between devices: 40.6 us -> 38.4 us
  waiting for transfers between devices: 13.8 us -> 15 us
    ppermute x27, starting transfers between devices: 40.6 us -> 38.4 us  [swap(): return lax.ppermute(value, axis, [(i, i ^ mask) for i in range(size)])]
    pallas_call x2, Pallas kernels: 11.1 us -> 9.88 us  [near_products(): pl.pallas_call(functools.partial(near_kernel, parts), out_shape=[jax.Shap...]
    ppermute x27, waiting for transfers between devices: 13.8 us -> 15 us  [swap(): return lax.ppermute(value, axis, [(i, i ^ mask) for i in range(size)])]
    pallas_call x2 -> x3, Pallas kernels: 2.06 us -> 2.68 us  [place(): pl.pallas_call(functools.partial(place_kernel, masks), out_shape=jax.Shap...]
  transfers between devices with their start and end apart: 27 -> 27, of which waited for: 7 -> 10; matrix products, arithmetic and copies ran while one was open for 1% -> 2% of each run, Pallas kernels for 17% -> 17%
where the time goes in v6:
time: 76.7 us; the launch traced here: 76.4 us
  starting transfers between devices  38.4 us (50%)
  Pallas kernels  19.3 us (25%)
  waiting for transfers between devices  15 us (20%)
  local copies, waits for them, and re-layouts  3.44 us (4%)
    ppermute x27, starting transfers between devices, swap(): return lax.ppermute(value, axis, [(i, i ^ mask) for i in range(size)])  38.4 us
    ppermute x27, waiting for transfers between devices, swap(): return lax.ppermute(value, axis, [(i, i ^ mask) for i in range(size)])  15 us
    pallas_call x2, Pallas kernels, near_products(): pl.pallas_call(functools.partial(near_kernel, parts), out_shape=[jax.Shap...  9.88 us
    pallas_call x1, Pallas kernels, far_field(): pl.pallas_call(functools.partial(far_kernel, groups, count), out_shape=ja...  3.89 us
    pallas_call x3, Pallas kernels, place(): pl.pallas_call(functools.partial(place_kernel, masks), out_shape=jax.Shap...  2.68 us
    unnamed x11, local copies, waits for them, and re-layouts  2.64 us
  transfers between devices with their start and end apart: 27, of which 10 were waited for; matrix products, arithmetic and copies ran while one was open for 2% of the time, Pallas kernels for 17%

profile of v6, /device:TPU:1, one launch (start us, length us, event | category | flops | bytes accessed | tf_op | source)
XLA Modules:
  0.0 76.4 jit_solution(16422927096515790841)
XLA Ops:
  0.0 4.0 %shard_map.91 = bf16[64,4352]{1,0:T(8,128)(2,1)} custom-call(s32[1]{0:T(128)} %bitcast.1.me_ref, s32[128]{0:T(128)} %src_ref.3, s32[1,128]{1,0:T(1,128)} %bitcast.11, bf16[64,2048]{1,0:T(8,128)(2,1)} %bitcast.9, bf16[16,64,128]{2,1,0:T(8,128)(2,1)} %basis_ref.3, bf16[128,128,128]{2,1,0:T(8,128)(2,1)} %tiles_ref.3), custom_call_target="tpu_custom_call" | custom-call | tf_op jit(solution)/shard_map/pallas_call | solution.py:94
  4.0 3.1 %collective-permute-start.2 = (bf16[64,4352]{1,0:T(8,128)(2,1)}, bf16[64,4352]{1,0:T(8,128)(2,1)S(1)}, u32[]{:S(2)}, u32[]{:S(2)}) collective-permute-start(bf16[64,4352]{1,0:T(8,128)(2,1)} %shard_map.91), channel_id=1, source_target_pairs={{0,3},{1,2},{2,1},{3,0},{4,7},{5,6},{6,5},{7,4},{8,11},{9,10},{10,... | collective-permute-start | bytes 1671176 | tf_op jit(solution)/shard_map/ppermute | solution.py:272
  7.1 5.9 %shard_map.92 = (bf16[64,768]{1,0:T(8,128)(2,1)}, bf16[64,768]{1,0:T(8,128)(2,1)}, bf16[64,4352]{1,0:T(8,128)(2,1)}, bf16[64,3584]{1,0:T(8,128)(2,1)}, bf16[64,3584]{1,0:T(8,128)(2,1)}) custom-call(s32[1]{0:T(128)} %bitcast.1.me_ref, s32[128]{0:T(128)} %src_ref.3, s32[1,128]{1,0:T(1,128)} %bitcast.12, bf16[64,2048]{1,0:T(8,128)(2,1)} %bitcast.10, ...), custom_call_target="tpu_custom_call" | custom-call | tf_op jit(solution)/shard_map/pallas_call | solution.py:94
  13.3 1.4 %collective-permute-start.3 = (bf16[64,3584]{1,0:T(8,128)(2,1)}, bf16[64,3584]{1,0:T(8,128)(2,1)S(1)}, u32[]{:S(2)}, u32[]{:S(2)}) collective-permute-start(bf16[64,3584]{1,0:T(8,128)(2,1)} %get-tuple-element.28), channel_id=1, source_target_pairs={{0,1},{1,0},{2,3},{3,2},{4,5},{5,4},{6,7},{7,6},{8,9},{9,8},{10,11... | collective-permute-start | bytes 1376264 | tf_op jit(solution)/shard_map/ppermute | solution.py:272
  14.7 1.2 %collective-permute-start.4 = (bf16[64,3584]{1,0:T(8,128)(2,1)}, bf16[64,3584]{1,0:T(8,128)(2,1)S(1)}, u32[]{:S(2)}, u32[]{:S(2)}) collective-permute-start(bf16[64,3584]{1,0:T(8,128)(2,1)} %get-tuple-element.29), channel_id=1, source_target_pairs={{0,2},{1,3},{2,0},{3,1},{4,6},{5,7},{6,4},{7,5},{8,10},{9,11},{10,... | collective-permute-start | bytes 1376264 | tf_op jit(solution)/shard_map/ppermute | solution.py:272
  16.9 4.8 %collective-permute-done.refs_1_.refs_0_ = bf16[64,768]{1,0:T(8,128)(2,1)S(1)} collective-permute-done((bf16[64,768]{1,0:T(8,128)(2,1)}, bf16[64,768]{1,0:T(8,128)(2,1)S(1)}, u32[]{:S(2)}, u32[]{:S(2)}) %collective-permute-start) | collective-permute-done | bytes 98336 | tf_op jit(solution)/shard_map/ppermute | solution.py:272
  22.5 1.0 %copy-done.2 = bf16[64,4352]{1,0:T(8,128)(2,1)S(1)} copy-done((bf16[64,4352]{1,0:T(8,128)(2,1)S(1)}, bf16[64,4352]{1,0:T(8,128)(2,1)}, u32[]{:S(2)}) %copy-start.2) | copy-done | bytes 557080
  23.6 1.4 %shard_map.93.refs_7_ = f32[8,64,2048]{2,1,0:T(8,128)S(1)} custom-call(s32[1]{0:T(128)} %bitcast.1.me_ref, s32[2,128]{1,0:T(2,128)S(1)} %convert_convert_fusion.1.tgt_ref, bf16[64,4352]{1,0:T(8,128)(2,1)S(1)} %collective-permute-done.2.refs_0_.refs_3_, bf16[64,4352]{1,0:T(8,128)(2,1)S(1)} %copy-done.2), custom_call_target="tpu_custom_call" | custom-call | flops 68719476736 | bytes 16777216 | tf_op jit(solution)/shard_map/pallas_call | solution.py:128
  25.0 0.8 %copy-done = bf16[1,128,64,256]{3,2,1,0:T(8,128)(2,1)S(1)} copy-done((bf16[1,128,64,256]{3,2,1,0:T(8,128)(2,1)S(1)}, bf16[1,128,64,256]{3,2,1,0:T(8,128)(2,1)}, u32[]{:S(2)}) %copy-start) | copy-done | bytes 4194328
  26.5 3.9 %shard_map.94.far_ref = f32[8,64,2048]{2,1,0:T(8,128)S(1)} custom-call(s32[1]{0:T(128)} %bitcast.1.me_ref, s32[512]{0:T(512)S(1)} %reshape_squeeze.3.node_ref, bf16[64,4352]{1,0:T(8,128)(2,1)S(1)} %copy-done.2, bf16[64,768]{1,0:T(8,128)(2,1)S(1)} %collective-permute-done.refs_1_.refs_0_, ...), custom_call_target="tpu_custom_call", output_to_operand_aliasing={{}: (9, {})} | custom-call | tf_op jit(solution)/shard_map/pallas_call | solution.py:183
  30.4 1.2 %collective-permute-done.3.refs_2_ = bf16[64,3584]{1,0:T(8,128)(2,1)S(1)} collective-permute-done((bf16[64,3584]{1,0:T(8,128)(2,1)}, bf16[64,3584]{1,0:T(8,128)(2,1)S(1)}, u32[]{:S(2)}, u32[]{:S(2)}) %collective-permute-start.3) | collective-permute-done | bytes 458784 | tf_op jit(solution)/shard_map/ppermute | solution.py:272
  32.3 1.3 %shard_map.95 = (f32[8,64,2048]{2,1,0:T(8,128)S(1)}, bf16[4,32,2048]{2,1,0:T(8,128)(2,1)S(1)}, bf16[4,32,2048]{2,1,0:T(8,128)(2,1)S(1)}) custom-call(s32[2]{0:T(128)S(1)} %pad_add_fusion.me_ref, s32[4,128]{1,0:T(4,128)S(1)} %convert_convert_fusion.tgt_ref, f32[8,64,2048]{2,1,0:T(8,128)S(1)} %shard_map.94.far_ref, ...), custom_call_target="tpu_custom_call", output_to_operand_aliasing={{0}: (2, {})} | custom-call | tf_op jit(solution)/shard_map/pallas_call | solution.py:211
  33.6 0.9 %collective-permute-start.16 = (bf16[4,32,2048]{2,1,0:T(8,128)(2,1)S(1)}, bf16[4,32,2048]{2,1,0:T(8,128)(2,1)S(1)}, u32[]{:S(2)}, u32[]{:S(2)}) collective-permute-start(bf16[4,32,2048]{2,1,0:T(8,128)(2,1)S(1)} %get-tuple-element.37), channel_id=1, source_target_pairs={{0,4},{4,0},{8,12},{12,8},{16,20},{20,16},{24,28},{28,24},{1,5},{5... | collective-permute-start | bytes 1572872 | tf_op jit(solution)/shard_map/ppermute | solution.py:272
  34.5 1.5 %collective-permute-done.16.got_ref = bf16[4,32,2048]{2,1,0:T(8,128)(2,1)S(1)} collective-permute-done((bf16[4,32,2048]{2,1,0:T(8,128)(2,1)S(1)}, bf16[4,32,2048]{2,1,0:T(8,128)(2,1)S(1)}, u32[]{:S(2)}, u32[]{:S(2)}) %collective-permute-start.16) | collective-permute-done | bytes 524320 | tf_op jit(solution)/shard_map/ppermute | solution.py:272
  36.0 1.4 %collective-permute-start.17 = (bf16[32,2048]{1,0:T(8,128)(2,1)S(1)}, bf16[32,2048]{1,0:T(8,128)(2,1)S(1)}, u32[]{:S(2)}, u32[]{:S(2)}) collective-permute-start(bf16[32,2048]{1,0:T(8,128)(2,1)S(1)} %get-tuple-element.40), channel_id=1, source_target_pairs={{0,8},{4,12},{8,0},{12,4},{16,24},{20,28},{24,16},{28,20},{1,9},{5... | collective-permute-start | bytes 393224 | tf_op jit(solution)/shard_map/ppermute | solution.py:272
  38.2 2.7 %collective-permute-done.17 = bf16[32,2048]{1,0:T(8,128)(2,1)S(1)} collective-permute-done((bf16[32,2048]{1,0:T(8,128)(2,1)S(1)}, bf16[32,2048]{1,0:T(8,128)(2,1)S(1)}, u32[]{:S(2)}, u32[]{:S(2)}) %collective-permute-start.17) | collective-permute-done | bytes 131104 | tf_op jit(solution)/shard_map/ppermute | solution.py:272
  40.9 2.4 %collective-permute-start.18 = (bf16[32,2048]{1,0:T(8,128)(2,1)S(1)}, bf16[32,2048]{1,0:T(8,128)(2,1)S(1)}, u32[]{:S(2)}, u32[]{:S(2)}) collective-permute-start(bf16[32,2048]{1,0:T(8,128)(2,1)S(1)} %add_convert_fusion.1), channel_id=1, source_target_pairs={{0,16},{4,20},{8,24},{12,28},{16,0},{20,4},{24,8},{28,12},{1,17},{... | collective-permute-start | bytes 393224 | tf_op jit(solution)/shard_map/ppermute | solution.py:272
  43.2 1.3 %collective-permute-start.19 = (bf16[32,2048]{1,0:T(8,128)(2,1)S(1)}, bf16[32,2048]{1,0:T(8,128)(2,1)S(1)}, u32[]{:S(2)}, u32[]{:S(2)}) collective-permute-start(bf16[32,2048]{1,0:T(8,128)(2,1)S(1)} %get-tuple-element.42), channel_id=1, source_target_pairs={{0,8},{4,12},{8,0},{12,4},{16,24},{20,28},{24,16},{28,20},{1,9},{5... | collective-permute-start | bytes 393224 | tf_op jit(solution)/shard_map/ppermute | solution.py:272
  44.6 1.5 %collective-permute-start.7 = (bf16[32,2048]{1,0:T(8,128)(2,1)S(1)}, bf16[32,2048]{1,0:T(8,128)(2,1)S(1)}, u32[]{:S(2)}, u32[]{:S(2)}) collective-permute-start(bf16[32,2048]{1,0:T(8,128)(2,1)S(1)} %add_convert_fusion.3), channel_id=1, source_target_pairs={{0,16},{4,20},{8,24},{12,28},{16,0},{20,4},{24,8},{28,12},{1,17},{... | collective-permute-start | bytes 393224 | tf_op jit(solution)/shard_map/ppermute | solution.py:272
  46.0 1.3 %collective-permute-start.8 = (bf16[32,2048]{1,0:T(8,128)(2,1)S(1)}, bf16[32,2048]{1,0:T(8,128)(2,1)S(1)}, u32[]{:S(2)}, u32[]{:S(2)}) collective-permute-start(bf16[32,2048]{1,0:T(8,128)(2,1)S(1)} %get-tuple-element.36), channel_id=1, source_target_pairs={{0,8},{4,12},{8,0},{12,4},{16,24},{20,28},{24,16},{28,20},{1,9},{5... | collective-permute-start | bytes 393224 | tf_op jit(solution)/shard_map/ppermute | solution.py:272
  47.8 3.1 %collective-permute-start.21 = (bf16[32,2048]{1,0:T(8,128)(2,1)S(1)}, bf16[32,2048]{1,0:T(8,128)(2,1)S(1)}, u32[]{:S(2)}, u32[]{:S(2)}) collective-permute-start(bf16[32,2048]{1,0:T(8,128)(2,1)S(1)} %add_convert_fusion.refs_0_), channel_id=1, source_target_pairs={{0,16},{4,20},{8,24},{12,28},{16,0},{20,4},{24,8},{28,12},{1,17},{... | collective-permute-start | bytes 393224 | tf_op jit(solution)/shard_map/ppermute | solution.py:272
  50.9 2.9 %collective-permute-start.20 = (bf16[32,2048]{1,0:T(8,128)(2,1)S(1)}, bf16[32,2048]{1,0:T(8,128)(2,1)S(1)}, u32[]{:S(2)}, u32[]{:S(2)}) collective-permute-start(bf16[32,2048]{1,0:T(8,128)(2,1)S(1)} %add_convert_fusion.refs_0_), channel_id=1, source_target_pairs={{0,8},{4,12},{8,0},{12,4},{16,24},{20,28},{24,16},{28,20},{1,9},{5... | collective-permute-start | bytes 393224 | tf_op jit(solution)/shard_map/ppermute | solution.py:272
  53.8 3.6 %collective-permute-start.23 = (bf16[32,2048]{1,0:T(8,128)(2,1)S(1)}, bf16[32,2048]{1,0:T(8,128)(2,1)S(1)}, u32[]{:S(2)}, u32[]{:S(2)}) collective-permute-start(bf16[32,2048]{1,0:T(8,128)(2,1)S(1)} %add_convert_fusion.refs_0_), channel_id=1, source_target_pairs={{0,4},{4,0},{8,12},{12,8},{16,20},{20,16},{24,28},{28,24},{1,5},{5... | collective-permute-start | bytes 393224 | tf_op jit(solution)/shard_map/ppermute | solution.py:272
  57.7 1.3 %collective-permute-done.21.refs_2_ = bf16[32,2048]{1,0:T(8,128)(2,1)S(1)} collective-permute-done((bf16[32,2048]{1,0:T(8,128)(2,1)S(1)}, bf16[32,2048]{1,0:T(8,128)(2,1)S(1)}, u32[]{:S(2)}, u32[]{:S(2)}) %collective-permute-start.21) | collective-permute-done | bytes 131104 | tf_op jit(solution)/shard_map/ppermute | solution.py:272
  59.5 1.0 %collective-permute-start.12 = (bf16[32,2048]{1,0:T(8,128)(2,1)S(1)}, bf16[32,2048]{1,0:T(8,128)(2,1)S(1)}, u32[]{:S(2)}, u32[]{:S(2)}) collective-permute-start(bf16[32,2048]{1,0:T(8,128)(2,1)S(1)} %add_convert_fusion.2.refs_0_), channel_id=1, source_target_pairs={{0,8},{4,12},{8,0},{12,4},{16,24},{20,28},{24,16},{28,20},{1,9},{5... | collective-permute-start | bytes 393224 | tf_op jit(solution)/shard_map/ppermute | solution.py:272
  60.8 4.5 %collective-permute-start.24 = (bf16[32,2048]{1,0:T(8,128)(2,1)S(1)}, bf16[32,2048]{1,0:T(8,128)(2,1)S(1)}, u32[]{:S(2)}, u32[]{:S(2)}) collective-permute-start(bf16[32,2048]{1,0:T(8,128)(2,1)S(1)} %collective-permute-done.20.refs_1_), channel_id=1, source_target_pairs={{0,4},{4,0},{8,12},{12,8},{16,20},{20,16},{24,28},{28,24},{1,5},{5... | collective-permute-start | bytes 393224 | tf_op jit(solution)/shard_map/ppermute | solution.py:272
  65.3 1.3 %collective-permute-done.9.refs_2_ = bf16[32,2048]{1,0:T(8,128)(2,1)S(1)} collective-permute-done((bf16[32,2048]{1,0:T(8,128)(2,1)S(1)}, bf16[32,2048]{1,0:T(8,128)(2,1)S(1)}, u32[]{:S(2)}, u32[]{:S(2)}) %collective-permute-start.9) | collective-permute-done | bytes 131104 | tf_op jit(solution)/shard_map/ppermute | solution.py:272
  67.1 2.4 %collective-permute-start.26 = (bf16[32,2048]{1,0:T(8,128)(2,1)S(1)}, bf16[32,2048]{1,0:T(8,128)(2,1)S(1)}, u32[]{:S(2)}, u32[]{:S(2)}) collective-permute-start(bf16[32,2048]{1,0:T(8,128)(2,1)S(1)} %collective-permute-done.22.refs_3_), channel_id=1, source_target_pairs={{0,4},{4,0},{8,12},{12,8},{16,20},{20,16},{24,28},{28,24},{1,5},{5... | collective-permute-start | bytes 393224 | tf_op jit(solution)/shard_map/ppermute | solution.py:272
  69.5 2.5 %collective-permute-start.13 = (bf16[32,2048]{1,0:T(8,128)(2,1)S(1)}, bf16[32,2048]{1,0:T(8,128)(2,1)S(1)}, u32[]{:S(2)}, u32[]{:S(2)}) collective-permute-start(bf16[32,2048]{1,0:T(8,128)(2,1)S(1)} %add_convert_fusion.2.refs_0_), channel_id=1, source_target_pairs={{0,4},{4,0},{8,12},{12,8},{16,20},{20,16},{24,28},{28,24},{1,5},{5... | collective-permute-start | bytes 393224 | tf_op jit(solution)/shard_map/ppermute | solution.py:272
  72.5 1.2 %collective-permute-start.11 = (bf16[32,2048]{1,0:T(8,128)(2,1)S(1)}, bf16[32,2048]{1,0:T(8,128)(2,1)S(1)}, u32[]{:S(2)}, u32[]{:S(2)}) collective-permute-start(bf16[32,2048]{1,0:T(8,128)(2,1)S(1)} %collective-permute-done.10.refs_0_), channel_id=1, source_target_pairs={{0,4},{4,0},{8,12},{12,8},{16,20},{20,16},{24,28},{28,24},{1,5},{5... | collective-permute-start | bytes 393224 | tf_op jit(solution)/shard_map/ppermute | solution.py:272
  73.7 1.0 %shard_map.98.refs_6_ = bf16[64,16384]{1,0:T(8,128)(2,1)} custom-call(s32[1]{0:T(128)} %bitcast.me_ref, bf16[32,2048]{1,0:T(8,128)(2,1)S(1)} %add_convert_fusion.refs_0_, bf16[32,2048]{1,0:T(8,128)(2,1)S(1)} %collective-permute-done.20.refs_1_, bf16[32,2048]{1,0:T(8,128)(2,1)S(1)} %collective-permute-done.21.refs_2_, ...), custom_call_target="tpu_custom_call" | custom-call | flops 68719476736 | bytes 16777216 | tf_op jit(solution)/shard_map/pallas_call | solution.py:258
  74.8 0.9 %shard_map.99.refs_2_ = bf16[64,16384]{1,0:T(8,128)(2,1)} custom-call(s32[1]{0:T(128)} %bitcast.me_ref, bf16[32,2048]{1,0:T(8,128)(2,1)S(1)} %add_convert_fusion.2.refs_0_, bf16[32,2048]{1,0:T(8,128)(2,1)S(1)} %collective-permute-done.12.refs_1_, bf16[32,2048]{1,0:T(8,128)(2,1)S(1)} %collective-permute-done.9.refs_2_, ...), custom_call_target="tpu_custom_call", output_to_operand_aliasing={{}: (7, {})} | custom-call | flops 68719476736 | bytes 16777216 | tf_op jit(solution)/shard_map/pallas_call | solution.py:258
  (55 shorter events, 7.7 us)
Async XLA Ops:
  0.0 16.6 %copy-start.4 = (s32[1,128,4]{1,2,0:T(4,128)S(1)}, s32[1,128,4]{1,2,0:T(4,128)}, u32[]{:S(2)}) copy-start(s32[1,128,4]{1,2,0:T(4,128)} %param.16) | copy-start | bytes 6148
  4.0 18.5 %collective-permute-start.2 = (bf16[64,4352]{1,0:T(8,128)(2,1)}, bf16[64,4352]{1,0:T(8,128)(2,1)S(1)}, u32[]{:S(2)}, u32[]{:S(2)}) collective-permute-start(bf16[64,4352]{1,0:T(8,128)(2,1)} %shard_map.91), channel_id=1, source_target_pairs={{0,3},{1,2},{2,1},{3,0},{4,7},{5,6},{6,5},{7,4},{8,11},{9,10},{10,... | collective-permute-start | bytes 1671176 | tf_op jit(solution)/shard_map/ppermute | solution.py:272
  13.0 8.7 %collective-permute-start = (bf16[64,768]{1,0:T(8,128)(2,1)}, bf16[64,768]{1,0:T(8,128)(2,1)S(1)}, u32[]{:S(2)}, u32[]{:S(2)}) collective-permute-start(bf16[64,768]{1,0:T(8,128)(2,1)} %get-tuple-element.25), channel_id=1, source_target_pairs={{0,1},{1,0},{2,3},{3,2},{4,5},{5,4},{6,7},{7,6},{8,9},{9,8},{10,11... | collective-permute-start | bytes 294920 | tf_op jit(solution)/shard_map/ppermute | solution.py:272
  13.3 9.2 %collective-permute-start.1 = (bf16[64,768]{1,0:T(8,128)(2,1)}, bf16[64,768]{1,0:T(8,128)(2,1)S(1)}, u32[]{:S(2)}, u32[]{:S(2)}) collective-permute-start(bf16[64,768]{1,0:T(8,128)(2,1)} %get-tuple-element.26), channel_id=1, source_target_pairs={{0,2},{1,3},{2,0},{3,1},{4,6},{5,7},{6,4},{7,5},{8,10},{9,11},{10,... | collective-permute-start | bytes 294920 | tf_op jit(solution)/shard_map/ppermute | solution.py:272
  13.3 18.2 %collective-permute-start.3 = (bf16[64,3584]{1,0:T(8,128)(2,1)}, bf16[64,3584]{1,0:T(8,128)(2,1)S(1)}, u32[]{:S(2)}, u32[]{:S(2)}) collective-permute-start(bf16[64,3584]{1,0:T(8,128)(2,1)} %get-tuple-element.28), channel_id=1, source_target_pairs={{0,1},{1,0},{2,3},{3,2},{4,5},{5,4},{6,7},{7,6},{8,9},{9,8},{10,11... | collective-permute-start | bytes 1376264 | tf_op jit(solution)/shard_map/ppermute | solution.py:272
  14.7 17.6 %collective-permute-start.4 = (bf16[64,3584]{1,0:T(8,128)(2,1)}, bf16[64,3584]{1,0:T(8,128)(2,1)S(1)}, u32[]{:S(2)}, u32[]{:S(2)}) collective-permute-start(bf16[64,3584]{1,0:T(8,128)(2,1)} %get-tuple-element.29), channel_id=1, source_target_pairs={{0,2},{1,3},{2,0},{3,1},{4,6},{5,7},{6,4},{7,5},{8,10},{9,11},{10,... | collective-permute-start | bytes 1376264 | tf_op jit(solution)/shard_map/ppermute | solution.py:272
  22.5 1.1 %copy-start.2 = (bf16[64,4352]{1,0:T(8,128)(2,1)S(1)}, bf16[64,4352]{1,0:T(8,128)(2,1)}, u32[]{:S(2)}) copy-start(bf16[64,4352]{1,0:T(8,128)(2,1)} %get-tuple-element.27.refs_1_.refs_0_) | copy-start | bytes 1671172
  23.6 2.2 %copy-start = (bf16[1,128,64,256]{3,2,1,0:T(8,128)(2,1)S(1)}, bf16[1,128,64,256]{3,2,1,0:T(8,128)(2,1)}, u32[]{:S(2)}) copy-start(bf16[1,128,64,256]{3,2,1,0:T(8,128)(2,1)} %param.15) | copy-start | bytes 12582916
  23.6 2.9 %copy-start.1 = (bf16[128,64,128]{2,1,0:T(8,128)(2,1)S(1)}, bf16[128,64,128]{2,1,0:T(8,128)(2,1)}, u32[]{:S(2)}) copy-start(bf16[128,64,128]{2,1,0:T(8,128)(2,1)} %refs_6_.1) | copy-start | bytes 6291460
  23.6 2.9 %copy-start.3 = (f32[1,3,64,128]{3,2,1,0:T(8,128)S(1)}, f32[1,3,64,128]{3,2,1,0:T(8,128)}, u32[]{:S(2)}) copy-start(f32[1,3,64,128]{3,2,1,0:T(8,128)} %param.14) | copy-start | bytes 294916
  33.6 2.4 %collective-permute-start.16 = (bf16[4,32,2048]{2,1,0:T(8,128)(2,1)S(1)}, bf16[4,32,2048]{2,1,0:T(8,128)(2,1)S(1)}, u32[]{:S(2)}, u32[]{:S(2)}) collective-permute-start(bf16[4,32,2048]{2,1,0:T(8,128)(2,1)S(1)} %get-tuple-element.37), channel_id=1, source_target_pairs={{0,4},{4,0},{8,12},{12,8},{16,20},{20,16},{24,28},{28,24},{1,5},{5... | collective-permute-start | bytes 1572872 | tf_op jit(solution)/shard_map/ppermute | solution.py:272
  34.4 3.0 %collective-permute-start.5 = (bf16[4,32,2048]{2,1,0:T(8,128)(2,1)S(1)}, bf16[4,32,2048]{2,1,0:T(8,128)(2,1)S(1)}, u32[]{:S(2)}, u32[]{:S(2)}) collective-permute-start(bf16[4,32,2048]{2,1,0:T(8,128)(2,1)S(1)} %get-tuple-element.31), channel_id=1, source_target_pairs={{0,4},{4,0},{8,12},{12,8},{16,20},{20,16},{24,28},{28,24},{1,5},{5... | collective-permute-start | bytes 1572872 | tf_op jit(solution)/shard_map/ppermute | solution.py:272
  36.0 4.8 %collective-permute-start.17 = (bf16[32,2048]{1,0:T(8,128)(2,1)S(1)}, bf16[32,2048]{1,0:T(8,128)(2,1)S(1)}, u32[]{:S(2)}, u32[]{:S(2)}) collective-permute-start(bf16[32,2048]{1,0:T(8,128)(2,1)S(1)} %get-tuple-element.40), channel_id=1, source_target_pairs={{0,8},{4,12},{8,0},{12,4},{16,24},{20,28},{24,16},{28,20},{1,9},{5... | collective-permute-start | bytes 393224 | tf_op jit(solution)/shard_map/ppermute | solution.py:272
  37.5 7.0 %collective-permute-start.6 = (bf16[32,2048]{1,0:T(8,128)(2,1)S(1)}, bf16[32,2048]{1,0:T(8,128)(2,1)S(1)}, u32[]{:S(2)}, u32[]{:S(2)}) collective-permute-start(bf16[32,2048]{1,0:T(8,128)(2,1)S(1)} %get-tuple-element.34), channel_id=1, source_target_pairs={{0,8},{4,12},{8,0},{12,4},{16,24},{20,28},{24,16},{28,20},{1,9},{5... | collective-permute-start | bytes 393224 | tf_op jit(solution)/shard_map/ppermute | solution.py:272
  40.9 6.9 %collective-permute-start.18 = (bf16[32,2048]{1,0:T(8,128)(2,1)S(1)}, bf16[32,2048]{1,0:T(8,128)(2,1)S(1)}, u32[]{:S(2)}, u32[]{:S(2)}) collective-permute-start(bf16[32,2048]{1,0:T(8,128)(2,1)S(1)} %add_convert_fusion.1), channel_id=1, source_target_pairs={{0,16},{4,20},{8,24},{12,28},{16,0},{20,4},{24,8},{28,12},{1,17},{... | collective-permute-start | bytes 393224 | tf_op jit(solution)/shard_map/ppermute | solution.py:272
  43.2 4.5 %collective-permute-start.19 = (bf16[32,2048]{1,0:T(8,128)(2,1)S(1)}, bf16[32,2048]{1,0:T(8,128)(2,1)S(1)}, u32[]{:S(2)}, u32[]{:S(2)}) collective-permute-start(bf16[32,2048]{1,0:T(8,128)(2,1)S(1)} %get-tuple-element.42), channel_id=1, source_target_pairs={{0,8},{4,12},{8,0},{12,4},{16,24},{20,28},{24,16},{28,20},{1,9},{5... | collective-permute-start | bytes 393224 | tf_op jit(solution)/shard_map/ppermute | solution.py:272
  44.6 12.9 %collective-permute-start.7 = (bf16[32,2048]{1,0:T(8,128)(2,1)S(1)}, bf16[32,2048]{1,0:T(8,128)(2,1)S(1)}, u32[]{:S(2)}, u32[]{:S(2)}) collective-permute-start(bf16[32,2048]{1,0:T(8,128)(2,1)S(1)} %add_convert_fusion.3), channel_id=1, source_target_pairs={{0,16},{4,20},{8,24},{12,28},{16,0},{20,4},{24,8},{28,12},{1,17},{... | collective-permute-start | bytes 393224 | tf_op jit(solution)/shard_map/ppermute | solution.py:272
  46.0 11.4 %collective-permute-start.8 = (bf16[32,2048]{1,0:T(8,128)(2,1)S(1)}, bf16[32,2048]{1,0:T(8,128)(2,1)S(1)}, u32[]{:S(2)}, u32[]{:S(2)}) collective-permute-start(bf16[32,2048]{1,0:T(8,128)(2,1)S(1)} %get-tuple-element.36), channel_id=1, source_target_pairs={{0,8},{4,12},{8,0},{12,4},{16,24},{20,28},{24,16},{28,20},{1,9},{5... | collective-permute-start | bytes 393224 | tf_op jit(solution)/shard_map/ppermute | solution.py:272
  47.8 11.2 %collective-permute-start.21 = (bf16[32,2048]{1,0:T(8,128)(2,1)S(1)}, bf16[32,2048]{1,0:T(8,128)(2,1)S(1)}, u32[]{:S(2)}, u32[]{:S(2)}) collective-permute-start(bf16[32,2048]{1,0:T(8,128)(2,1)S(1)} %add_convert_fusion.refs_0_), channel_id=1, source_target_pairs={{0,16},{4,20},{8,24},{12,28},{16,0},{20,4},{24,8},{28,12},{1,17},{... | collective-permute-start | bytes 393224 | tf_op jit(solution)/shard_map/ppermute | solution.py:272
  50.9 9.9 %collective-permute-start.20 = (bf16[32,2048]{1,0:T(8,128)(2,1)S(1)}, bf16[32,2048]{1,0:T(8,128)(2,1)S(1)}, u32[]{:S(2)}, u32[]{:S(2)}) collective-permute-start(bf16[32,2048]{1,0:T(8,128)(2,1)S(1)} %add_convert_fusion.refs_0_), channel_id=1, source_target_pairs={{0,8},{4,12},{8,0},{12,4},{16,24},{20,28},{24,16},{28,20},{1,9},{5... | collective-permute-start | bytes 393224 | tf_op jit(solution)/shard_map/ppermute | solution.py:272
  53.8 11.5 %collective-permute-start.23 = (bf16[32,2048]{1,0:T(8,128)(2,1)S(1)}, bf16[32,2048]{1,0:T(8,128)(2,1)S(1)}, u32[]{:S(2)}, u32[]{:S(2)}) collective-permute-start(bf16[32,2048]{1,0:T(8,128)(2,1)S(1)} %add_convert_fusion.refs_0_), channel_id=1, source_target_pairs={{0,4},{4,0},{8,12},{12,8},{16,20},{20,16},{24,28},{28,24},{1,5},{5... | collective-permute-start | bytes 393224 | tf_op jit(solution)/shard_map/ppermute | solution.py:272
  57.5 9.1 %collective-permute-start.9 = (bf16[32,2048]{1,0:T(8,128)(2,1)S(1)}, bf16[32,2048]{1,0:T(8,128)(2,1)S(1)}, u32[]{:S(2)}, u32[]{:S(2)}) collective-permute-start(bf16[32,2048]{1,0:T(8,128)(2,1)S(1)} %add_convert_fusion.2.refs_0_), channel_id=1, source_target_pairs={{0,16},{4,20},{8,24},{12,28},{16,0},{20,4},{24,8},{28,12},{1,17},{... | collective-permute-start | bytes 393224 | tf_op jit(solution)/shard_map/ppermute | solution.py:272
  59.0 8.0 %collective-permute-start.22 = (bf16[32,2048]{1,0:T(8,128)(2,1)S(1)}, bf16[32,2048]{1,0:T(8,128)(2,1)S(1)}, u32[]{:S(2)}, u32[]{:S(2)}) collective-permute-start(bf16[32,2048]{1,0:T(8,128)(2,1)S(1)} %collective-permute-done.21.refs_2_), channel_id=1, source_target_pairs={{0,8},{4,12},{8,0},{12,4},{16,24},{20,28},{24,16},{28,20},{1,9},{5... | collective-permute-start | bytes 393224 | tf_op jit(solution)/shard_map/ppermute | solution.py:272
  59.5 10.0 %collective-permute-start.12 = (bf16[32,2048]{1,0:T(8,128)(2,1)S(1)}, bf16[32,2048]{1,0:T(8,128)(2,1)S(1)}, u32[]{:S(2)}, u32[]{:S(2)}) collective-permute-start(bf16[32,2048]{1,0:T(8,128)(2,1)S(1)} %add_convert_fusion.2.refs_0_), channel_id=1, source_target_pairs={{0,8},{4,12},{8,0},{12,4},{16,24},{20,28},{24,16},{28,20},{1,9},{5... | collective-permute-start | bytes 393224 | tf_op jit(solution)/shard_map/ppermute | solution.py:272
  60.8 11.2 %collective-permute-start.24 = (bf16[32,2048]{1,0:T(8,128)(2,1)S(1)}, bf16[32,2048]{1,0:T(8,128)(2,1)S(1)}, u32[]{:S(2)}, u32[]{:S(2)}) collective-permute-start(bf16[32,2048]{1,0:T(8,128)(2,1)S(1)} %collective-permute-done.20.refs_1_), channel_id=1, source_target_pairs={{0,4},{4,0},{8,12},{12,8},{16,20},{20,16},{24,28},{28,24},{1,5},{5... | collective-permute-start | bytes 393224 | tf_op jit(solution)/shard_map/ppermute | solution.py:272
  65.3 6.7 %collective-permute-start.25 = (bf16[32,2048]{1,0:T(8,128)(2,1)S(1)}, bf16[32,2048]{1,0:T(8,128)(2,1)S(1)}, u32[]{:S(2)}, u32[]{:S(2)}) collective-permute-start(bf16[32,2048]{1,0:T(8,128)(2,1)S(1)} %collective-permute-done.21.refs_2_), channel_id=1, source_target_pairs={{0,4},{4,0},{8,12},{12,8},{16,20},{20,16},{24,28},{28,24},{1,5},{5... | collective-permute-start | bytes 393224 | tf_op jit(solution)/shard_map/ppermute | solution.py:272
  66.6 5.9 %collective-permute-start.10 = (bf16[32,2048]{1,0:T(8,128)(2,1)S(1)}, bf16[32,2048]{1,0:T(8,128)(2,1)S(1)}, u32[]{:S(2)}, u32[]{:S(2)}) collective-permute-start(bf16[32,2048]{1,0:T(8,128)(2,1)S(1)} %collective-permute-done.9.refs_2_), channel_id=1, source_target_pairs={{0,8},{4,12},{8,0},{12,4},{16,24},{20,28},{24,16},{28,20},{1,9},{5... | collective-permute-start | bytes 393224 | tf_op jit(solution)/shard_map/ppermute | solution.py:272
  67.1 6.7 %collective-permute-start.26 = (bf16[32,2048]{1,0:T(8,128)(2,1)S(1)}, bf16[32,2048]{1,0:T(8,128)(2,1)S(1)}, u32[]{:S(2)}, u32[]{:S(2)}) collective-permute-start(bf16[32,2048]{1,0:T(8,128)(2,1)S(1)} %collective-permute-done.22.refs_3_), channel_id=1, source_target_pairs={{0,4},{4,0},{8,12},{12,8},{16,20},{20,16},{24,28},{28,24},{1,5},{5... | collective-permute-start | bytes 393224 | tf_op jit(solution)/shard_map/ppermute | solution.py:272
  69.5 5.2 %collective-permute-start.13 = (bf16[32,2048]{1,0:T(8,128)(2,1)S(1)}, bf16[32,2048]{1,0:T(8,128)(2,1)S(1)}, u32[]{:S(2)}, u32[]{:S(2)}) collective-permute-start(bf16[32,2048]{1,0:T(8,128)(2,1)S(1)} %add_convert_fusion.2.refs_0_), channel_id=1, source_target_pairs={{0,4},{4,0},{8,12},{12,8},{16,20},{20,16},{24,28},{28,24},{1,5},{5... | collective-permute-start | bytes 393224 | tf_op jit(solution)/shard_map/ppermute | solution.py:272
  72.0 2.8 %collective-permute-start.15 = (bf16[32,2048]{1,0:T(8,128)(2,1)S(1)}, bf16[32,2048]{1,0:T(8,128)(2,1)S(1)}, u32[]{:S(2)}, u32[]{:S(2)}) collective-permute-start(bf16[32,2048]{1,0:T(8,128)(2,1)S(1)} %collective-permute-done.9.refs_2_), channel_id=1, source_target_pairs={{0,4},{4,0},{8,12},{12,8},{16,20},{20,16},{24,28},{28,24},{1,5},{5... | collective-permute-start | bytes 393224 | tf_op jit(solution)/shard_map/ppermute | solution.py:272
  72.0 2.8 %collective-permute-start.14 = (bf16[32,2048]{1,0:T(8,128)(2,1)S(1)}, bf16[32,2048]{1,0:T(8,128)(2,1)S(1)}, u32[]{:S(2)}, u32[]{:S(2)}) collective-permute-start(bf16[32,2048]{1,0:T(8,128)(2,1)S(1)} %collective-permute-done.12.refs_1_), channel_id=1, source_target_pairs={{0,4},{4,0},{8,12},{12,8},{16,20},{20,16},{24,28},{28,24},{1,5},{5... | collective-permute-start | bytes 393224 | tf_op jit(solution)/shard_map/ppermute | solution.py:272
  72.5 3.2 %collective-permute-start.11 = (bf16[32,2048]{1,0:T(8,128)(2,1)S(1)}, bf16[32,2048]{1,0:T(8,128)(2,1)S(1)}, u32[]{:S(2)}, u32[]{:S(2)}) collective-permute-start(bf16[32,2048]{1,0:T(8,128)(2,1)S(1)} %collective-permute-done.10.refs_0_), channel_id=1, source_target_pairs={{0,4},{4,0},{8,12},{12,8},{16,20},{20,16},{24,28},{28,24},{1,5},{5... | collective-permute-start | bytes 393224 | tf_op jit(solution)/shard_map/ppermute | solution.py:272

commit v7 on v6

--- a/solution.py
+++ b/solution.py
@@ -65,15 +65,15 @@
             root += lax.dot_general(
                 x_ref[:, i * tile : (i + 1) * tile], basis[i], NT, preferred_element_type=F32
             )
-        high = root.astype(BF16)
-        low = (root - high.astype(F32)).astype(BF16)
-        roots = jnp.concatenate([high, low], axis=1)
-        tgt = jnp.broadcast_to(tgt_ref[...].astype(F32).astype(BF16), (nrhs, count))
+        tgt = tgt_ref[...].astype(F32).astype(BF16)
+        rows = nrhs * rank // count
+        tgt = [
+            jnp.broadcast_to(tgt[:, i : i + rank], (rows, rank)) for i in range(0, count, rank)
+        ]
+        roots = jnp.concatenate([root.astype(BF16), jnp.concatenate(tgt, axis=0)], axis=1)
         for part, out in zip(parts, outs):
             if part.head:
-                end = out.shape[1] - count
-                out[:, end - 2 * rank : end] = roots
-                out[:, end:] = tgt
+                out[:, out.shape[1] - 2 * rank :] = roots
     for (part, begin, size, at), copy in zip(spans, copies):
         copy.wait()
         first = (me_ref[0] ^ part.mask) * slots
@@ -89,7 +89,7 @@
 def near_products(parts, me, near_src, near_tgt, x, basis, tiles):
     count, tile, _ = tiles.shape
     nrhs, rank = x.shape[0], basis.shape[1]
-    widths = [(p.end - p.begin) * tile + (2 * rank + count if p.head else 0) for p in parts]
+    widths = [(p.end - p.begin) * tile + (2 * rank if p.head else 0) for p in parts]
     blocks = sum(-(-(p.end - p.begin) // STEP) for p in parts)
     return pl.pallas_call(
         functools.partial(near_kernel, parts),
@@ -135,7 +135,7 @@
     )(me, tgt, *got)
 
 
-def far_kernel(groups, count, me_ref, node_ref, *refs):
+def far_kernel(groups, me_ref, node_ref, *refs):
     head_refs = refs[:groups]
     edge_ref, coupling_ref, basis_ref, near_ref, out_ref, exact, low, high = refs[groups:]
     tgt_tiles, rank, tile = basis_ref.shape
@@ -143,9 +143,8 @@
     pieces, nrhs, width = out_ref.shape
     leaves = width // tile
     for m in range(groups):
-        end = head_refs[m].shape[1] - count
-        pair = head_refs[m][:, end - 2 * rank : end].astype(F32)
-        exact[groups - 1 + (me_ref[0] ^ m)] = pair[:, :rank] + pair[:, rank:]
+        end = head_refs[m].shape[1] - 2 * rank
+        exact[groups - 1 + (me_ref[0] ^ m)] = head_refs[m][:, end : end + rank].astype(F32)
     for n in range(groups - 2, -1, -1):
         pair = jnp.concatenate([exact[2 * n + 1], exact[2 * n + 2]], axis=1)
         exact[n] = lax.dot_general(
@@ -175,13 +174,13 @@
             out_ref[p, :, at] = near_ref[p, :, at] + far
 
 
-def far_field(me, far_node, heads, transfer, coupling, target_basis, near, count):
+def far_field(me, far_node, heads, transfer, coupling, target_basis, near):
     groups = len(heads)
     rank = target_basis.shape[1]
     nrhs = near.shape[1]
     nodes = 2 * groups - 1
     return pl.pallas_call(
-        functools.partial(far_kernel, groups, count),
+        functools.partial(far_kernel, groups),
         out_shape=jax.ShapeDtypeStruct(near.shape, F32),
         in_specs=[SMEM, SMEM] + [VMEM] * (groups + 4),
         out_specs=VMEM,
@@ -276,26 +275,39 @@
     return lax.optimization_barrier((value,) + others)[0]
 
 
-def sum_and_share(half, me, acc, got):
+def begin_sums(half, me, acc, got):
+    first, near, cross, own = split(half, (3, 1, 2, 0), (BF16, BF16, F32, F32), me, acc, got)
+    a = swap(first, "src", 2)
+    cross = (cross + a.astype(F32)).astype(BF16)
+    return own, cross, swap(cross, "src", 4), swap(tied(near, cross), "src", 2)
+
+
+def share(own, b, c):
+    own = (own + b.astype(F32) + c.astype(F32)).astype(BF16)
+    d = swap(own, "src", 4)
+    return [own, swap(own, "src", 2), d, swap(d, "src", 2)]
+
+
+def sums(me, acc, gots):
     chips = acc.shape[0] // 2
+    masks = tuple(range(chips))
     if chips == 4:
-        first, near, cross, own = split(half, (3, 1, 2, 0), (BF16, BF16, F32, F32), me, acc, got)
-        a = swap(first, "src", 2)
-        cross = (cross + a.astype(F32)).astype(BF16)
-        b = swap(cross, "src", 4)
-        c = swap(tied(near, cross), "src", 2)
-        own = own + b.astype(F32)
-        own = (own + c.astype(F32)).astype(BF16)
-        d = swap(own, "src", 4)
-        e = swap(own, "src", 2)
-        return (0, 1, 2, 3), [own, e, d, swap(d, "src", 2)]
-    masks = tuple(range(chips))
-    dtypes = (F32,) + (BF16,) * (chips - 1)
-    own, *rest = split(half, masks, dtypes, me, acc, got)
-    for m, part in zip(masks[1:], rest):
-        own = own + swap(part, "src", 2 * m).astype(F32)
-    own = own.astype(BF16)
-    return masks, [own] + [swap(own, "src", 2 * m) for m in masks[1:]]
+        begun = [begin_sums(half, me, acc, got) for half, got in enumerate(gots)]
+        shared = []
+        for half, (own, _, b, c) in enumerate(begun):
+            if half + 1 < len(begun):
+                b = tied(b, begun[half + 1][1])
+            shared.append(share(own, b, c))
+        return masks, shared
+    shared = []
+    for half, got in enumerate(gots):
+        dtypes = (F32,) + (BF16,) * (chips - 1)
+        own, *rest = split(half, masks, dtypes, me, acc, got)
+        for m, part in zip(masks[1:], rest):
+            own = own + swap(part, "src", 2 * m).astype(F32)
+        own = own.astype(BF16)
+        shared.append([own] + [swap(own, "src", 2 * m) for m in masks[1:]])
+    return masks, shared
 
 
 def shards(
@@ -307,6 +319,7 @@
     me_s = lax.axis_index("src").astype(jnp.int32)
     count, tile, _ = near_tiles.shape
     slots = count // groups
+    nrhs = charges.shape[1]
     x = charges.T
     me = me_t.reshape(1)
 
@@ -325,8 +338,11 @@
     }
     by_mask = {part.mask: got[part] for part in heads}
 
+    rank = leaf_basis.shape[1]
+    band = nrhs * rank // count
+
     def targets(some):
-        rows = [by_mask[part.mask][:1, -count:] for part in some]
+        rows = [by_mask[part.mask][::band, -rank:].reshape(1, count) for part in some]
         return jnp.concatenate(rows).astype(F32).astype(jnp.int32)
 
     early = [part for part in heads if part.mask in (masks[0], masks[-1])]
@@ -348,7 +364,6 @@
         coupling[0],
         target_basis,
         acc,
-        count,
     )
     here = jnp.stack([me_t, me_s])
     acc, *sends = gather_near(
@@ -356,8 +371,8 @@
     )
     me = me_s.reshape(1)
     parts = []
-    for half, send in enumerate(sends):
-        owners, mine = sum_and_share(half, me, acc, swap(send, "src", 1))
+    owners, shared = sums(me, acc, [swap(send, "src", 1) for send in sends])
+    for half, mine in enumerate(shared):
         parts += [((half, 2 * m), q) for m, q in zip(owners, mine)]
         parts += [((half, 2 * m + 1), swap(q, "src", 1)) for m, q in zip(owners, mine)]
     last = parts[-len(owners) - 1], parts[-1]

time: 76.7 us -> 75.9 us (0.990)
  waiting for transfers between devices: 15 us -> 13.7 us
    ppermute x27, waiting for transfers between devices: 15 us -> 13.7 us  [swap(): return lax.ppermute(value, axis, [(i, i ^ mask) for i in range(size)])]
  transfers between devices with their start and end apart: 27 -> 27, of which waited for: 10 -> 10; matrix products, arithmetic and copies ran while one was open for 2% -> 3% of each run, Pallas kernels for 17% -> 17%
where the time goes in v7:
time: 75.9 us; the launch traced here: 75.7 us
  starting transfers between devices  38.4 us (51%)
  Pallas kernels  19 us (25%)
  waiting for transfers between devices  13.7 us (18%)
  local copies, waits for them, and re-layouts  4.18 us (6%)
    ppermute x27, starting transfers between devices, swap(): return lax.ppermute(value, axis, [(i, i ^ mask) for i in range(size)])  38.4 us
    ppermute x27, waiting for transfers between devices, swap(): return lax.ppermute(value, axis, [(i, i ^ mask) for i in range(size)])  13.7 us
    pallas_call x2, Pallas kernels, near_products(): pl.pallas_call(functools.partial(near_kernel, parts), out_shape=[jax.Shap...  9.71 us
    pallas_call x1, Pallas kernels, far_field(): pl.pallas_call(functools.partial(far_kernel, groups), out_shape=jax.Shape...  3.82 us
    pallas_call x3, Pallas kernels, place(): pl.pallas_call(functools.partial(place_kernel, masks), out_shape=jax.Shap...  2.68 us
    unnamed x11, local copies, waits for them, and re-layouts  2.63 us
  transfers between devices with their start and end apart: 27, of which 10 were waited for; matrix products, arithmetic and copies ran while one was open for 3% of the time, Pallas kernels for 17%

profile of v7, /device:TPU:1, one launch (start us, length us, event | category | flops | bytes accessed | tf_op | source)
XLA Modules:
  0.0 75.7 jit_solution(16602881969662498223)
XLA Ops:
  0.0 3.9 %shard_map.91 = bf16[64,4224]{1,0:T(8,128)(2,1)} custom-call(s32[1]{0:T(128)} %bitcast.1.me_ref, s32[128]{0:T(128)} %src_ref.3, s32[1,128]{1,0:T(1,128)} %bitcast.11, bf16[64,2048]{1,0:T(8,128)(2,1)} %bitcast.9, bf16[16,64,128]{2,1,0:T(8,128)(2,1)} %basis_ref.3, bf16[128,128,128]{2,1,0:T(8,128)(2,1)} %tiles_ref.3), custom_call_target="tpu_custom_call" | custom-call | tf_op jit(solution)/shard_map/pallas_call | solution.py:94
  3.9 3.1 %collective-permute-start.2 = (bf16[64,4224]{1,0:T(8,128)(2,1)}, bf16[64,4224]{1,0:T(8,128)(2,1)S(1)}, u32[]{:S(2)}, u32[]{:S(2)}) collective-permute-start(bf16[64,4224]{1,0:T(8,128)(2,1)} %shard_map.91), channel_id=1, source_target_pairs={{0,3},{1,2},{2,1},{3,0},{4,7},{5,6},{6,5},{7,4},{8,11},{9,10},{10,... | collective-permute-start | bytes 1622024 | tf_op jit(solution)/shard_map/ppermute | solution.py:271
  7.0 5.8 %shard_map.92 = (bf16[64,640]{1,0:T(8,128)(2,1)}, bf16[64,640]{1,0:T(8,128)(2,1)}, bf16[64,4224]{1,0:T(8,128)(2,1)}, bf16[64,3584]{1,0:T(8,128)(2,1)}, bf16[64,3584]{1,0:T(8,128)(2,1)}) custom-call(s32[1]{0:T(128)} %bitcast.1.me_ref, s32[128]{0:T(128)} %src_ref.3, s32[1,128]{1,0:T(1,128)} %bitcast.12, bf16[64,2048]{1,0:T(8,128)(2,1)} %bitcast.10, ...), custom_call_target="tpu_custom_call" | custom-call | tf_op jit(solution)/shard_map/pallas_call | solution.py:94
  13.2 1.4 %collective-permute-start.3 = (bf16[64,3584]{1,0:T(8,128)(2,1)}, bf16[64,3584]{1,0:T(8,128)(2,1)S(1)}, u32[]{:S(2)}, u32[]{:S(2)}) collective-permute-start(bf16[64,3584]{1,0:T(8,128)(2,1)} %get-tuple-element.29), channel_id=1, source_target_pairs={{0,1},{1,0},{2,3},{3,2},{4,5},{5,4},{6,7},{7,6},{8,9},{9,8},{10,11... | collective-permute-start | bytes 1376264 | tf_op jit(solution)/shard_map/ppermute | solution.py:271
  14.6 1.2 %collective-permute-start.4 = (bf16[64,3584]{1,0:T(8,128)(2,1)}, bf16[64,3584]{1,0:T(8,128)(2,1)S(1)}, u32[]{:S(2)}, u32[]{:S(2)}) collective-permute-start(bf16[64,3584]{1,0:T(8,128)(2,1)} %get-tuple-element.30), channel_id=1, source_target_pairs={{0,2},{1,3},{2,0},{3,1},{4,6},{5,7},{6,4},{7,5},{8,10},{9,11},{10,... | collective-permute-start | bytes 1376264 | tf_op jit(solution)/shard_map/ppermute | solution.py:271
  15.8 0.8 %slice.17 = bf16[2,64]{1,0:T(2,128)(2,1)S(1)} slice(bf16[64,4224]{1,0:T(8,128)(2,1)} %get-tuple-element.28.refs_1_.refs_0_), slice={[0:64:32], [4160:4224:1]} | slice | bytes 512 | tf_op jit(solution)/shard_map/slice | solution.py:345
  17.0 3.9 %collective-permute-done.refs_1_.refs_0_ = bf16[64,640]{1,0:T(8,128)(2,1)S(1)} collective-permute-done((bf16[64,640]{1,0:T(8,128)(2,1)}, bf16[64,640]{1,0:T(8,128)(2,1)S(1)}, u32[]{:S(2)}, u32[]{:S(2)}) %collective-permute-start) | collective-permute-done | bytes 81952 | tf_op jit(solution)/shard_map/ppermute | solution.py:271
  22.1 1.0 %copy-done.2 = bf16[64,4224]{1,0:T(8,128)(2,1)S(1)} copy-done((bf16[64,4224]{1,0:T(8,128)(2,1)S(1)}, bf16[64,4224]{1,0:T(8,128)(2,1)}, u32[]{:S(2)}) %copy-start.2) | copy-done | bytes 540696
  23.2 1.4 %shard_map.93.refs_7_ = f32[8,64,2048]{2,1,0:T(8,128)S(1)} custom-call(s32[1]{0:T(128)} %bitcast.1.me_ref, s32[2,128]{1,0:T(2,128)S(1)} %convert_convert_fusion.1.tgt_ref, bf16[64,4224]{1,0:T(8,128)(2,1)S(1)} %collective-permute-done.2.refs_0_.refs_3_, bf16[64,4224]{1,0:T(8,128)(2,1)S(1)} %copy-done.2), custom_call_target="tpu_custom_call" | custom-call | flops 68719476736 | bytes 16777216 | tf_op jit(solution)/shard_map/pallas_call | solution.py:128
  26.0 3.8 %shard_map.94.far_ref = f32[8,64,2048]{2,1,0:T(8,128)S(1)} custom-call(s32[1]{0:T(128)} %bitcast.1.me_ref, s32[512]{0:T(512)S(1)} %reshape_squeeze.3.node_ref, bf16[64,4224]{1,0:T(8,128)(2,1)S(1)} %copy-done.2, bf16[64,640]{1,0:T(8,128)(2,1)S(1)} %collective-permute-done.refs_1_.refs_0_, ...), custom_call_target="tpu_custom_call", output_to_operand_aliasing={{}: (9, {})} | custom-call | tf_op jit(solution)/shard_map/pallas_call | solution.py:182
  29.8 0.9 %collective-permute-done.3.refs_2_ = bf16[64,3584]{1,0:T(8,128)(2,1)S(1)} collective-permute-done((bf16[64,3584]{1,0:T(8,128)(2,1)}, bf16[64,3584]{1,0:T(8,128)(2,1)S(1)}, u32[]{:S(2)}, u32[]{:S(2)}) %collective-permute-start.3) | collective-permute-done | bytes 458784 | tf_op jit(solution)/shard_map/ppermute | solution.py:271
  31.5 1.3 %shard_map.95 = (f32[8,64,2048]{2,1,0:T(8,128)S(1)}, bf16[4,32,2048]{2,1,0:T(8,128)(2,1)S(1)}, bf16[4,32,2048]{2,1,0:T(8,128)(2,1)S(1)}) custom-call(s32[2]{0:T(128)S(1)} %pad_add_fusion.me_ref, s32[4,128]{1,0:T(4,128)S(1)} %convert_convert_fusion.tgt_ref, f32[8,64,2048]{2,1,0:T(8,128)S(1)} %shard_map.94.far_ref, ...), custom_call_target="tpu_custom_call", output_to_operand_aliasing={{0}: (2, {})} | custom-call | tf_op jit(solution)/shard_map/pallas_call | solution.py:210
  32.8 0.9 %collective-permute-start.16 = (bf16[4,32,2048]{2,1,0:T(8,128)(2,1)S(1)}, bf16[4,32,2048]{2,1,0:T(8,128)(2,1)S(1)}, u32[]{:S(2)}, u32[]{:S(2)}) collective-permute-start(bf16[4,32,2048]{2,1,0:T(8,128)(2,1)S(1)} %get-tuple-element.38), channel_id=1, source_target_pairs={{0,4},{4,0},{8,12},{12,8},{16,20},{20,16},{24,28},{28,24},{1,5},{5... | collective-permute-start | bytes 1572872 | tf_op jit(solution)/shard_map/ppermute | solution.py:271
  33.7 1.5 %collective-permute-done.16.got_ref = bf16[4,32,2048]{2,1,0:T(8,128)(2,1)S(1)} collective-permute-done((bf16[4,32,2048]{2,1,0:T(8,128)(2,1)S(1)}, bf16[4,32,2048]{2,1,0:T(8,128)(2,1)S(1)}, u32[]{:S(2)}, u32[]{:S(2)}) %collective-permute-start.16) | collective-permute-done | bytes 524320 | tf_op jit(solution)/shard_map/ppermute | solution.py:271
  35.3 1.4 %collective-permute-start.17 = (bf16[32,2048]{1,0:T(8,128)(2,1)S(1)}, bf16[32,2048]{1,0:T(8,128)(2,1)S(1)}, u32[]{:S(2)}, u32[]{:S(2)}) collective-permute-start(bf16[32,2048]{1,0:T(8,128)(2,1)S(1)} %get-tuple-element.41), channel_id=1, source_target_pairs={{0,8},{4,12},{8,0},{12,4},{16,24},{20,28},{24,16},{28,20},{1,9},{5... | collective-permute-start | bytes 393224 | tf_op jit(solution)/shard_map/ppermute | solution.py:271
  37.4 2.7 %collective-permute-done.17 = bf16[32,2048]{1,0:T(8,128)(2,1)S(1)} collective-permute-done((bf16[32,2048]{1,0:T(8,128)(2,1)S(1)}, bf16[32,2048]{1,0:T(8,128)(2,1)S(1)}, u32[]{:S(2)}, u32[]{:S(2)}) %collective-permute-start.17) | collective-permute-done | bytes 131104 | tf_op jit(solution)/shard_map/ppermute | solution.py:271
  40.1 2.4 %collective-permute-start.18 = (bf16[32,2048]{1,0:T(8,128)(2,1)S(1)}, bf16[32,2048]{1,0:T(8,128)(2,1)S(1)}, u32[]{:S(2)}, u32[]{:S(2)}) collective-permute-start(bf16[32,2048]{1,0:T(8,128)(2,1)S(1)} %add_convert_fusion.1), channel_id=1, source_target_pairs={{0,16},{4,20},{8,24},{12,28},{16,0},{20,4},{24,8},{28,12},{1,17},{... | collective-permute-start | bytes 393224 | tf_op jit(solution)/shard_map/ppermute | solution.py:271
  42.5 1.3 %collective-permute-start.19 = (bf16[32,2048]{1,0:T(8,128)(2,1)S(1)}, bf16[32,2048]{1,0:T(8,128)(2,1)S(1)}, u32[]{:S(2)}, u32[]{:S(2)}) collective-permute-start(bf16[32,2048]{1,0:T(8,128)(2,1)S(1)} %get-tuple-element.44), channel_id=1, source_target_pairs={{0,8},{4,12},{8,0},{12,4},{16,24},{20,28},{24,16},{28,20},{1,9},{5... | collective-permute-start | bytes 393224 | tf_op jit(solution)/shard_map/ppermute | solution.py:271
  43.8 1.5 %collective-permute-start.7 = (bf16[32,2048]{1,0:T(8,128)(2,1)S(1)}, bf16[32,2048]{1,0:T(8,128)(2,1)S(1)}, u32[]{:S(2)}, u32[]{:S(2)}) collective-permute-start(bf16[32,2048]{1,0:T(8,128)(2,1)S(1)} %add_convert_fusion.3), channel_id=1, source_target_pairs={{0,16},{4,20},{8,24},{12,28},{16,0},{20,4},{24,8},{28,12},{1,17},{... | collective-permute-start | bytes 393224 | tf_op jit(solution)/shard_map/ppermute | solution.py:271
  45.3 1.3 %collective-permute-start.8 = (bf16[32,2048]{1,0:T(8,128)(2,1)S(1)}, bf16[32,2048]{1,0:T(8,128)(2,1)S(1)}, u32[]{:S(2)}, u32[]{:S(2)}) collective-permute-start(bf16[32,2048]{1,0:T(8,128)(2,1)S(1)} %get-tuple-element.37), channel_id=1, source_target_pairs={{0,8},{4,12},{8,0},{12,4},{16,24},{20,28},{24,16},{28,20},{1,9},{5... | collective-permute-start | bytes 393224 | tf_op jit(solution)/shard_map/ppermute | solution.py:271
  47.0 3.1 %collective-permute-start.21 = (bf16[32,2048]{1,0:T(8,128)(2,1)S(1)}, bf16[32,2048]{1,0:T(8,128)(2,1)S(1)}, u32[]{:S(2)}, u32[]{:S(2)}) collective-permute-start(bf16[32,2048]{1,0:T(8,128)(2,1)S(1)} %add_convert_fusion.refs_0_), channel_id=1, source_target_pairs={{0,16},{4,20},{8,24},{12,28},{16,0},{20,4},{24,8},{28,12},{1,17},{... | collective-permute-start | bytes 393224 | tf_op jit(solution)/shard_map/ppermute | solution.py:271
  50.1 2.9 %collective-permute-start.20 = (bf16[32,2048]{1,0:T(8,128)(2,1)S(1)}, bf16[32,2048]{1,0:T(8,128)(2,1)S(1)}, u32[]{:S(2)}, u32[]{:S(2)}) collective-permute-start(bf16[32,2048]{1,0:T(8,128)(2,1)S(1)} %add_convert_fusion.refs_0_), channel_id=1, source_target_pairs={{0,8},{4,12},{8,0},{12,4},{16,24},{20,28},{24,16},{28,20},{1,9},{5... | collective-permute-start | bytes 393224 | tf_op jit(solution)/shard_map/ppermute | solution.py:271
  53.0 3.6 %collective-permute-start.23 = (bf16[32,2048]{1,0:T(8,128)(2,1)S(1)}, bf16[32,2048]{1,0:T(8,128)(2,1)S(1)}, u32[]{:S(2)}, u32[]{:S(2)}) collective-permute-start(bf16[32,2048]{1,0:T(8,128)(2,1)S(1)} %add_convert_fusion.refs_0_), channel_id=1, source_target_pairs={{0,4},{4,0},{8,12},{12,8},{16,20},{20,16},{24,28},{28,24},{1,5},{5... | collective-permute-start | bytes 393224 | tf_op jit(solution)/shard_map/ppermute | solution.py:271
  56.9 1.3 %collective-permute-done.21.refs_2_ = bf16[32,2048]{1,0:T(8,128)(2,1)S(1)} collective-permute-done((bf16[32,2048]{1,0:T(8,128)(2,1)S(1)}, bf16[32,2048]{1,0:T(8,128)(2,1)S(1)}, u32[]{:S(2)}, u32[]{:S(2)}) %collective-permute-start.21) | collective-permute-done | bytes 131104 | tf_op jit(solution)/shard_map/ppermute | solution.py:271
  58.7 1.0 %collective-permute-start.12 = (bf16[32,2048]{1,0:T(8,128)(2,1)S(1)}, bf16[32,2048]{1,0:T(8,128)(2,1)S(1)}, u32[]{:S(2)}, u32[]{:S(2)}) collective-permute-start(bf16[32,2048]{1,0:T(8,128)(2,1)S(1)} %add_convert_fusion.2.refs_0_), channel_id=1, source_target_pairs={{0,8},{4,12},{8,0},{12,4},{16,24},{20,28},{24,16},{28,20},{1,9},{5... | collective-permute-start | bytes 393224 | tf_op jit(solution)/shard_map/ppermute | solution.py:271
  60.0 4.5 %collective-permute-start.24 = (bf16[32,2048]{1,0:T(8,128)(2,1)S(1)}, bf16[32,2048]{1,0:T(8,128)(2,1)S(1)}, u32[]{:S(2)}, u32[]{:S(2)}) collective-permute-start(bf16[32,2048]{1,0:T(8,128)(2,1)S(1)} %collective-permute-done.20.refs_1_), channel_id=1, source_target_pairs={{0,4},{4,0},{8,12},{12,8},{16,20},{20,16},{24,28},{28,24},{1,5},{5... | collective-permute-start | bytes 393224 | tf_op jit(solution)/shard_map/ppermute | solution.py:271
  64.6 1.3 %collective-permute-done.9.refs_2_ = bf16[32,2048]{1,0:T(8,128)(2,1)S(1)} collective-permute-done((bf16[32,2048]{1,0:T(8,128)(2,1)S(1)}, bf16[32,2048]{1,0:T(8,128)(2,1)S(1)}, u32[]{:S(2)}, u32[]{:S(2)}) %collective-permute-start.9) | collective-permute-done | bytes 131104 | tf_op jit(solution)/shard_map/ppermute | solution.py:271
  66.3 2.4 %collective-permute-start.26 = (bf16[32,2048]{1,0:T(8,128)(2,1)S(1)}, bf16[32,2048]{1,0:T(8,128)(2,1)S(1)}, u32[]{:S(2)}, u32[]{:S(2)}) collective-permute-start(bf16[32,2048]{1,0:T(8,128)(2,1)S(1)} %collective-permute-done.22.refs_3_), channel_id=1, source_target_pairs={{0,4},{4,0},{8,12},{12,8},{16,20},{20,16},{24,28},{28,24},{1,5},{5... | collective-permute-start | bytes 393224 | tf_op jit(solution)/shard_map/ppermute | solution.py:271
  68.7 2.5 %collective-permute-start.13 = (bf16[32,2048]{1,0:T(8,128)(2,1)S(1)}, bf16[32,2048]{1,0:T(8,128)(2,1)S(1)}, u32[]{:S(2)}, u32[]{:S(2)}) collective-permute-start(bf16[32,2048]{1,0:T(8,128)(2,1)S(1)} %add_convert_fusion.2.refs_0_), channel_id=1, source_target_pairs={{0,4},{4,0},{8,12},{12,8},{16,20},{20,16},{24,28},{28,24},{1,5},{5... | collective-permute-start | bytes 393224 | tf_op jit(solution)/shard_map/ppermute | solution.py:271
  71.7 1.2 %collective-permute-start.11 = (bf16[32,2048]{1,0:T(8,128)(2,1)S(1)}, bf16[32,2048]{1,0:T(8,128)(2,1)S(1)}, u32[]{:S(2)}, u32[]{:S(2)}) collective-permute-start(bf16[32,2048]{1,0:T(8,128)(2,1)S(1)} %collective-permute-done.10.refs_0_), channel_id=1, source_target_pairs={{0,4},{4,0},{8,12},{12,8},{16,20},{20,16},{24,28},{28,24},{1,5},{5... | collective-permute-start | bytes 393224 | tf_op jit(solution)/shard_map/ppermute | solution.py:271
  72.9 1.0 %shard_map.98.refs_6_ = bf16[64,16384]{1,0:T(8,128)(2,1)} custom-call(s32[1]{0:T(128)} %bitcast.me_ref, bf16[32,2048]{1,0:T(8,128)(2,1)S(1)} %add_convert_fusion.refs_0_, bf16[32,2048]{1,0:T(8,128)(2,1)S(1)} %collective-permute-done.20.refs_1_, bf16[32,2048]{1,0:T(8,128)(2,1)S(1)} %collective-permute-done.21.refs_2_, ...), custom_call_target="tpu_custom_call" | custom-call | flops 68719476736 | bytes 16777216 | tf_op jit(solution)/shard_map/pallas_call | solution.py:257
  74.0 0.9 %shard_map.99.refs_2_ = bf16[64,16384]{1,0:T(8,128)(2,1)} custom-call(s32[1]{0:T(128)} %bitcast.me_ref, bf16[32,2048]{1,0:T(8,128)(2,1)S(1)} %add_convert_fusion.2.refs_0_, bf16[32,2048]{1,0:T(8,128)(2,1)S(1)} %collective-permute-done.12.refs_1_, bf16[32,2048]{1,0:T(8,128)(2,1)S(1)} %collective-permute-done.9.refs_2_, ...), custom_call_target="tpu_custom_call", output_to_operand_aliasing={{}: (7, {})} | custom-call | flops 68719476736 | bytes 16777216 | tf_op jit(solution)/shard_map/pallas_call | solution.py:257
  (59 shorter events, 8.3 us)
Async XLA Ops:
  0.0 16.7 %copy-start.4 = (s32[1,128,4]{1,2,0:T(4,128)S(1)}, s32[1,128,4]{1,2,0:T(4,128)}, u32[]{:S(2)}) copy-start(s32[1,128,4]{1,2,0:T(4,128)} %param.16) | copy-start | bytes 6148
  3.9 18.0 %collective-permute-start.2 = (bf16[64,4224]{1,0:T(8,128)(2,1)}, bf16[64,4224]{1,0:T(8,128)(2,1)S(1)}, u32[]{:S(2)}, u32[]{:S(2)}) collective-permute-start(bf16[64,4224]{1,0:T(8,128)(2,1)} %shard_map.91), channel_id=1, source_target_pairs={{0,3},{1,2},{2,1},{3,0},{4,7},{5,6},{6,5},{7,4},{8,11},{9,10},{10,... | collective-permute-start | bytes 1622024 | tf_op jit(solution)/shard_map/ppermute | solution.py:271
  12.8 8.1 %collective-permute-start = (bf16[64,640]{1,0:T(8,128)(2,1)}, bf16[64,640]{1,0:T(8,128)(2,1)S(1)}, u32[]{:S(2)}, u32[]{:S(2)}) collective-permute-start(bf16[64,640]{1,0:T(8,128)(2,1)} %get-tuple-element.26), channel_id=1, source_target_pairs={{0,1},{1,0},{2,3},{3,2},{4,5},{5,4},{6,7},{7,6},{8,9},{9,8},{10,11... | collective-permute-start | bytes 245768 | tf_op jit(solution)/shard_map/ppermute | solution.py:271
  13.1 8.6 %collective-permute-start.1 = (bf16[64,640]{1,0:T(8,128)(2,1)}, bf16[64,640]{1,0:T(8,128)(2,1)S(1)}, u32[]{:S(2)}, u32[]{:S(2)}) collective-permute-start(bf16[64,640]{1,0:T(8,128)(2,1)} %get-tuple-element.27), channel_id=1, source_target_pairs={{0,2},{1,3},{2,0},{3,1},{4,6},{5,7},{6,4},{7,5},{8,10},{9,11},{10,... | collective-permute-start | bytes 245768 | tf_op jit(solution)/shard_map/ppermute | solution.py:271
  13.2 17.6 %collective-permute-start.3 = (bf16[64,3584]{1,0:T(8,128)(2,1)}, bf16[64,3584]{1,0:T(8,128)(2,1)S(1)}, u32[]{:S(2)}, u32[]{:S(2)}) collective-permute-start(bf16[64,3584]{1,0:T(8,128)(2,1)} %get-tuple-element.29), channel_id=1, source_target_pairs={{0,1},{1,0},{2,3},{3,2},{4,5},{5,4},{6,7},{7,6},{8,9},{9,8},{10,11... | collective-permute-start | bytes 1376264 | tf_op jit(solution)/shard_map/ppermute | solution.py:271
  14.6 17.0 %collective-permute-start.4 = (bf16[64,3584]{1,0:T(8,128)(2,1)}, bf16[64,3584]{1,0:T(8,128)(2,1)S(1)}, u32[]{:S(2)}, u32[]{:S(2)}) collective-permute-start(bf16[64,3584]{1,0:T(8,128)(2,1)} %get-tuple-element.30), channel_id=1, source_target_pairs={{0,2},{1,3},{2,0},{3,1},{4,6},{5,7},{6,4},{7,5},{8,10},{9,11},{10,... | collective-permute-start | bytes 1376264 | tf_op jit(solution)/shard_map/ppermute | solution.py:271
  22.1 1.0 %copy-start.2 = (bf16[64,4224]{1,0:T(8,128)(2,1)S(1)}, bf16[64,4224]{1,0:T(8,128)(2,1)}, u32[]{:S(2)}) copy-start(bf16[64,4224]{1,0:T(8,128)(2,1)} %get-tuple-element.28.refs_1_.refs_0_) | copy-start | bytes 1622020
  23.2 2.2 %copy-start = (bf16[1,128,64,256]{3,2,1,0:T(8,128)(2,1)S(1)}, bf16[1,128,64,256]{3,2,1,0:T(8,128)(2,1)}, u32[]{:S(2)}) copy-start(bf16[1,128,64,256]{3,2,1,0:T(8,128)(2,1)} %param.15) | copy-start | bytes 12582916
  23.2 2.9 %copy-start.1 = (bf16[128,64,128]{2,1,0:T(8,128)(2,1)S(1)}, bf16[128,64,128]{2,1,0:T(8,128)(2,1)}, u32[]{:S(2)}) copy-start(bf16[128,64,128]{2,1,0:T(8,128)(2,1)} %refs_6_.1) | copy-start | bytes 6291460
  23.2 2.9 %copy-start.3 = (f32[1,3,64,128]{3,2,1,0:T(8,128)S(1)}, f32[1,3,64,128]{3,2,1,0:T(8,128)}, u32[]{:S(2)}) copy-start(f32[1,3,64,128]{3,2,1,0:T(8,128)} %param.14) | copy-start | bytes 294916
  32.8 2.4 %collective-permute-start.16 = (bf16[4,32,2048]{2,1,0:T(8,128)(2,1)S(1)}, bf16[4,32,2048]{2,1,0:T(8,128)(2,1)S(1)}, u32[]{:S(2)}, u32[]{:S(2)}) collective-permute-start(bf16[4,32,2048]{2,1,0:T(8,128)(2,1)S(1)} %get-tuple-element.38), channel_id=1, source_target_pairs={{0,4},{4,0},{8,12},{12,8},{16,20},{20,16},{24,28},{28,24},{1,5},{5... | collective-permute-start | bytes 1572872 | tf_op jit(solution)/shard_map/ppermute | solution.py:271
  33.6 3.0 %collective-permute-start.5 = (bf16[4,32,2048]{2,1,0:T(8,128)(2,1)S(1)}, bf16[4,32,2048]{2,1,0:T(8,128)(2,1)S(1)}, u32[]{:S(2)}, u32[]{:S(2)}) collective-permute-start(bf16[4,32,2048]{2,1,0:T(8,128)(2,1)S(1)} %get-tuple-element.32), channel_id=1, source_target_pairs={{0,4},{4,0},{8,12},{12,8},{16,20},{20,16},{24,28},{28,24},{1,5},{5... | collective-permute-start | bytes 1572872 | tf_op jit(solution)/shard_map/ppermute | solution.py:271
  35.3 4.8 %collective-permute-start.17 = (bf16[32,2048]{1,0:T(8,128)(2,1)S(1)}, bf16[32,2048]{1,0:T(8,128)(2,1)S(1)}, u32[]{:S(2)}, u32[]{:S(2)}) collective-permute-start(bf16[32,2048]{1,0:T(8,128)(2,1)S(1)} %get-tuple-element.41), channel_id=1, source_target_pairs={{0,8},{4,12},{8,0},{12,4},{16,24},{20,28},{24,16},{28,20},{1,9},{5... | collective-permute-start | bytes 393224 | tf_op jit(solution)/shard_map/ppermute | solution.py:271
  36.7 7.0 %collective-permute-start.6 = (bf16[32,2048]{1,0:T(8,128)(2,1)S(1)}, bf16[32,2048]{1,0:T(8,128)(2,1)S(1)}, u32[]{:S(2)}, u32[]{:S(2)}) collective-permute-start(bf16[32,2048]{1,0:T(8,128)(2,1)S(1)} %get-tuple-element.35), channel_id=1, source_target_pairs={{0,8},{4,12},{8,0},{12,4},{16,24},{20,28},{24,16},{28,20},{1,9},{5... | collective-permute-start | bytes 393224 | tf_op jit(solution)/shard_map/ppermute | solution.py:271
  40.1 6.5 %collective-permute-start.18 = (bf16[32,2048]{1,0:T(8,128)(2,1)S(1)}, bf16[32,2048]{1,0:T(8,128)(2,1)S(1)}, u32[]{:S(2)}, u32[]{:S(2)}) collective-permute-start(bf16[32,2048]{1,0:T(8,128)(2,1)S(1)} %add_convert_fusion.1), channel_id=1, source_target_pairs={{0,16},{4,20},{8,24},{12,28},{16,0},{20,4},{24,8},{28,12},{1,17},{... | collective-permute-start | bytes 393224 | tf_op jit(solution)/shard_map/ppermute | solution.py:271
  42.5 4.5 %collective-permute-start.19 = (bf16[32,2048]{1,0:T(8,128)(2,1)S(1)}, bf16[32,2048]{1,0:T(8,128)(2,1)S(1)}, u32[]{:S(2)}, u32[]{:S(2)}) collective-permute-start(bf16[32,2048]{1,0:T(8,128)(2,1)S(1)} %get-tuple-element.44), channel_id=1, source_target_pairs={{0,8},{4,12},{8,0},{12,4},{16,24},{20,28},{24,16},{28,20},{1,9},{5... | collective-permute-start | bytes 393224 | tf_op jit(solution)/shard_map/ppermute | solution.py:271
  43.8 12.9 %collective-permute-start.7 = (bf16[32,2048]{1,0:T(8,128)(2,1)S(1)}, bf16[32,2048]{1,0:T(8,128)(2,1)S(1)}, u32[]{:S(2)}, u32[]{:S(2)}) collective-permute-start(bf16[32,2048]{1,0:T(8,128)(2,1)S(1)} %add_convert_fusion.3), channel_id=1, source_target_pairs={{0,16},{4,20},{8,24},{12,28},{16,0},{20,4},{24,8},{28,12},{1,17},{... | collective-permute-start | bytes 393224 | tf_op jit(solution)/shard_map/ppermute | solution.py:271
  45.3 11.4 %collective-permute-start.8 = (bf16[32,2048]{1,0:T(8,128)(2,1)S(1)}, bf16[32,2048]{1,0:T(8,128)(2,1)S(1)}, u32[]{:S(2)}, u32[]{:S(2)}) collective-permute-start(bf16[32,2048]{1,0:T(8,128)(2,1)S(1)} %get-tuple-element.37), channel_id=1, source_target_pairs={{0,8},{4,12},{8,0},{12,4},{16,24},{20,28},{24,16},{28,20},{1,9},{5... | collective-permute-start | bytes 393224 | tf_op jit(solution)/shard_map/ppermute | solution.py:271
  47.0 11.3 %collective-permute-start.21 = (bf16[32,2048]{1,0:T(8,128)(2,1)S(1)}, bf16[32,2048]{1,0:T(8,128)(2,1)S(1)}, u32[]{:S(2)}, u32[]{:S(2)}) collective-permute-start(bf16[32,2048]{1,0:T(8,128)(2,1)S(1)} %add_convert_fusion.refs_0_), channel_id=1, source_target_pairs={{0,16},{4,20},{8,24},{12,28},{16,0},{20,4},{24,8},{28,12},{1,17},{... | collective-permute-start | bytes 393224 | tf_op jit(solution)/shard_map/ppermute | solution.py:271
  50.1 9.9 %collective-permute-start.20 = (bf16[32,2048]{1,0:T(8,128)(2,1)S(1)}, bf16[32,2048]{1,0:T(8,128)(2,1)S(1)}, u32[]{:S(2)}, u32[]{:S(2)}) collective-permute-start(bf16[32,2048]{1,0:T(8,128)(2,1)S(1)} %add_convert_fusion.refs_0_), channel_id=1, source_target_pairs={{0,8},{4,12},{8,0},{12,4},{16,24},{20,28},{24,16},{28,20},{1,9},{5... | collective-permute-start | bytes 393224 | tf_op jit(solution)/shard_map/ppermute | solution.py:271
  53.0 11.4 %collective-permute-start.23 = (bf16[32,2048]{1,0:T(8,128)(2,1)S(1)}, bf16[32,2048]{1,0:T(8,128)(2,1)S(1)}, u32[]{:S(2)}, u32[]{:S(2)}) collective-permute-start(bf16[32,2048]{1,0:T(8,128)(2,1)S(1)} %add_convert_fusion.refs_0_), channel_id=1, source_target_pairs={{0,4},{4,0},{8,12},{12,8},{16,20},{20,16},{24,28},{28,24},{1,5},{5... | collective-permute-start | bytes 393224 | tf_op jit(solution)/shard_map/ppermute | solution.py:271
  56.7 9.1 %collective-permute-start.9 = (bf16[32,2048]{1,0:T(8,128)(2,1)S(1)}, bf16[32,2048]{1,0:T(8,128)(2,1)S(1)}, u32[]{:S(2)}, u32[]{:S(2)}) collective-permute-start(bf16[32,2048]{1,0:T(8,128)(2,1)S(1)} %add_convert_fusion.2.refs_0_), channel_id=1, source_target_pairs={{0,16},{4,20},{8,24},{12,28},{16,0},{20,4},{24,8},{28,12},{1,17},{... | collective-permute-start | bytes 393224 | tf_op jit(solution)/shard_map/ppermute | solution.py:271
  58.2 8.0 %collective-permute-start.22 = (bf16[32,2048]{1,0:T(8,128)(2,1)S(1)}, bf16[32,2048]{1,0:T(8,128)(2,1)S(1)}, u32[]{:S(2)}, u32[]{:S(2)}) collective-permute-start(bf16[32,2048]{1,0:T(8,128)(2,1)S(1)} %collective-permute-done.21.refs_2_), channel_id=1, source_target_pairs={{0,8},{4,12},{8,0},{12,4},{16,24},{20,28},{24,16},{28,20},{1,9},{5... | collective-permute-start | bytes 393224 | tf_op jit(solution)/shard_map/ppermute | solution.py:271
  58.7 10.0 %collective-permute-start.12 = (bf16[32,2048]{1,0:T(8,128)(2,1)S(1)}, bf16[32,2048]{1,0:T(8,128)(2,1)S(1)}, u32[]{:S(2)}, u32[]{:S(2)}) collective-permute-start(bf16[32,2048]{1,0:T(8,128)(2,1)S(1)} %add_convert_fusion.2.refs_0_), channel_id=1, source_target_pairs={{0,8},{4,12},{8,0},{12,4},{16,24},{20,28},{24,16},{28,20},{1,9},{5... | collective-permute-start | bytes 393224 | tf_op jit(solution)/shard_map/ppermute | solution.py:271
  60.0 11.2 %collective-permute-start.24 = (bf16[32,2048]{1,0:T(8,128)(2,1)S(1)}, bf16[32,2048]{1,0:T(8,128)(2,1)S(1)}, u32[]{:S(2)}, u32[]{:S(2)}) collective-permute-start(bf16[32,2048]{1,0:T(8,128)(2,1)S(1)} %collective-permute-done.20.refs_1_), channel_id=1, source_target_pairs={{0,4},{4,0},{8,12},{12,8},{16,20},{20,16},{24,28},{28,24},{1,5},{5... | collective-permute-start | bytes 393224 | tf_op jit(solution)/shard_map/ppermute | solution.py:271
  64.5 6.7 %collective-permute-start.25 = (bf16[32,2048]{1,0:T(8,128)(2,1)S(1)}, bf16[32,2048]{1,0:T(8,128)(2,1)S(1)}, u32[]{:S(2)}, u32[]{:S(2)}) collective-permute-start(bf16[32,2048]{1,0:T(8,128)(2,1)S(1)} %collective-permute-done.21.refs_2_), channel_id=1, source_target_pairs={{0,4},{4,0},{8,12},{12,8},{16,20},{20,16},{24,28},{28,24},{1,5},{5... | collective-permute-start | bytes 393224 | tf_op jit(solution)/shard_map/ppermute | solution.py:271
  65.9 5.9 %collective-permute-start.10 = (bf16[32,2048]{1,0:T(8,128)(2,1)S(1)}, bf16[32,2048]{1,0:T(8,128)(2,1)S(1)}, u32[]{:S(2)}, u32[]{:S(2)}) collective-permute-start(bf16[32,2048]{1,0:T(8,128)(2,1)S(1)} %collective-permute-done.9.refs_2_), channel_id=1, source_target_pairs={{0,8},{4,12},{8,0},{12,4},{16,24},{20,28},{24,16},{28,20},{1,9},{5... | collective-permute-start | bytes 393224 | tf_op jit(solution)/shard_map/ppermute | solution.py:271
  66.3 6.7 %collective-permute-start.26 = (bf16[32,2048]{1,0:T(8,128)(2,1)S(1)}, bf16[32,2048]{1,0:T(8,128)(2,1)S(1)}, u32[]{:S(2)}, u32[]{:S(2)}) collective-permute-start(bf16[32,2048]{1,0:T(8,128)(2,1)S(1)} %collective-permute-done.22.refs_3_), channel_id=1, source_target_pairs={{0,4},{4,0},{8,12},{12,8},{16,20},{20,16},{24,28},{28,24},{1,5},{5... | collective-permute-start | bytes 393224 | tf_op jit(solution)/shard_map/ppermute | solution.py:271
  68.7 5.2 %collective-permute-start.13 = (bf16[32,2048]{1,0:T(8,128)(2,1)S(1)}, bf16[32,2048]{1,0:T(8,128)(2,1)S(1)}, u32[]{:S(2)}, u32[]{:S(2)}) collective-permute-start(bf16[32,2048]{1,0:T(8,128)(2,1)S(1)} %add_convert_fusion.2.refs_0_), channel_id=1, source_target_pairs={{0,4},{4,0},{8,12},{12,8},{16,20},{20,16},{24,28},{28,24},{1,5},{5... | collective-permute-start | bytes 393224 | tf_op jit(solution)/shard_map/ppermute | solution.py:271
  71.2 2.8 %collective-permute-start.15 = (bf16[32,2048]{1,0:T(8,128)(2,1)S(1)}, bf16[32,2048]{1,0:T(8,128)(2,1)S(1)}, u32[]{:S(2)}, u32[]{:S(2)}) collective-permute-start(bf16[32,2048]{1,0:T(8,128)(2,1)S(1)} %collective-permute-done.9.refs_2_), channel_id=1, source_target_pairs={{0,4},{4,0},{8,12},{12,8},{16,20},{20,16},{24,28},{28,24},{1,5},{5... | collective-permute-start | bytes 393224 | tf_op jit(solution)/shard_map/ppermute | solution.py:271
  71.2 2.8 %collective-permute-start.14 = (bf16[32,2048]{1,0:T(8,128)(2,1)S(1)}, bf16[32,2048]{1,0:T(8,128)(2,1)S(1)}, u32[]{:S(2)}, u32[]{:S(2)}) collective-permute-start(bf16[32,2048]{1,0:T(8,128)(2,1)S(1)} %collective-permute-done.12.refs_1_), channel_id=1, source_target_pairs={{0,4},{4,0},{8,12},{12,8},{16,20},{20,16},{24,28},{28,24},{1,5},{5... | collective-permute-start | bytes 393224 | tf_op jit(solution)/shard_map/ppermute | solution.py:271
  71.7 3.2 %collective-permute-start.11 = (bf16[32,2048]{1,0:T(8,128)(2,1)S(1)}, bf16[32,2048]{1,0:T(8,128)(2,1)S(1)}, u32[]{:S(2)}, u32[]{:S(2)}) collective-permute-start(bf16[32,2048]{1,0:T(8,128)(2,1)S(1)} %collective-permute-done.10.refs_0_), channel_id=1, source_target_pairs={{0,4},{4,0},{8,12},{12,8},{16,20},{20,16},{24,28},{28,24},{1,5},{5... | collective-permute-start | bytes 393224 | tf_op jit(solution)/shard_map/ppermute | solution.py:271

commit v8 on v7

--- a/solution.py
+++ b/solution.py
@@ -9,7 +9,7 @@
 from jax.sharding import PartitionSpec as P
 
 STEP = 32
-HEAD = 4
+HEAD = 2
 FIRST_HEAD = 32
 FAR_PIECES = 4
 HALVES = 2

time: 75.9 us -> 75.9 us (level)
  no operation moved by 1% of the time
where the time goes in v8:
time: 75.9 us; the launch traced here: 75.7 us
  starting transfers between devices  38.4 us (51%)
  Pallas kernels  19 us (25%)
  waiting for transfers between devices  13.7 us (18%)
  local copies, waits for them, and re-layouts  4.18 us (6%)
    ppermute x27, starting transfers between devices, swap(): return lax.ppermute(value, axis, [(i, i ^ mask) for i in range(size)])  38.4 us
    ppermute x27, waiting for transfers between devices, swap(): return lax.ppermute(value, axis, [(i, i ^ mask) for i in range(size)])  13.7 us
    pallas_call x2, Pallas kernels, near_products(): pl.pallas_call(functools.partial(near_kernel, parts), out_shape=[jax.Shap...  9.69 us
    pallas_call x1, Pallas kernels, far_field(): pl.pallas_call(functools.partial(far_kernel, groups), out_shape=jax.Shape...  3.82 us
    pallas_call x3, Pallas kernels, place(): pl.pallas_call(functools.partial(place_kernel, masks), out_shape=jax.Shap...  2.68 us
    unnamed x11, local copies, waits for them, and re-layouts  2.63 us
  transfers between devices with their start and end apart: 27, of which 10 were waited for; matrix products, arithmetic and copies ran while one was open for 3% of the time, Pallas kernels for 17%

profile of v8, /device:TPU:1, one launch (start us, length us, event | category | flops | bytes accessed | tf_op | source)
XLA Modules:
  0.0 75.7 jit_solution(10550202183704089582)
XLA Ops:
  0.0 3.9 %shard_map.91 = bf16[64,4224]{1,0:T(8,128)(2,1)} custom-call(s32[1]{0:T(128)} %bitcast.1.me_ref, s32[128]{0:T(128)} %src_ref.3, s32[1,128]{1,0:T(1,128)} %bitcast.11, bf16[64,2048]{1,0:T(8,128)(2,1)} %bitcast.9, bf16[16,64,128]{2,1,0:T(8,128)(2,1)} %basis_ref.3, bf16[128,128,128]{2,1,0:T(8,128)(2,1)} %tiles_ref.3), custom_call_target="tpu_custom_call" | custom-call | tf_op jit(solution)/shard_map/pallas_call | solution.py:94
  3.9 3.1 %collective-permute-start.2 = (bf16[64,4224]{1,0:T(8,128)(2,1)}, bf16[64,4224]{1,0:T(8,128)(2,1)S(1)}, u32[]{:S(2)}, u32[]{:S(2)}) collective-permute-start(bf16[64,4224]{1,0:T(8,128)(2,1)} %shard_map.91), channel_id=1, source_target_pairs={{0,3},{1,2},{2,1},{3,0},{4,7},{5,6},{6,5},{7,4},{8,11},{9,10},{10,... | collective-permute-start | bytes 1622024 | tf_op jit(solution)/shard_map/ppermute | solution.py:271
  7.0 5.8 %shard_map.92 = (bf16[64,384]{1,0:T(8,128)(2,1)}, bf16[64,384]{1,0:T(8,128)(2,1)}, bf16[64,4224]{1,0:T(8,128)(2,1)}, bf16[64,3840]{1,0:T(8,128)(2,1)}, bf16[64,3840]{1,0:T(8,128)(2,1)}) custom-call(s32[1]{0:T(128)} %bitcast.1.me_ref, s32[128]{0:T(128)} %src_ref.3, s32[1,128]{1,0:T(1,128)} %bitcast.12, bf16[64,2048]{1,0:T(8,128)(2,1)} %bitcast.10, ...), custom_call_target="tpu_custom_call" | custom-call | tf_op jit(solution)/shard_map/pallas_call | solution.py:94
  13.1 1.4 %collective-permute-start.3 = (bf16[64,3840]{1,0:T(8,128)(2,1)}, bf16[64,3840]{1,0:T(8,128)(2,1)S(1)}, u32[]{:S(2)}, u32[]{:S(2)}) collective-permute-start(bf16[64,3840]{1,0:T(8,128)(2,1)} %get-tuple-element.29), channel_id=1, source_target_pairs={{0,1},{1,0},{2,3},{3,2},{4,5},{5,4},{6,7},{7,6},{8,9},{9,8},{10,11... | collective-permute-start | bytes 1474568 | tf_op jit(solution)/shard_map/ppermute | solution.py:271
  14.5 1.2 %collective-permute-start.4 = (bf16[64,3840]{1,0:T(8,128)(2,1)}, bf16[64,3840]{1,0:T(8,128)(2,1)S(1)}, u32[]{:S(2)}, u32[]{:S(2)}) collective-permute-start(bf16[64,3840]{1,0:T(8,128)(2,1)} %get-tuple-element.30), channel_id=1, source_target_pairs={{0,2},{1,3},{2,0},{3,1},{4,6},{5,7},{6,4},{7,5},{8,10},{9,11},{10,... | collective-permute-start | bytes 1474568 | tf_op jit(solution)/shard_map/ppermute | solution.py:271
  15.8 0.8 %slice.17 = bf16[2,64]{1,0:T(2,128)(2,1)S(1)} slice(bf16[64,4224]{1,0:T(8,128)(2,1)} %get-tuple-element.28.refs_1_.refs_0_), slice={[0:64:32], [4160:4224:1]} | slice | bytes 512 | tf_op jit(solution)/shard_map/slice | solution.py:345
  17.0 3.3 %collective-permute-done.refs_1_.refs_0_ = bf16[64,384]{1,0:T(8,128)(2,1)S(1)} collective-permute-done((bf16[64,384]{1,0:T(8,128)(2,1)}, bf16[64,384]{1,0:T(8,128)(2,1)S(1)}, u32[]{:S(2)}, u32[]{:S(2)}) %collective-permute-start) | collective-permute-done | bytes 49184 | tf_op jit(solution)/shard_map/ppermute | solution.py:271
  21.4 1.0 %copy-done.2 = bf16[64,4224]{1,0:T(8,128)(2,1)S(1)} copy-done((bf16[64,4224]{1,0:T(8,128)(2,1)S(1)}, bf16[64,4224]{1,0:T(8,128)(2,1)}, u32[]{:S(2)}) %copy-start.2) | copy-done | bytes 540696
  22.5 1.4 %shard_map.93.refs_7_ = f32[8,64,2048]{2,1,0:T(8,128)S(1)} custom-call(s32[1]{0:T(128)} %bitcast.1.me_ref, s32[2,128]{1,0:T(2,128)S(1)} %convert_convert_fusion.1.tgt_ref, bf16[64,4224]{1,0:T(8,128)(2,1)S(1)} %collective-permute-done.2.refs_0_.refs_3_, bf16[64,4224]{1,0:T(8,128)(2,1)S(1)} %copy-done.2), custom_call_target="tpu_custom_call" | custom-call | flops 68719476736 | bytes 16777216 | tf_op jit(solution)/shard_map/pallas_call | solution.py:128
  25.3 3.8 %shard_map.94.far_ref = f32[8,64,2048]{2,1,0:T(8,128)S(1)} custom-call(s32[1]{0:T(128)} %bitcast.1.me_ref, s32[512]{0:T(512)S(1)} %reshape_squeeze.3.node_ref, bf16[64,4224]{1,0:T(8,128)(2,1)S(1)} %copy-done.2, bf16[64,384]{1,0:T(8,128)(2,1)S(1)} %collective-permute-done.refs_1_.refs_0_, ...), custom_call_target="tpu_custom_call", output_to_operand_aliasing={{}: (9, {})} | custom-call | tf_op jit(solution)/shard_map/pallas_call | solution.py:182
  29.1 1.6 %collective-permute-done.3.refs_2_ = bf16[64,3840]{1,0:T(8,128)(2,1)S(1)} collective-permute-done((bf16[64,3840]{1,0:T(8,128)(2,1)}, bf16[64,3840]{1,0:T(8,128)(2,1)S(1)}, u32[]{:S(2)}, u32[]{:S(2)}) %collective-permute-start.3) | collective-permute-done | bytes 491552 | tf_op jit(solution)/shard_map/ppermute | solution.py:271
  31.5 1.3 %shard_map.95 = (f32[8,64,2048]{2,1,0:T(8,128)S(1)}, bf16[4,32,2048]{2,1,0:T(8,128)(2,1)S(1)}, bf16[4,32,2048]{2,1,0:T(8,128)(2,1)S(1)}) custom-call(s32[2]{0:T(128)S(1)} %pad_add_fusion.me_ref, s32[4,128]{1,0:T(4,128)S(1)} %convert_convert_fusion.tgt_ref, f32[8,64,2048]{2,1,0:T(8,128)S(1)} %shard_map.94.far_ref, ...), custom_call_target="tpu_custom_call", output_to_operand_aliasing={{0}: (2, {})} | custom-call | tf_op jit(solution)/shard_map/pallas_call | solution.py:210
  32.8 0.9 %collective-permute-start.16 = (bf16[4,32,2048]{2,1,0:T(8,128)(2,1)S(1)}, bf16[4,32,2048]{2,1,0:T(8,128)(2,1)S(1)}, u32[]{:S(2)}, u32[]{:S(2)}) collective-permute-start(bf16[4,32,2048]{2,1,0:T(8,128)(2,1)S(1)} %get-tuple-element.38), channel_id=1, source_target_pairs={{0,4},{4,0},{8,12},{12,8},{16,20},{20,16},{24,28},{28,24},{1,5},{5... | collective-permute-start | bytes 1572872 | tf_op jit(solution)/shard_map/ppermute | solution.py:271
  33.7 1.5 %collective-permute-done.16.got_ref = bf16[4,32,2048]{2,1,0:T(8,128)(2,1)S(1)} collective-permute-done((bf16[4,32,2048]{2,1,0:T(8,128)(2,1)S(1)}, bf16[4,32,2048]{2,1,0:T(8,128)(2,1)S(1)}, u32[]{:S(2)}, u32[]{:S(2)}) %collective-permute-start.16) | collective-permute-done | bytes 524320 | tf_op jit(solution)/shard_map/ppermute | solution.py:271
  35.3 1.4 %collective-permute-start.17 = (bf16[32,2048]{1,0:T(8,128)(2,1)S(1)}, bf16[32,2048]{1,0:T(8,128)(2,1)S(1)}, u32[]{:S(2)}, u32[]{:S(2)}) collective-permute-start(bf16[32,2048]{1,0:T(8,128)(2,1)S(1)} %get-tuple-element.41), channel_id=1, source_target_pairs={{0,8},{4,12},{8,0},{12,4},{16,24},{20,28},{24,16},{28,20},{1,9},{5... | collective-permute-start | bytes 393224 | tf_op jit(solution)/shard_map/ppermute | solution.py:271
  37.4 2.7 %collective-permute-done.17 = bf16[32,2048]{1,0:T(8,128)(2,1)S(1)} collective-permute-done((bf16[32,2048]{1,0:T(8,128)(2,1)S(1)}, bf16[32,2048]{1,0:T(8,128)(2,1)S(1)}, u32[]{:S(2)}, u32[]{:S(2)}) %collective-permute-start.17) | collective-permute-done | bytes 131104 | tf_op jit(solution)/shard_map/ppermute | solution.py:271
  40.1 2.4 %collective-permute-start.18 = (bf16[32,2048]{1,0:T(8,128)(2,1)S(1)}, bf16[32,2048]{1,0:T(8,128)(2,1)S(1)}, u32[]{:S(2)}, u32[]{:S(2)}) collective-permute-start(bf16[32,2048]{1,0:T(8,128)(2,1)S(1)} %add_convert_fusion.1), channel_id=1, source_target_pairs={{0,16},{4,20},{8,24},{12,28},{16,0},{20,4},{24,8},{28,12},{1,17},{... | collective-permute-start | bytes 393224 | tf_op jit(solution)/shard_map/ppermute | solution.py:271
  42.5 1.3 %collective-permute-start.19 = (bf16[32,2048]{1,0:T(8,128)(2,1)S(1)}, bf16[32,2048]{1,0:T(8,128)(2,1)S(1)}, u32[]{:S(2)}, u32[]{:S(2)}) collective-permute-start(bf16[32,2048]{1,0:T(8,128)(2,1)S(1)} %get-tuple-element.44), channel_id=1, source_target_pairs={{0,8},{4,12},{8,0},{12,4},{16,24},{20,28},{24,16},{28,20},{1,9},{5... | collective-permute-start | bytes 393224 | tf_op jit(solution)/shard_map/ppermute | solution.py:271
  43.8 1.5 %collective-permute-start.7 = (bf16[32,2048]{1,0:T(8,128)(2,1)S(1)}, bf16[32,2048]{1,0:T(8,128)(2,1)S(1)}, u32[]{:S(2)}, u32[]{:S(2)}) collective-permute-start(bf16[32,2048]{1,0:T(8,128)(2,1)S(1)} %add_convert_fusion.3), channel_id=1, source_target_pairs={{0,16},{4,20},{8,24},{12,28},{16,0},{20,4},{24,8},{28,12},{1,17},{... | collective-permute-start | bytes 393224 | tf_op jit(solution)/shard_map/ppermute | solution.py:271
  45.3 1.3 %collective-permute-start.8 = (bf16[32,2048]{1,0:T(8,128)(2,1)S(1)}, bf16[32,2048]{1,0:T(8,128)(2,1)S(1)}, u32[]{:S(2)}, u32[]{:S(2)}) collective-permute-start(bf16[32,2048]{1,0:T(8,128)(2,1)S(1)} %get-tuple-element.37), channel_id=1, source_target_pairs={{0,8},{4,12},{8,0},{12,4},{16,24},{20,28},{24,16},{28,20},{1,9},{5... | collective-permute-start | bytes 393224 | tf_op jit(solution)/shard_map/ppermute | solution.py:271
  47.0 3.1 %collective-permute-start.21 = (bf16[32,2048]{1,0:T(8,128)(2,1)S(1)}, bf16[32,2048]{1,0:T(8,128)(2,1)S(1)}, u32[]{:S(2)}, u32[]{:S(2)}) collective-permute-start(bf16[32,2048]{1,0:T(8,128)(2,1)S(1)} %add_convert_fusion.refs_0_), channel_id=1, source_target_pairs={{0,16},{4,20},{8,24},{12,28},{16,0},{20,4},{24,8},{28,12},{1,17},{... | collective-permute-start | bytes 393224 | tf_op jit(solution)/shard_map/ppermute | solution.py:271
  50.1 2.9 %collective-permute-start.20 = (bf16[32,2048]{1,0:T(8,128)(2,1)S(1)}, bf16[32,2048]{1,0:T(8,128)(2,1)S(1)}, u32[]{:S(2)}, u32[]{:S(2)}) collective-permute-start(bf16[32,2048]{1,0:T(8,128)(2,1)S(1)} %add_convert_fusion.refs_0_), channel_id=1, source_target_pairs={{0,8},{4,12},{8,0},{12,4},{16,24},{20,28},{24,16},{28,20},{1,9},{5... | collective-permute-start | bytes 393224 | tf_op jit(solution)/shard_map/ppermute | solution.py:271
  53.0 3.6 %collective-permute-start.23 = (bf16[32,2048]{1,0:T(8,128)(2,1)S(1)}, bf16[32,2048]{1,0:T(8,128)(2,1)S(1)}, u32[]{:S(2)}, u32[]{:S(2)}) collective-permute-start(bf16[32,2048]{1,0:T(8,128)(2,1)S(1)} %add_convert_fusion.refs_0_), channel_id=1, source_target_pairs={{0,4},{4,0},{8,12},{12,8},{16,20},{20,16},{24,28},{28,24},{1,5},{5... | collective-permute-start | bytes 393224 | tf_op jit(solution)/shard_map/ppermute | solution.py:271
  56.9 1.3 %collective-permute-done.21.refs_2_ = bf16[32,2048]{1,0:T(8,128)(2,1)S(1)} collective-permute-done((bf16[32,2048]{1,0:T(8,128)(2,1)S(1)}, bf16[32,2048]{1,0:T(8,128)(2,1)S(1)}, u32[]{:S(2)}, u32[]{:S(2)}) %collective-permute-start.21) | collective-permute-done | bytes 131104 | tf_op jit(solution)/shard_map/ppermute | solution.py:271
  58.7 1.0 %collective-permute-start.12 = (bf16[32,2048]{1,0:T(8,128)(2,1)S(1)}, bf16[32,2048]{1,0:T(8,128)(2,1)S(1)}, u32[]{:S(2)}, u32[]{:S(2)}) collective-permute-start(bf16[32,2048]{1,0:T(8,128)(2,1)S(1)} %add_convert_fusion.2.refs_0_), channel_id=1, source_target_pairs={{0,8},{4,12},{8,0},{12,4},{16,24},{20,28},{24,16},{28,20},{1,9},{5... | collective-permute-start | bytes 393224 | tf_op jit(solution)/shard_map/ppermute | solution.py:271
  60.0 4.5 %collective-permute-start.24 = (bf16[32,2048]{1,0:T(8,128)(2,1)S(1)}, bf16[32,2048]{1,0:T(8,128)(2,1)S(1)}, u32[]{:S(2)}, u32[]{:S(2)}) collective-permute-start(bf16[32,2048]{1,0:T(8,128)(2,1)S(1)} %collective-permute-done.20.refs_1_), channel_id=1, source_target_pairs={{0,4},{4,0},{8,12},{12,8},{16,20},{20,16},{24,28},{28,24},{1,5},{5... | collective-permute-start | bytes 393224 | tf_op jit(solution)/shard_map/ppermute | solution.py:271
  64.6 1.3 %collective-permute-done.9.refs_2_ = bf16[32,2048]{1,0:T(8,128)(2,1)S(1)} collective-permute-done((bf16[32,2048]{1,0:T(8,128)(2,1)S(1)}, bf16[32,2048]{1,0:T(8,128)(2,1)S(1)}, u32[]{:S(2)}, u32[]{:S(2)}) %collective-permute-start.9) | collective-permute-done | bytes 131104 | tf_op jit(solution)/shard_map/ppermute | solution.py:271
  66.3 2.5 %collective-permute-start.26 = (bf16[32,2048]{1,0:T(8,128)(2,1)S(1)}, bf16[32,2048]{1,0:T(8,128)(2,1)S(1)}, u32[]{:S(2)}, u32[]{:S(2)}) collective-permute-start(bf16[32,2048]{1,0:T(8,128)(2,1)S(1)} %collective-permute-done.22.refs_3_), channel_id=1, source_target_pairs={{0,4},{4,0},{8,12},{12,8},{16,20},{20,16},{24,28},{28,24},{1,5},{5... | collective-permute-start | bytes 393224 | tf_op jit(solution)/shard_map/ppermute | solution.py:271
  68.7 2.5 %collective-permute-start.13 = (bf16[32,2048]{1,0:T(8,128)(2,1)S(1)}, bf16[32,2048]{1,0:T(8,128)(2,1)S(1)}, u32[]{:S(2)}, u32[]{:S(2)}) collective-permute-start(bf16[32,2048]{1,0:T(8,128)(2,1)S(1)} %add_convert_fusion.2.refs_0_), channel_id=1, source_target_pairs={{0,4},{4,0},{8,12},{12,8},{16,20},{20,16},{24,28},{28,24},{1,5},{5... | collective-permute-start | bytes 393224 | tf_op jit(solution)/shard_map/ppermute | solution.py:271
  71.7 1.2 %collective-permute-start.11 = (bf16[32,2048]{1,0:T(8,128)(2,1)S(1)}, bf16[32,2048]{1,0:T(8,128)(2,1)S(1)}, u32[]{:S(2)}, u32[]{:S(2)}) collective-permute-start(bf16[32,2048]{1,0:T(8,128)(2,1)S(1)} %collective-permute-done.10.refs_0_), channel_id=1, source_target_pairs={{0,4},{4,0},{8,12},{12,8},{16,20},{20,16},{24,28},{28,24},{1,5},{5... | collective-permute-start | bytes 393224 | tf_op jit(solution)/shard_map/ppermute | solution.py:271
  72.9 1.0 %shard_map.98.refs_6_ = bf16[64,16384]{1,0:T(8,128)(2,1)} custom-call(s32[1]{0:T(128)} %bitcast.me_ref, bf16[32,2048]{1,0:T(8,128)(2,1)S(1)} %add_convert_fusion.refs_0_, bf16[32,2048]{1,0:T(8,128)(2,1)S(1)} %collective-permute-done.20.refs_1_, bf16[32,2048]{1,0:T(8,128)(2,1)S(1)} %collective-permute-done.21.refs_2_, ...), custom_call_target="tpu_custom_call" | custom-call | flops 68719476736 | bytes 16777216 | tf_op jit(solution)/shard_map/pallas_call | solution.py:257
  74.0 0.9 %shard_map.99.refs_2_ = bf16[64,16384]{1,0:T(8,128)(2,1)} custom-call(s32[1]{0:T(128)} %bitcast.me_ref, bf16[32,2048]{1,0:T(8,128)(2,1)S(1)} %add_convert_fusion.2.refs_0_, bf16[32,2048]{1,0:T(8,128)(2,1)S(1)} %collective-permute-done.12.refs_1_, bf16[32,2048]{1,0:T(8,128)(2,1)S(1)} %collective-permute-done.9.refs_2_, ...), custom_call_target="tpu_custom_call", output_to_operand_aliasing={{}: (7, {})} | custom-call | flops 68719476736 | bytes 16777216 | tf_op jit(solution)/shard_map/pallas_call | solution.py:257
  (59 shorter events, 8.3 us)
Async XLA Ops:
  0.0 16.7 %copy-start.4 = (s32[1,128,4]{1,2,0:T(4,128)S(1)}, s32[1,128,4]{1,2,0:T(4,128)}, u32[]{:S(2)}) copy-start(s32[1,128,4]{1,2,0:T(4,128)} %param.16) | copy-start | bytes 6148
  3.9 17.3 %collective-permute-start.2 = (bf16[64,4224]{1,0:T(8,128)(2,1)}, bf16[64,4224]{1,0:T(8,128)(2,1)S(1)}, u32[]{:S(2)}, u32[]{:S(2)}) collective-permute-start(bf16[64,4224]{1,0:T(8,128)(2,1)} %shard_map.91), channel_id=1, source_target_pairs={{0,3},{1,2},{2,1},{3,0},{4,7},{5,6},{6,5},{7,4},{8,11},{9,10},{10,... | collective-permute-start | bytes 1622024 | tf_op jit(solution)/shard_map/ppermute | solution.py:271
  12.8 7.5 %collective-permute-start = (bf16[64,384]{1,0:T(8,128)(2,1)}, bf16[64,384]{1,0:T(8,128)(2,1)S(1)}, u32[]{:S(2)}, u32[]{:S(2)}) collective-permute-start(bf16[64,384]{1,0:T(8,128)(2,1)} %get-tuple-element.26), channel_id=1, source_target_pairs={{0,1},{1,0},{2,3},{3,2},{4,5},{5,4},{6,7},{7,6},{8,9},{9,8},{10,11... | collective-permute-start | bytes 147464 | tf_op jit(solution)/shard_map/ppermute | solution.py:271
  13.1 7.9 %collective-permute-start.1 = (bf16[64,384]{1,0:T(8,128)(2,1)}, bf16[64,384]{1,0:T(8,128)(2,1)S(1)}, u32[]{:S(2)}, u32[]{:S(2)}) collective-permute-start(bf16[64,384]{1,0:T(8,128)(2,1)} %get-tuple-element.27), channel_id=1, source_target_pairs={{0,2},{1,3},{2,0},{3,1},{4,6},{5,7},{6,4},{7,5},{8,10},{9,11},{10,... | collective-permute-start | bytes 147464 | tf_op jit(solution)/shard_map/ppermute | solution.py:271
  13.1 17.6 %collective-permute-start.3 = (bf16[64,3840]{1,0:T(8,128)(2,1)}, bf16[64,3840]{1,0:T(8,128)(2,1)S(1)}, u32[]{:S(2)}, u32[]{:S(2)}) collective-permute-start(bf16[64,3840]{1,0:T(8,128)(2,1)} %get-tuple-element.29), channel_id=1, source_target_pairs={{0,1},{1,0},{2,3},{3,2},{4,5},{5,4},{6,7},{7,6},{8,9},{9,8},{10,11... | collective-permute-start | bytes 1474568 | tf_op jit(solution)/shard_map/ppermute | solution.py:271
  14.5 17.0 %collective-permute-start.4 = (bf16[64,3840]{1,0:T(8,128)(2,1)}, bf16[64,3840]{1,0:T(8,128)(2,1)S(1)}, u32[]{:S(2)}, u32[]{:S(2)}) collective-permute-start(bf16[64,3840]{1,0:T(8,128)(2,1)} %get-tuple-element.30), channel_id=1, source_target_pairs={{0,2},{1,3},{2,0},{3,1},{4,6},{5,7},{6,4},{7,5},{8,10},{9,11},{10,... | collective-permute-start | bytes 1474568 | tf_op jit(solution)/shard_map/ppermute | solution.py:271
  21.4 1.0 %copy-start.2 = (bf16[64,4224]{1,0:T(8,128)(2,1)S(1)}, bf16[64,4224]{1,0:T(8,128)(2,1)}, u32[]{:S(2)}) copy-start(bf16[64,4224]{1,0:T(8,128)(2,1)} %get-tuple-element.28.refs_1_.refs_0_) | copy-start | bytes 1622020
  22.4 2.2 %copy-start = (bf16[1,128,64,256]{3,2,1,0:T(8,128)(2,1)S(1)}, bf16[1,128,64,256]{3,2,1,0:T(8,128)(2,1)}, u32[]{:S(2)}) copy-start(bf16[1,128,64,256]{3,2,1,0:T(8,128)(2,1)} %param.15) | copy-start | bytes 12582916
  22.4 2.9 %copy-start.1 = (bf16[128,64,128]{2,1,0:T(8,128)(2,1)S(1)}, bf16[128,64,128]{2,1,0:T(8,128)(2,1)}, u32[]{:S(2)}) copy-start(bf16[128,64,128]{2,1,0:T(8,128)(2,1)} %refs_6_.1) | copy-start | bytes 6291460
  22.5 2.9 %copy-start.3 = (f32[1,3,64,128]{3,2,1,0:T(8,128)S(1)}, f32[1,3,64,128]{3,2,1,0:T(8,128)}, u32[]{:S(2)}) copy-start(f32[1,3,64,128]{3,2,1,0:T(8,128)} %param.14) | copy-start | bytes 294916
  32.8 2.4 %collective-permute-start.16 = (bf16[4,32,2048]{2,1,0:T(8,128)(2,1)S(1)}, bf16[4,32,2048]{2,1,0:T(8,128)(2,1)S(1)}, u32[]{:S(2)}, u32[]{:S(2)}) collective-permute-start(bf16[4,32,2048]{2,1,0:T(8,128)(2,1)S(1)} %get-tuple-element.38), channel_id=1, source_target_pairs={{0,4},{4,0},{8,12},{12,8},{16,20},{20,16},{24,28},{28,24},{1,5},{5... | collective-permute-start | bytes 1572872 | tf_op jit(solution)/shard_map/ppermute | solution.py:271
  33.6 3.0 %collective-permute-start.5 = (bf16[4,32,2048]{2,1,0:T(8,128)(2,1)S(1)}, bf16[4,32,2048]{2,1,0:T(8,128)(2,1)S(1)}, u32[]{:S(2)}, u32[]{:S(2)}) collective-permute-start(bf16[4,32,2048]{2,1,0:T(8,128)(2,1)S(1)} %get-tuple-element.32), channel_id=1, source_target_pairs={{0,4},{4,0},{8,12},{12,8},{16,20},{20,16},{24,28},{28,24},{1,5},{5... | collective-permute-start | bytes 1572872 | tf_op jit(solution)/shard_map/ppermute | solution.py:271
  35.3 4.8 %collective-permute-start.17 = (bf16[32,2048]{1,0:T(8,128)(2,1)S(1)}, bf16[32,2048]{1,0:T(8,128)(2,1)S(1)}, u32[]{:S(2)}, u32[]{:S(2)}) collective-permute-start(bf16[32,2048]{1,0:T(8,128)(2,1)S(1)} %get-tuple-element.41), channel_id=1, source_target_pairs={{0,8},{4,12},{8,0},{12,4},{16,24},{20,28},{24,16},{28,20},{1,9},{5... | collective-permute-start | bytes 393224 | tf_op jit(solution)/shard_map/ppermute | solution.py:271
  36.7 7.0 %collective-permute-start.6 = (bf16[32,2048]{1,0:T(8,128)(2,1)S(1)}, bf16[32,2048]{1,0:T(8,128)(2,1)S(1)}, u32[]{:S(2)}, u32[]{:S(2)}) collective-permute-start(bf16[32,2048]{1,0:T(8,128)(2,1)S(1)} %get-tuple-element.35), channel_id=1, source_target_pairs={{0,8},{4,12},{8,0},{12,4},{16,24},{20,28},{24,16},{28,20},{1,9},{5... | collective-permute-start | bytes 393224 | tf_op jit(solution)/shard_map/ppermute | solution.py:271
  40.1 6.5 %collective-permute-start.18 = (bf16[32,2048]{1,0:T(8,128)(2,1)S(1)}, bf16[32,2048]{1,0:T(8,128)(2,1)S(1)}, u32[]{:S(2)}, u32[]{:S(2)}) collective-permute-start(bf16[32,2048]{1,0:T(8,128)(2,1)S(1)} %add_convert_fusion.1), channel_id=1, source_target_pairs={{0,16},{4,20},{8,24},{12,28},{16,0},{20,4},{24,8},{28,12},{1,17},{... | collective-permute-start | bytes 393224 | tf_op jit(solution)/shard_map/ppermute | solution.py:271
  42.5 4.5 %collective-permute-start.19 = (bf16[32,2048]{1,0:T(8,128)(2,1)S(1)}, bf16[32,2048]{1,0:T(8,128)(2,1)S(1)}, u32[]{:S(2)}, u32[]{:S(2)}) collective-permute-start(bf16[32,2048]{1,0:T(8,128)(2,1)S(1)} %get-tuple-element.44), channel_id=1, source_target_pairs={{0,8},{4,12},{8,0},{12,4},{16,24},{20,28},{24,16},{28,20},{1,9},{5... | collective-permute-start | bytes 393224 | tf_op jit(solution)/shard_map/ppermute | solution.py:271
  43.8 12.9 %collective-permute-start.7 = (bf16[32,2048]{1,0:T(8,128)(2,1)S(1)}, bf16[32,2048]{1,0:T(8,128)(2,1)S(1)}, u32[]{:S(2)}, u32[]{:S(2)}) collective-permute-start(bf16[32,2048]{1,0:T(8,128)(2,1)S(1)} %add_convert_fusion.3), channel_id=1, source_target_pairs={{0,16},{4,20},{8,24},{12,28},{16,0},{20,4},{24,8},{28,12},{1,17},{... | collective-permute-start | bytes 393224 | tf_op jit(solution)/shard_map/ppermute | solution.py:271
  45.3 11.4 %collective-permute-start.8 = (bf16[32,2048]{1,0:T(8,128)(2,1)S(1)}, bf16[32,2048]{1,0:T(8,128)(2,1)S(1)}, u32[]{:S(2)}, u32[]{:S(2)}) collective-permute-start(bf16[32,2048]{1,0:T(8,128)(2,1)S(1)} %get-tuple-element.37), channel_id=1, source_target_pairs={{0,8},{4,12},{8,0},{12,4},{16,24},{20,28},{24,16},{28,20},{1,9},{5... | collective-permute-start | bytes 393224 | tf_op jit(solution)/shard_map/ppermute | solution.py:271
  47.0 11.2 %collective-permute-start.21 = (bf16[32,2048]{1,0:T(8,128)(2,1)S(1)}, bf16[32,2048]{1,0:T(8,128)(2,1)S(1)}, u32[]{:S(2)}, u32[]{:S(2)}) collective-permute-start(bf16[32,2048]{1,0:T(8,128)(2,1)S(1)} %add_convert_fusion.refs_0_), channel_id=1, source_target_pairs={{0,16},{4,20},{8,24},{12,28},{16,0},{20,4},{24,8},{28,12},{1,17},{... | collective-permute-start | bytes 393224 | tf_op jit(solution)/shard_map/ppermute | solution.py:271
  50.1 9.9 %collective-permute-start.20 = (bf16[32,2048]{1,0:T(8,128)(2,1)S(1)}, bf16[32,2048]{1,0:T(8,128)(2,1)S(1)}, u32[]{:S(2)}, u32[]{:S(2)}) collective-permute-start(bf16[32,2048]{1,0:T(8,128)(2,1)S(1)} %add_convert_fusion.refs_0_), channel_id=1, source_target_pairs={{0,8},{4,12},{8,0},{12,4},{16,24},{20,28},{24,16},{28,20},{1,9},{5... | collective-permute-start | bytes 393224 | tf_op jit(solution)/shard_map/ppermute | solution.py:271
  53.0 11.4 %collective-permute-start.23 = (bf16[32,2048]{1,0:T(8,128)(2,1)S(1)}, bf16[32,2048]{1,0:T(8,128)(2,1)S(1)}, u32[]{:S(2)}, u32[]{:S(2)}) collective-permute-start(bf16[32,2048]{1,0:T(8,128)(2,1)S(1)} %add_convert_fusion.refs_0_), channel_id=1, source_target_pairs={{0,4},{4,0},{8,12},{12,8},{16,20},{20,16},{24,28},{28,24},{1,5},{5... | collective-permute-start | bytes 393224 | tf_op jit(solution)/shard_map/ppermute | solution.py:271
  56.7 9.1 %collective-permute-start.9 = (bf16[32,2048]{1,0:T(8,128)(2,1)S(1)}, bf16[32,2048]{1,0:T(8,128)(2,1)S(1)}, u32[]{:S(2)}, u32[]{:S(2)}) collective-permute-start(bf16[32,2048]{1,0:T(8,128)(2,1)S(1)} %add_convert_fusion.2.refs_0_), channel_id=1, source_target_pairs={{0,16},{4,20},{8,24},{12,28},{16,0},{20,4},{24,8},{28,12},{1,17},{... | collective-permute-start | bytes 393224 | tf_op jit(solution)/shard_map/ppermute | solution.py:271
  58.2 8.0 %collective-permute-start.22 = (bf16[32,2048]{1,0:T(8,128)(2,1)S(1)}, bf16[32,2048]{1,0:T(8,128)(2,1)S(1)}, u32[]{:S(2)}, u32[]{:S(2)}) collective-permute-start(bf16[32,2048]{1,0:T(8,128)(2,1)S(1)} %collective-permute-done.21.refs_2_), channel_id=1, source_target_pairs={{0,8},{4,12},{8,0},{12,4},{16,24},{20,28},{24,16},{28,20},{1,9},{5... | collective-permute-start | bytes 393224 | tf_op jit(solution)/shard_map/ppermute | solution.py:271
  58.7 10.0 %collective-permute-start.12 = (bf16[32,2048]{1,0:T(8,128)(2,1)S(1)}, bf16[32,2048]{1,0:T(8,128)(2,1)S(1)}, u32[]{:S(2)}, u32[]{:S(2)}) collective-permute-start(bf16[32,2048]{1,0:T(8,128)(2,1)S(1)} %add_convert_fusion.2.refs_0_), channel_id=1, source_target_pairs={{0,8},{4,12},{8,0},{12,4},{16,24},{20,28},{24,16},{28,20},{1,9},{5... | collective-permute-start | bytes 393224 | tf_op jit(solution)/shard_map/ppermute | solution.py:271
  60.0 11.2 %collective-permute-start.24 = (bf16[32,2048]{1,0:T(8,128)(2,1)S(1)}, bf16[32,2048]{1,0:T(8,128)(2,1)S(1)}, u32[]{:S(2)}, u32[]{:S(2)}) collective-permute-start(bf16[32,2048]{1,0:T(8,128)(2,1)S(1)} %collective-permute-done.20.refs_1_), channel_id=1, source_target_pairs={{0,4},{4,0},{8,12},{12,8},{16,20},{20,16},{24,28},{28,24},{1,5},{5... | collective-permute-start | bytes 393224 | tf_op jit(solution)/shard_map/ppermute | solution.py:271
  64.5 6.7 %collective-permute-start.25 = (bf16[32,2048]{1,0:T(8,128)(2,1)S(1)}, bf16[32,2048]{1,0:T(8,128)(2,1)S(1)}, u32[]{:S(2)}, u32[]{:S(2)}) collective-permute-start(bf16[32,2048]{1,0:T(8,128)(2,1)S(1)} %collective-permute-done.21.refs_2_), channel_id=1, source_target_pairs={{0,4},{4,0},{8,12},{12,8},{16,20},{20,16},{24,28},{28,24},{1,5},{5... | collective-permute-start | bytes 393224 | tf_op jit(solution)/shard_map/ppermute | solution.py:271
  65.9 5.9 %collective-permute-start.10 = (bf16[32,2048]{1,0:T(8,128)(2,1)S(1)}, bf16[32,2048]{1,0:T(8,128)(2,1)S(1)}, u32[]{:S(2)}, u32[]{:S(2)}) collective-permute-start(bf16[32,2048]{1,0:T(8,128)(2,1)S(1)} %collective-permute-done.9.refs_2_), channel_id=1, source_target_pairs={{0,8},{4,12},{8,0},{12,4},{16,24},{20,28},{24,16},{28,20},{1,9},{5... | collective-permute-start | bytes 393224 | tf_op jit(solution)/shard_map/ppermute | solution.py:271
  66.3 6.7 %collective-permute-start.26 = (bf16[32,2048]{1,0:T(8,128)(2,1)S(1)}, bf16[32,2048]{1,0:T(8,128)(2,1)S(1)}, u32[]{:S(2)}, u32[]{:S(2)}) collective-permute-start(bf16[32,2048]{1,0:T(8,128)(2,1)S(1)} %collective-permute-done.22.refs_3_), channel_id=1, source_target_pairs={{0,4},{4,0},{8,12},{12,8},{16,20},{20,16},{24,28},{28,24},{1,5},{5... | collective-permute-start | bytes 393224 | tf_op jit(solution)/shard_map/ppermute | solution.py:271
  68.7 5.2 %collective-permute-start.13 = (bf16[32,2048]{1,0:T(8,128)(2,1)S(1)}, bf16[32,2048]{1,0:T(8,128)(2,1)S(1)}, u32[]{:S(2)}, u32[]{:S(2)}) collective-permute-start(bf16[32,2048]{1,0:T(8,128)(2,1)S(1)} %add_convert_fusion.2.refs_0_), channel_id=1, source_target_pairs={{0,4},{4,0},{8,12},{12,8},{16,20},{20,16},{24,28},{28,24},{1,5},{5... | collective-permute-start | bytes 393224 | tf_op jit(solution)/shard_map/ppermute | solution.py:271
  71.2 2.8 %collective-permute-start.15 = (bf16[32,2048]{1,0:T(8,128)(2,1)S(1)}, bf16[32,2048]{1,0:T(8,128)(2,1)S(1)}, u32[]{:S(2)}, u32[]{:S(2)}) collective-permute-start(bf16[32,2048]{1,0:T(8,128)(2,1)S(1)} %collective-permute-done.9.refs_2_), channel_id=1, source_target_pairs={{0,4},{4,0},{8,12},{12,8},{16,20},{20,16},{24,28},{28,24},{1,5},{5... | collective-permute-start | bytes 393224 | tf_op jit(solution)/shard_map/ppermute | solution.py:271
  71.2 2.8 %collective-permute-start.14 = (bf16[32,2048]{1,0:T(8,128)(2,1)S(1)}, bf16[32,2048]{1,0:T(8,128)(2,1)S(1)}, u32[]{:S(2)}, u32[]{:S(2)}) collective-permute-start(bf16[32,2048]{1,0:T(8,128)(2,1)S(1)} %collective-permute-done.12.refs_1_), channel_id=1, source_target_pairs={{0,4},{4,0},{8,12},{12,8},{16,20},{20,16},{24,28},{28,24},{1,5},{5... | collective-permute-start | bytes 393224 | tf_op jit(solution)/shard_map/ppermute | solution.py:271
  71.7 3.2 %collective-permute-start.11 = (bf16[32,2048]{1,0:T(8,128)(2,1)S(1)}, bf16[32,2048]{1,0:T(8,128)(2,1)S(1)}, u32[]{:S(2)}, u32[]{:S(2)}) collective-permute-start(bf16[32,2048]{1,0:T(8,128)(2,1)S(1)} %collective-permute-done.10.refs_0_), channel_id=1, source_target_pairs={{0,4},{4,0},{8,12},{12,8},{16,20},{20,16},{24,28},{28,24},{1,5},{5... | collective-permute-start | bytes 393224 | tf_op jit(solution)/shard_map/ppermute | solution.py:271
